TPU v7x, 128 devices: a whole 4x4x4 slice. The times are simulated.
128 devices in a mesh: tile: 32 (over x, y_hi, z), tm: 4 (over y_lo, core).
Axes of the slice: x: 4, y: 4 (y_hi: 2, y_lo: 2; y = y_hi * 2 + y_lo), z: 4, core: 2. Of those that a mesh axis runs over, the one named last changes fastest.
Arguments:
- volume: bfloat16 [16, 256, 16, 128], P('tm', 'tile'), may hold values from -6 to 6
- frame_index: int32 [16], P('tm'), may hold values from 0 to 31, as said below
- tile_offset: int32 [3], replicated, may hold values from 0 to 255
- conv_first: bfloat16 [16, 1, 3, 3, 3], replicated, may hold values from -1.25 to 1.25
- conv_second: bfloat16 [16, 16, 3, 3, 3], replicated, may hold values from -0.3125 to 0.3125
- patch_weight: bfloat16 [8192, 1024], replicated, may hold values from -0.5 to 0.5
- attend_weight: bfloat16 [1024, 3072], P(None, 'tile')
- mixing_weight: bfloat16 [1024, 1024], P(None, 'tile'), may hold values from -0.1875 to 0.1875
- cube_output_projector: bfloat16 [1024, 512], replicated, may hold values from -0.1875 to 0.1875
Outputs:
- prediction_tensor: bfloat16 [16, 32, 2, 16, 512], P('tm', 'tile')
Inputs may be any that keep to these rules, and one draw needn't show every extreme that they name: `frame_index`: strictly increasing; the first frame is 0 and the last is 31.
All inputs are finite; a program needn't handle non-finite values.
Results may differ from a plain program's by a relative error of at most 0.015.
Values may be sent and summed in bfloat16 or wider, within the bound.
No kernel may reach another device: no remote copies, remote signals or barrier semaphores. Data moves between devices by JAX's collectives and lax.ppermute only.
A program may use at most 256 MiB of HBM per device.

v0:
```python
import math

import jax
import jax.numpy as jnp
from jax import lax
from jax.sharding import PartitionSpec as P

CH = 16
D = 1024
HEADS = 8
HD = 128
BLOCK_EDGE_UNITS = 8


def with_halo(cells, sides, width):
    for axis, dim in sides:
        count = lax.axis_size(axis)
        ends = count - 1
        head = lax.slice_in_dim(cells, 0, width, axis=dim)
        tail = lax.slice_in_dim(cells, cells.shape[dim] - width, cells.shape[dim], axis=dim)
        cells = jnp.concatenate(
            [
                lax.ppermute(tail, axis, [(i, (i + 1) % count) for i in range(ends)]),
                cells,
                lax.ppermute(head, axis, [((i + 1) % count, i) for i in range(ends)]),
            ],
            axis=dim,
        )
    return cells


def convolve_strip(field_in, kernel):
    return lax.conv_general_dilated(
        field_in,
        kernel,
        (1, 1, 1),
        ((0, 0), (1, 1), (1, 1)),
        dimension_numbers=("NCDHW", "OIDHW", "NCDHW"),
        preferred_element_type=jnp.float32,
    )


def settle(values_in):
    return values_in * lax.rsqrt(jnp.mean(values_in * values_in, axis=-1, keepdims=True) + 1e-05)


def embed_time(frame_index):
    frequency = jnp.exp(-math.log(1000.0) * jnp.arange(D, dtype=jnp.float32) / D)
    phase_shift = (jnp.arange(D) % 2).astype(jnp.float32) * (math.pi / 2)
    return (jnp.sin(frame_index.astype(jnp.float32)[:, None] * frequency + phase_shift), frequency)


def embed_space(tile_offset, place_x, place_z, place_y, frequency):
    along_x = (tile_offset[0] + BLOCK_EDGE_UNITS * place_x).astype(jnp.float32)
    along_z = (tile_offset[1] + BLOCK_EDGE_UNITS * place_z).astype(jnp.float32)
    along_y = (tile_offset[2] + BLOCK_EDGE_UNITS * place_y).astype(jnp.float32)
    summed = jnp.sin(along_x[:, None, None, None] * frequency) + jnp.sin(
        along_z[None, :, None, None] * frequency + 1.0
    )
    summed = summed + jnp.sin(along_y[None, None, :, None] * frequency + 2.0)
    return summed.reshape(-1, D)


def attend_frames(query, keys_all, values_all, first_frame):
    cube_count = keys_all.shape[1]
    scores = jnp.einsum(
        "tnhd,smhd->htnsm", query, keys_all, preferred_element_type=jnp.float32
    ) / math.sqrt(HD)
    scores = scores.reshape(scores.shape[0], query.shape[0], query.shape[1], -1)
    query_frame = first_frame + jnp.arange(query.shape[0])
    allowed = jnp.arange(keys_all.shape[0])[None, :] <= query_frame[:, None]
    allowed = jnp.repeat(allowed, cube_count, axis=1)
    scores = jnp.where(allowed[None, :, None, :], scores, -1e30)
    shifted = jnp.exp(scores - jnp.max(scores, axis=-1, keepdims=True))
    weights = (shifted / jnp.sum(shifted, axis=-1, keepdims=True)).astype(jnp.bfloat16)
    flat_values = values_all.reshape(-1, values_all.shape[2], values_all.shape[3])
    return jnp.einsum(
        "htnk,khd->tnhd", weights, flat_values, preferred_element_type=jnp.float32
    ).astype(jnp.bfloat16)


def local(
    volume,
    frame_index,
    tile_offset,
    conv_first,
    conv_second,
    patch_weight,
    attend_weight,
    mixing_weight,
    cube_output_projector,
):
    local_frames, width_here, cells_in_depth, height_extent = volume.shape
    tile_place = lax.axis_index("tile")
    padded = with_halo(volume, (("tile", 1),), 1)
    first_maps = jax.nn.silu(convolve_strip(padded[:, None], conv_first)).astype(jnp.bfloat16)
    first_maps = with_halo(first_maps, (("tile", 2),), 1)
    second_maps = jax.nn.silu(convolve_strip(first_maps, conv_second)).astype(jnp.bfloat16)
    stride_along_x = width_here // BLOCK_EDGE_UNITS
    patch_cubes = second_maps.reshape(
        local_frames,
        CH,
        stride_along_x,
        BLOCK_EDGE_UNITS,
        cells_in_depth // BLOCK_EDGE_UNITS,
        BLOCK_EDGE_UNITS,
        height_extent // BLOCK_EDGE_UNITS,
        BLOCK_EDGE_UNITS,
    )
    patch_cubes = patch_cubes.transpose(0, 2, 4, 6, 1, 3, 5, 7).reshape(
        -1, CH * BLOCK_EDGE_UNITS**3
    )
    encoded = jnp.dot(patch_cubes, patch_weight, preferred_element_type=jnp.float32).reshape(
        local_frames, -1, D
    )
    time_emb, frequency = embed_time(frame_index)
    place_x = tile_place * stride_along_x + jnp.arange(stride_along_x)
    space_emb = embed_space(
        tile_offset,
        place_x,
        jnp.arange(cells_in_depth // BLOCK_EDGE_UNITS),
        jnp.arange(height_extent // BLOCK_EDGE_UNITS),
        frequency,
    )
    tokens = (encoded + time_emb[:, None, :] + space_emb[None]).astype(jnp.bfloat16)
    token_rows = tokens.reshape(-1, D)
    normed = settle(token_rows.astype(jnp.float32)).astype(jnp.bfloat16)
    row_count = token_rows.shape[0]
    projected = jnp.dot(
        normed,
        lax.all_gather(attend_weight, "tile", axis=1, tiled=True),
        preferred_element_type=jnp.float32,
    ).astype(jnp.bfloat16)
    cube_count = row_count // local_frames
    projected = projected.reshape(local_frames, cube_count, 3, HEADS, HD)
    keys_values = lax.all_gather(projected[:, :, 1:], "tm", axis=0, tiled=True)
    attended = attend_frames(
        projected[:, :, 0],
        keys_values[:, :, 0],
        keys_values[:, :, 1],
        lax.axis_index("tm") * local_frames,
    )
    attended_rows = attended.reshape(row_count, D)
    mixed_terms = jnp.dot(
        attended_rows,
        lax.all_gather(mixing_weight, "tile", axis=1, tiled=True),
        preferred_element_type=jnp.float32,
    )
    residual = token_rows.astype(jnp.float32) + mixed_terms
    ending_entries = settle(residual).astype(jnp.bfloat16)
    prediction_tensor = jnp.dot(
        ending_entries, cube_output_projector, preferred_element_type=jnp.float32
    ).astype(jnp.bfloat16)
    return prediction_tensor.reshape(
        local_frames,
        stride_along_x,
        cells_in_depth // BLOCK_EDGE_UNITS,
        height_extent // BLOCK_EDGE_UNITS,
        -1,
    )


def solution(mesh):
    placed = (
        P("tm", "tile", None, None),
        P("tm"),
        P(),
        P(),
        P(),
        P(),
        P(None, "tile"),
        P(None, "tile"),
        P(),
    )
    return jax.shard_map(
        local,
        mesh=mesh,
        in_specs=placed,
        out_specs=P("tm", "tile", None, None, None),
        check_vma=False,
    )
```

profile of v0, /device:TPU:1, one launch (start us, length us, event | category | flops | bytes accessed | tf_op | source)
XLA Modules:
  0.0 538.2 jit_solution(4593768674398260444)
XLA Ops:
  6.5 0.8 fusion.34
  7.4 4.4 collective-permute-start
  11.7 1.3 collective-permute-start.1
  13.1 1.4 fusion.35
  16.0 0.7 add_convert_fusion
  18.5 0.8 add_sine_fusion.1
  19.3 0.9 maximum_bitcast_fusion.1
  20.4 0.9 reshape.256
  22.0 2.0 fusion.6
  24.0 4.4 copy.19
  28.4 19.7 %multiply_convert_fusion.1 = bf16[8,16,32,17,16]{2,4,3,1,0:T(8,128)(2,1)} fusion(pred[32,17]{0,1:T(8,128)(4,1)S(1)} %copy-done.7, bf16[1,10,16,32,19]{3,0,4,2,1:T(2,128)(2,1)S(1)} %copy.19, bf16[16,1,3,3,3]{0,4,3,2,1:T(4,128)(2,1)S(1)} %copy-done.6), kind=kOutput, calls=%fused_computation.5 | convolution fusion | flops 64339968 | bytes 2424192 | tf_op jit(solution)/shard_map/conv_general_dilated | solution.py:33
  48.1 24.1 %copy.22 = bf16[8,16,32,17,16]{3,2,4,1,0:T(8,128)(2,1)} copy(bf16[8,16,32,17,16]{2,4,3,1,0:T(8,128)(2,1)} %multiply_convert_fusion.1) | data formatting | bytes 4456448 | tf_op jit(solution)/shard_map/convert_element_type | solution.py:96
  72.3 3.9 fusion.33
  76.2 3.6 copy.21
  79.8 2.3 reshape.260
  82.1 1.8 slice_bitcast_fusion.5
  83.9 3.7 collective-permute-start.2
  87.6 3.6 copy.23
  91.2 2.3 reshape.262
  93.5 1.1 slice_bitcast_fusion.4
  94.6 1.3 collective-permute-start.3
  95.9 21.5 %reshape.271 = bf16[8,16,4,136,16]{3,2,4,1,0:T(4,128)(2,1)} reshape(bf16[8,16,32,17,16]{3,2,4,1,0:T(8,128)(2,1)} %copy.22) | data formatting | bytes 4456448 | tf_op jit(solution)/shard_map/convert_element_type | solution.py:96
  117.4 2.6 slice_bitcast_fusion.1
  120.0 2.0 maximum_bitcast_fusion
  122.0 3.0 copy.42
  125.1 4.4 pad.2.clone
  129.5 24.7 %reshape.265 = bf16[16,10,16,4,8,17]{5,4,2,3,1,0:T(8,128)(2,1)} reshape(bf16[16,10,16,4,136]{4,2,3,1,0:T(8,128)(2,1)} %pad.2.clone) | data formatting | bytes 5570560 | tf_op jit(solution)/shard_map/conv_general_dilated | solution.py:33
  154.1 21.6 %slice.58 = bf16[16,10,16,4,7,2]{5,4,2,3,1,0:T(8,128)(2,1)} slice(bf16[16,10,16,4,8,17]{5,4,2,3,1,0:T(8,128)(2,1)} %reshape.265), slice={[0:16], [0:10], [0:16], [0:4], [1:8], [0:2]} | slice | bytes 573440 | tf_op jit(solution)/shard_map/conv_general_dilated | solution.py:33
  175.8 21.9 %copy_bitcast_fusion = bf16[16,10,16,32,19]{4,3,2,1,0:T(8,128)(2,1)} fusion(bf16[16,10,16,4,7,2]{5,4,2,3,1,0:T(8,128)(2,1)} %slice.58, bf16[16,10,16,4,8,17]{5,4,2,3,1,0:T(8,128)(2,1)S(1)} %copy-done.1), kind=kLoop, calls=%fused_computation.3 | loop fusion | flops 9338880 | bytes 6184960 | tf_op jit(solution)/shard_map/conv_general_dilated | solution.py:33
  197.7 28.3 %copy.26 = bf16[16,10,16,32,19]{3,0,4,2,1:T(8,128)(2,1)} copy(bf16[16,10,16,32,19]{4,3,2,1,0:T(8,128)(2,1)} %copy_bitcast_fusion) | data formatting | bytes 6225920 | tf_op jit(solution)/shard_map/conv_general_dilated | solution.py:33
  226.0 35.9 %multiply_convert_fusion = bf16[8,16,32,17,16]{2,4,3,1,0:T(8,128)(2,1)} fusion(bf16[16,10,16,32,19]{3,0,4,2,1:T(8,128)(2,1)} %copy.26, bf16[16,16,3,3,3]{1,0,4,3,2:T(8,128)(2,1)S(1)} %copy-done.5, pred[32,17]{0,1:T(8,128)(4,1)S(1)} %copy-done.7), kind=kOutput, calls=%fused_computation.4 | convolution fusion | flops 929169408 | bytes 5355552 | tf_op jit(solution)/shard_map/conv_general_dilated | solution.py:33
  261.9 24.1 %copy.27 = bf16[8,16,32,17,16]{3,2,4,1,0:T(8,128)(2,1)} copy(bf16[8,16,32,17,16]{2,4,3,1,0:T(8,128)(2,1)} %multiply_convert_fusion) | data formatting | bytes 4456448 | tf_op jit(solution)/shard_map/convert_element_type | solution.py:98
  286.0 21.3 %reshape.269 = bf16[8,16,4,136,16]{3,2,4,1,0:T(4,128)(2,1)} reshape(bf16[8,16,32,17,16]{3,2,4,1,0:T(8,128)(2,1)} %copy.27) | data formatting | bytes 4456448 | tf_op jit(solution)/shard_map/convert_element_type | solution.py:98
  307.4 2.6 slice_bitcast_fusion
  309.9 11.0 %copy.28 = bf16[4,16,8,16,128]{1,4,3,2,0:T(8,128)(2,1)} copy(bf16[4,16,8,16,128]{4,0,1,3,2:T(4,128)(2,1)S(1)} %slice_bitcast_fusion) | data formatting | bytes 4194304 | tf_op jit(solution)/shard_map/convert_element_type | solution.py:98
  321.0 51.2 %copy.29 = bf16[4,1,2,16,16,8,8,8]{3,2,7,6,5,4,0,1:T(2,128)(2,1)} copy(bf16[4,1,2,16,16,8,8,8]{4,7,3,6,2,5,0,1:T(8,128)(2,1)} %bitcast.117) | data formatting | bytes 4194304 | tf_op jit(solution)/shard_map/transpose | solution.py:110
  372.2 27.0 %dot_general.20 = bf16[4,32,8192]{1,2,0:T(8,128)(2,1)} reshape(bf16[4,1,2,16,16,8,8,8]{3,2,7,6,5,4,0,1:T(2,128)(2,1)} %copy.29) | data formatting | bytes 4194304 | tf_op jit(solution)/shard_map/dot_general | solution.py:113
  399.2 11.8 %multiply_reduce_fusion.1 = (f32[4,32]{1,0:T(4,128)S(1)}, f32[4,32,1024]{2,1,0:T(8,128)S(1)}) fusion(f32[32,1024]{1,0:T(8,128)S(1)} %bitcast.123, f32[4,1024]{1,0:T(4,128)S(1)} %copy-done.4, bf16[4,32,8192]{1,2,0:T(8,128)(2,1)} %dot_general.20, bf16[8192,1024]{1,0:T(8,128)(2,1)} %param.14), kind=kOutput, calls=%fused_computation.35 | convolution fusion | flops 2148270080 | bytes 19546624 | tf_op jit(solution)/shard_map/dot_general | solution.py:113
  411.3 5.0 fusion.7
  416.5 0.9 copy.40
  417.5 0.7 all-gather.8.cloned.1.call-update
  418.5 36.3 %all-gather.6.cloned.1.call-done = bf16[16,32,2,8,128]{4,1,0,3,2:T(8,128)(2,1)} async-done(((bf16[4,32,2,8,128]{4,1,0,3,2:T(8,128)(2,1)}), bf16[16,32,2,8,128]{4,1,0,3,2:T(8,128)(2,1)}) %all-gather.6.cloned.1.call-update) | async-done | bytes 2097168 | tf_op jit(solution)/shard_map/all_gather | solution.py:136
  454.8 6.2 %select_reduce_fusion = (f32[8,4,32]{2,1,0:T(4,128)S(1)}, f32[8,4,32,16,32]{2,4,3,1,0:T(8,128)}) fusion(pred[4,16]{1,0:T(4,128)(4,1)S(1)} %iota_compare_fusion.2, bf16[16,32,2,8,128]{4,1,0,3,2:T(8,128)(2,1)} %all-gather.6.cloned.1.call-done, bf16[4,32,1,8,128]{4,3,2,1,0:T(8,128)(2,1)S(1)} %slice.62), kind=kOutput, calls=%fused_computation.9 | convolution fusion | flops 135789568 | bytes 3412032 | tf_op jit(solution)/shard_map/tnhd,smhd->htnsm/dot_general | solution.py:66
  461.0 6.3 %copy.33 = f32[8,4,32,512]{3,2,1,0:T(8,128)} copy(f32[8,4,32,512]{2,3,1,0:T(8,128)} %bitcast.116) | data formatting | bytes 4194304 | tf_op jit(solution)/shard_map/reshape | solution.py:69
  467.3 4.6 exponential_reduce_fusion
  472.7 55.2 %all-gather.8.cloned.1.call-done = bf16[1024,1024]{0,1:T(8,128)(2,1)} async-done(((bf16[1024,32]{0,1:T(8,128)(2,1)}), bf16[1024,1024]{0,1:T(8,128)(2,1)}) %all-gather.8.cloned.1.call-update) | async-done | bytes 2097168 | tf_op jit(solution)/shard_map/all_gather | solution.py:146
  528.0 2.5 multiply_reduce_fusion
  530.5 1.0 convolution_convert_fusion.2
  (51 shorter events, 5.0 us)
Async XLA Ops:
  6.5 524.0 %copy-start = (bf16[1024,512]{1,0:T(8,128)(2,1)S(1)}, bf16[1024,512]{1,0:T(8,128)(2,1)}, u32[]{:S(2)}) copy-start(bf16[1024,512]{1,0:T(8,128)(2,1)} %param.17) | copy-start | bytes 3145732
  6.5 404.7 %all-gather.4.cloned.1.call-start = ((), (), s32[]{:S(2)}) async-start(), calls=%async_computation | async-start | bytes 6488064 | tf_op jit(solution)/shard_map/all_gather | solution.py:131
  7.4 11.9 %collective-permute-start = (bf16[4,1,16,128]{3,2,1,0:T(8,128)(2,1)S(1)}, bf16[4,1,16,128]{3,2,1,0:T(8,128)(2,1)S(1)}, u32[]{:S(2)}, u32[]{:S(2)}) collective-permute-start(bf16[4,1,16,128]{3,2,1,0:T(8,128)(2,1)S(1)} %get-tuple-element.7), channel_id=1, source_target_pairs={{0,4},{4,8},{8,12},{12,16},{16,20},{20,24},{24,28},{28,32},{32,36}... | collective-permute-start | bytes 49160 | tf_op jit(solution)/shard_map/ppermute | solution.py:23
  11.7 7.6 %collective-permute-start.1 = (bf16[4,1,16,128]{3,2,1,0:T(8,128)(2,1)S(1)}, bf16[4,1,16,128]{3,2,1,0:T(8,128)(2,1)S(1)}, u32[]{:S(2)}, u32[]{:S(2)}) collective-permute-start(bf16[4,1,16,128]{3,2,1,0:T(8,128)(2,1)S(1)} %get-tuple-element.8), channel_id=1, source_target_pairs={{4,0},{8,4},{12,8},{16,12},{20,16},{24,20},{28,24},{32,28},{36,32}... | collective-permute-start | bytes 49160 | tf_op jit(solution)/shard_map/ppermute | solution.py:25
  13.1 441.8 %all-gather.6.cloned.1.call-start = ((), (), s32[]{:S(2)}) async-start(), calls=%async_computation.1 | async-start | bytes 2621440 | tf_op jit(solution)/shard_map/all_gather | solution.py:136
  21.3 7.1 %copy-start.6 = (bf16[16,1,3,3,3]{0,4,3,2,1:T(4,128)(2,1)S(1)}, bf16[16,1,3,3,3]{0,4,3,2,1:T(4,128)(2,1)}, u32[]{:S(2)}) copy-start(bf16[16,1,3,3,3]{0,4,3,2,1:T(4,128)(2,1)} %param.12) | copy-start | bytes 2596
  21.3 7.1 %copy-start.7 = (pred[32,17]{0,1:T(8,128)(4,1)S(1)}, pred[32,17]{0,1:T(8,128)(4,1)}, u32[]{:S(2)}) copy-start(pred[32,17]{0,1:T(8,128)(4,1)} %constant.72) | copy-start | bytes 1636
  83.9 36.1 %collective-permute-start.2 = (bf16[4,16,1,16,128]{4,0,1,3,2:T(4,128)(2,1)}, bf16[4,16,1,16,128]{4,0,1,3,2:T(4,128)(2,1)S(1)}, u32[]{:S(2)}, u32[]{:S(2)}) collective-permute-start(bf16[4,16,1,16,128]{4,0,1,3,2:T(4,128)(2,1)} %slice_bitcast_fusion.5), channel_id=1, source_target_pairs={{0,4},{4,8},{8,12},{12,16},{16,20},{20,24},{24,28},{28,32},{32,36}... | collective-permute-start | bytes 786440 | tf_op jit(solution)/shard_map/ppermute | solution.py:23
  94.6 25.4 %collective-permute-start.3 = (bf16[4,16,1,16,128]{4,0,1,3,2:T(4,128)(2,1)S(1)}, bf16[4,16,1,16,128]{4,0,1,3,2:T(4,128)(2,1)S(1)}, u32[]{:S(2)}, u32[]{:S(2)}) collective-permute-start(bf16[4,16,1,16,128]{4,0,1,3,2:T(4,128)(2,1)S(1)} %slice_bitcast_fusion.4), channel_id=1, source_target_pairs={{4,0},{8,4},{12,8},{16,12},{20,16},{24,20},{28,24},{32,28},{36,32}... | collective-permute-start | bytes 786440 | tf_op jit(solution)/shard_map/ppermute | solution.py:25
  154.1 21.6 %copy-start.1 = (bf16[16,10,16,4,8,17]{5,4,2,3,1,0:T(8,128)(2,1)S(1)}, bf16[16,10,16,4,8,17]{5,4,2,3,1,0:T(8,128)(2,1)}, u32[]{:S(2)}) copy-start(bf16[16,10,16,4,8,17]{5,4,2,3,1,0:T(8,128)(2,1)} %reshape.265) | copy-start | bytes 8355844
  197.7 28.3 %copy-start.5 = (bf16[16,16,3,3,3]{1,0,4,3,2:T(8,128)(2,1)S(1)}, bf16[16,16,3,3,3]{1,0,4,3,2:T(8,128)(2,1)}, u32[]{:S(2)}) copy-start(bf16[16,16,3,3,3]{1,0,4,3,2:T(8,128)(2,1)} %param.13) | copy-start | bytes 41476
  372.2 27.0 %copy-start.3 = (f32[2,16,1024]{2,1,0:T(8,128)S(1)}, f32[2,16,1024]{2,1,0:T(8,128)}, u32[]{:S(2)}) copy-start(f32[2,16,1024]{2,1,0:T(8,128)} %broadcast_add_fusion) | copy-start | bytes 393220
  372.2 27.0 %copy-start.4 = (f32[4,1024]{1,0:T(4,128)S(1)}, f32[4,1024]{1,0:T(4,128)}, u32[]{:S(2)}) copy-start(f32[4,1024]{1,0:T(4,128)} %add_sine_fusion.1) | copy-start | bytes 49156
  417.4 110.5 %all-gather.8.cloned.1.call-start = ((), (), s32[]{:S(2)}) async-start(), calls=%async_computation.2 | async-start | bytes 2162688 | tf_op jit(solution)/shard_map/all_gather | solution.py:146
  467.3 4.6 copy-start.2
  467.3 4.6 slice-start
Sparse Core Ops, SparseCore 0:
  13.2 97.7 all-gather.3
  417.6 37.2 all-gather.5
  457.9 69.9 all-gather.7
where the time goes:
time: 548 us; the launch traced here: 538 us
  local copies, waits for them, and re-layouts  302 us (55%)
  waiting for transfers between devices  92.3 us (17%)
  matrix products  82.8 us (15%)
  other arithmetic  35.7 us (7%)
  between operations  14.4 us (3%)
  starting transfers between devices  10.7 us (2%)
    conv_general_dilated x6, local copies, waits for them, and re-layouts, convolve_strip(): lax.conv_general_dilated(field_in, kernel, (1, 1, 1), ((0, 0), (1, 1), (1...  80.2 us
    convert_element_type x8, local copies, waits for them, and re-layouts, local(): jax.nn.silu(convolve_strip(padded[:, None], conv_first))  64 us
    convert_element_type x4, local copies, waits for them, and re-layouts, local(): jax.nn.silu(convolve_strip(first_maps, conv_second)).astype(jnp.bfloat16)  59 us
    conv_general_dilated x2, matrix products, convolve_strip(): lax.conv_general_dilated(field_in, kernel, (1, 1, 1), ((0, 0), (1, 1), (1...  55.7 us
    all_gather x1, waiting for transfers between devices, local(): lax.all_gather(mixing_weight, 'tile', axis=1, tiled=True)  55.2 us
    transpose x1, local copies, waits for them, and re-layouts, local(): patch_cubes.transpose(0, 2, 4, 6, 1, 3, 5, 7)  51.2 us
    all_gather x1, waiting for transfers between devices, local(): keys_values = lax.all_gather(projected[:, :, 1:], 'tm', axis=0, tiled=True)  36.3 us
    dot_general x1, local copies, waits for them, and re-layouts, local(): jnp.dot(patch_cubes, patch_weight, preferred_element_type=jnp.float32)  27 us
  transfers between devices with their start and end apart: 7, of which 2 were waited for; matrix products, arithmetic and copies ran while one was open for 76% of the time, Pallas kernels for 0%

commit v1 on v0

v1 whole, which is shorter than its diff:
```python
import functools
import math

import jax
import jax.numpy as jnp
from jax import lax
from jax.experimental import pallas as pl
from jax.experimental.pallas import tpu as pltpu
from jax.sharding import PartitionSpec as P

CH = 16
D = 1024
HEADS = 8
HD = 128
BLOCK_EDGE_UNITS = 8

F32 = jnp.float32
BF16 = jnp.bfloat16

ROWS = 8
XV = 12
XM = 10
ZV = 12
ZM = 10
BLK = 128
PAIRS = 8


def silu(v):
    return 0.5 * v * (1.0 + jnp.tanh(0.5 * v))


def weights_kernel(first_ref, second_ref, g_ref, w2_ref):
    col = lax.broadcasted_iota(jnp.int32, (48, 768), 1)
    row = lax.broadcasted_iota(jnp.int32, (48, 768), 0)
    spread = (
        ((col // 256) == (row // CH)) & (((col % 128) // 8) == (row % CH))
    ).astype(BF16)
    first = jnp.dot(first_ref[...], spread, preferred_element_type=F32)
    second = jnp.dot(second_ref[...], spread, preferred_element_type=F32).astype(BF16)

    lane = lax.broadcasted_iota(jnp.int32, (48, 256), 1)
    here = lax.broadcasted_iota(jnp.int32, (48, 256), 0) - 16
    out_y = (lane // 128) * 8 + lane % 8
    for tap in range(9):
        total = jnp.zeros((48, 256), F32)
        for k in range(3):
            value = first[tap : tap + 1, 256 * k : 256 * (k + 1)]
            total = total + jnp.where(here == out_y + (k - 1), value, 0.0)
        g_ref[tap] = total.astype(BF16)

    r = lax.broadcasted_iota(jnp.int32, (512, CH), 0)
    c = lax.broadcasted_iota(jnp.int32, (512, CH), 1)
    pick = (((r % 128) // 8) == c).astype(BF16)
    lane = lax.broadcasted_iota(jnp.int32, (512, 256), 1)
    r = lax.broadcasted_iota(jnp.int32, (512, 256), 0)
    shift = (r // 128 - 1) * 8 + r % 8 - ((lane // 128) * 8 + lane % 8)
    for tap in range(9):
        rows = jnp.dot(
            pick, second[CH * tap : CH * (tap + 1)], preferred_element_type=F32
        )
        total = jnp.zeros((512, 256), F32)
        for k in range(3):
            total = total + jnp.where(
                shift == k - 1, rows[:, 256 * k : 256 * (k + 1)], 0.0
            )
        w2_ref[tap] = total.astype(BF16)


def encode_kernel(
    place_ref,
    volume_ref,
    left_ref,
    right_ref,
    g_ref,
    w2_ref,
    time_ref,
    space_ref,
    along_y_ref,
    patch_hbm,
    tokens_ref,
    normed_ref,
    cells,
    planes,
    taps,
    w1,
    maps_even,
    maps_odd,
    second,
    patch,
    patch_sem,
):
    copies = [
        pltpu.make_async_copy(
            patch_hbm.at[:, pl.ds(8 * i, 8)],
            patch.at[:, pl.ds(8 * i, 8)],
            patch_sem.at[i],
        )
        for i in range(8)
    ]
    for copy in copies:
        copy.start()
    place = place_ref[0]
    count = place_ref[1]

    cells[:, 0:2] = left_ref[...].astype(F32)
    cells[:, 2:10] = volume_ref[...].astype(F32)
    cells[:, 10:12] = right_ref[...].astype(F32)
    planes[...] = jnp.zeros_like(planes)
    for x in range(XV):
        for f in range(4):
            planes[x, pl.ds(16 + 2 * f, 10, stride=8), :] = cells[f, x, pl.ds(0, 10), :]
            planes[x, pl.ds(2 * f + 1, 10, stride=8), :] = cells[f, x, pl.ds(6, 10), :]
    for dx in range(3):
        for dz in range(3):
            tap = 3 * dx + dz
            for x in range(XM):
                taps[x, :, BLK * tap : BLK * (tap + 1)] = planes[
                    x + dx, 8 * dz : 8 * dz + 80, :
                ].astype(BF16)

    w1[...] = jnp.zeros_like(w1)
    maps_even[:, :, 0:BLK] = jnp.zeros((XM, 80, BLK), BF16)
    maps_even[:, :, 17 * BLK :] = jnp.zeros((XM, 80, BLK), BF16)
    maps_odd[:, :, 0:BLK] = jnp.zeros((XM, 64, BLK), BF16)
    maps_odd[:, :, 17 * BLK :] = jnp.zeros((XM, 64, BLK), BF16)

    x = lax.broadcasted_iota(jnp.int32, (XM, 80, 1), 0) + 8 * place - 1
    r = lax.broadcasted_iota(jnp.int32, (XM, 80, 1), 1)
    z = 8 * (r % 2) + r // 8 - 1
    inside = (x >= 0) & (x < 8 * count) & (z >= 0) & (z < 16)

    def first_step(n, carry):
        before = pl.ds(pl.multiple_of(16 * jnp.maximum(n - 1, 0), 16), 16)
        now = pl.ds(pl.multiple_of(16 * n, 16), 48)
        for tap in range(9):
            w1[tap, before, :] = jnp.zeros((16, 256), BF16)
            w1[tap, now, :] = g_ref[tap]
        acc = jnp.zeros((XM * 80, 256), F32)
        for tap in range(9):
            acc = acc + jnp.dot(
                taps[:, :, BLK * tap : BLK * (tap + 1)].reshape(XM * 80, BLK),
                w1[tap, 16:144, :],
                preferred_element_type=F32,
            )
        out = jnp.where(inside, silu(acc).reshape(XM, 80, 256), 0.0)
        lanes = pl.ds(pl.multiple_of(256 * n + BLK, BLK), 256)
        maps_even[:, :, lanes] = out.astype(BF16)
        maps_odd[:, :, lanes] = out[:, 8:72].astype(BF16)
        return carry

    lax.fori_loop(0, PAIRS, first_step, 0)

    def second_step(p, carry):
        lanes = pl.ds(pl.multiple_of(256 * p, 256), 512)
        acc = jnp.zeros((512, 256), F32)
        for dx in range(3):
            for dz in range(3):
                if dz == 1:
                    source = maps_odd[dx : dx + 8, :, lanes]
                else:
                    source = maps_even[dx : dx + 8, 8 * dz : 8 * dz + 64, lanes]
                acc = acc + jnp.dot(
                    source.reshape(512, 512), w2_ref[3 * dx + dz], preferred_element_type=F32
                )
        out = silu(acc)
        both = jnp.concatenate(
            [out[:, :BLK].reshape(64, 8, BLK), out[:, BLK:].reshape(64, 8, BLK)], axis=1
        )
        second[:, pl.ds(pl.multiple_of(16 * p, 16), 16), :] = both.astype(BF16)
        return carry

    lax.fori_loop(0, PAIRS, second_step, 0)

    encoded = jnp.zeros((128, D), F32)
    for x in range(8):
        copies[x].wait()
        for z in range(0, 8, 2):
            i = 8 * x + z
            lhs = jnp.concatenate([second[i], second[i + 1]], axis=1)
            rhs = jnp.concatenate(
                [patch[:, i].reshape(BLK, D), patch[:, i + 1].reshape(BLK, D)], axis=0
            )
            encoded = encoded + jnp.dot(lhs, rhs, preferred_element_type=F32)

    encoded = encoded.reshape(16, 8, D) + time_ref[...][None]
    space = space_ref[...][None] + along_y_ref[...][:, None, :]
    tokens = (encoded + space).reshape(128, D).astype(BF16)
    tokens_ref[...] = tokens
    wide = tokens.astype(F32)
    scale = lax.rsqrt(jnp.mean(wide * wide, axis=-1, keepdims=True) + 1e-05)
    normed_ref[...] = (wide * scale).astype(BF16)


def attend_kernel(
    place_ref,
    tokens_ref,
    n0_ref,
    n1_ref,
    n2_ref,
    n3_ref,
    wide_ref,
    mixing_ref,
    projector_ref,
    out_ref,
    normed,
    query,
    keys,
    attended,
):
    place = place_ref[0]
    contract = (((1,), (1,)), ((), ()))
    for i, ref in enumerate((n0_ref, n1_ref, n2_ref, n3_ref)):
        normed[128 * i : 128 * (i + 1)] = ref[...]
    query[...] = lax.dot_general(
        normed[0:128], wide_ref[0:D], contract, preferred_element_type=F32
    ).astype(BF16)
    for i in range(4):
        keys[:, 512 * i : 512 * (i + 1)] = lax.dot_general(
            normed[...],
            wide_ref[D + 512 * i : D + 512 * (i + 1)],
            contract,
            preferred_element_type=F32,
        ).astype(BF16)
    col = lax.broadcasted_iota(jnp.int32, (128, 512), 1)
    row = lax.broadcasted_iota(jnp.int32, (128, 512), 0)
    source = place ^ (col // 128)
    allowed = 4 * source + (col % 8) // 2 <= 4 * place + (row % 8) // 2
    for h in range(HEADS):
        q = query[:, HD * h : HD * (h + 1)]
        k = keys[:, HD * h : HD * (h + 1)]
        v = keys[:, D + HD * h : D + HD * (h + 1)]
        scores = lax.dot_general(q, k, contract, preferred_element_type=F32) * (
            1.0 / math.sqrt(HD)
        )
        scores = jnp.where(allowed, scores, -1e30)
        shifted = jnp.exp(scores - jnp.max(scores, axis=-1, keepdims=True))
        weights = shifted * (1.0 / jnp.sum(shifted, axis=-1, keepdims=True))
        attended[:, HD * h : HD * (h + 1)] = jnp.dot(
            weights.astype(BF16), v, preferred_element_type=F32
        ).astype(BF16)
    residual = tokens_ref[...].astype(F32) + lax.dot_general(
        attended[...], mixing_ref[...], contract, preferred_element_type=F32
    )
    scale = lax.rsqrt(jnp.mean(residual * residual, axis=-1, keepdims=True) + 1e-05)
    final = (residual * scale).astype(BF16)
    out_ref[...] = jnp.dot(final, projector_ref[...], preferred_element_type=F32).astype(
        BF16
    )


def vmem():
    return pl.BlockSpec(memory_space=pltpu.VMEM)


def smem():
    return pl.BlockSpec(memory_space=pltpu.SMEM)


def local(
    volume,
    frame_index,
    tile_offset,
    conv_first,
    conv_second,
    patch_weight,
    attend_weight,
    mixing_weight,
    cube_output_projector,
):
    count = lax.axis_size("tile")
    tile_place = lax.axis_index("tile")
    tm_place = lax.axis_index("tm")
    up = [(i, i + 1) for i in range(count - 1)]
    down = [(i + 1, i) for i in range(count - 1)]
    left = lax.ppermute(volume[:, 6:8], "tile", up)
    right = lax.ppermute(volume[:, 0:2], "tile", down)

    wide = lax.all_gather(attend_weight.T, "tile", axis=0, tiled=True)
    mixing = lax.all_gather(mixing_weight.T, "tile", axis=0, tiled=True)

    frequency = jnp.exp(-math.log(1000.0) * jnp.arange(D, dtype=F32) / D)
    phase_shift = (jnp.arange(D) % 2).astype(F32) * (math.pi / 2)
    time_emb = jnp.sin(
        jnp.repeat(frame_index.astype(F32), 2)[:, None] * frequency + phase_shift
    )
    at = lambda axis, place: (tile_offset[axis] + BLOCK_EDGE_UNITS * place).astype(F32)
    along_x = jnp.sin(at(0, tile_place) * frequency)
    along_z = jnp.sin(at(1, jnp.arange(8) % 2)[:, None] * frequency + 1.0)
    along_y = jnp.sin(at(2, jnp.arange(16))[:, None] * frequency + 2.0)

    first = conv_first.transpose(2, 3, 1, 4, 0).reshape(9, 48)
    first = jnp.pad(first, ((0, 7), (0, 0)))
    second = conv_second.transpose(2, 3, 1, 4, 0).reshape(144, 48)
    g, w2 = pl.pallas_call(
        weights_kernel,
        out_shape=(
            jax.ShapeDtypeStruct((9, 48, 256), BF16),
            jax.ShapeDtypeStruct((9, 512, 256), BF16),
        ),
        in_specs=[vmem(), vmem()],
        out_specs=(vmem(), vmem()),
        name="conv_weights",
        compiler_params=pltpu.CompilerParams(vmem_limit_bytes=24 << 20),
    )(first, second)

    tokens, normed = pl.pallas_call(
        encode_kernel,
        out_shape=(
            jax.ShapeDtypeStruct((128, D), BF16),
            jax.ShapeDtypeStruct((128, D), BF16),
        ),
        in_specs=[smem()] + [vmem()] * 8 + [pl.BlockSpec(memory_space=pl.ANY)],
        out_specs=(vmem(), vmem()),
        scratch_shapes=[
            pltpu.VMEM((4, XV, 16, 128), F32),
            pltpu.VMEM((XV, ZV * ROWS, 128), F32),
            pltpu.VMEM((XM, 80, 9 * BLK), BF16),
            pltpu.VMEM((9, 160, 256), BF16),
            pltpu.VMEM((XM, 80, 18 * BLK), BF16),
            pltpu.VMEM((XM, 64, 18 * BLK), BF16),
            pltpu.VMEM((64, 128, BLK), BF16),
            pltpu.VMEM((CH, 64, 8, D), BF16),
            pltpu.SemaphoreType.DMA((8,)),
        ],
        name="encode",
        compiler_params=pltpu.CompilerParams(vmem_limit_bytes=56 << 20),
    )(
        jnp.stack([tile_place, jnp.int32(count)]).astype(jnp.int32),
        volume,
        left,
        right,
        g,
        w2,
        time_emb,
        along_x[None] + along_z,
        along_y,
        patch_weight.reshape(CH, 64, 8, D),
    )

    by_chip = lax.ppermute(normed, "tm", [(0, 2), (2, 0), (1, 3), (3, 1)])
    by_core = lax.ppermute(normed, "tm", [(0, 1), (1, 0), (2, 3), (3, 2)])
    by_both = lax.ppermute(by_chip, "tm", [(0, 1), (1, 0), (2, 3), (3, 2)])

    out = pl.pallas_call(
        attend_kernel,
        out_shape=jax.ShapeDtypeStruct((128, 512), BF16),
        in_specs=[smem()] + [vmem()] * 8,
        out_specs=vmem(),
        scratch_shapes=[
            pltpu.VMEM((512, D), BF16),
            pltpu.VMEM((128, D), BF16),
            pltpu.VMEM((512, 2 * D), BF16),
            pltpu.VMEM((128, D), BF16),
        ],
        name="attend",
        compiler_params=pltpu.CompilerParams(vmem_limit_bytes=48 << 20),
    )(
        tm_place[None].astype(jnp.int32),
        tokens,
        normed,
        by_core,
        by_chip,
        by_both,
        wide,
        mixing,
        cube_output_projector,
    )
    return out.reshape(16, 4, 2, 512).transpose(1, 2, 0, 3)[:, None]


def solution(mesh):
    placed = (
        P("tm", "tile", None, None),
        P("tm"),
        P(),
        P(),
        P(),
        P(),
        P(None, "tile"),
        P(None, "tile"),
        P(),
    )
    return jax.shard_map(
        local,
        mesh=mesh,
        in_specs=placed,
        out_specs=P("tm", "tile", None, None, None),
        check_vma=False,
    )
```

time: 548 us -> 198 us (0.36); the launches traced: 538 us -> 197 us
  local copies, waits for them, and re-layouts: 302 us -> 11.3 us
  matrix products: 82.8 us -> 0 us
  Pallas kernels: 0 us -> 38.7 us
  other arithmetic: 35.7 us -> 4.46 us
  waiting for transfers between devices: 92.3 us -> 119 us
    convert_element_type x13 -> x0, local copies, waits for them, and re-layouts: 123 us -> none  [the longest x8 64 us: local(): jax.nn.silu(convolve_strip(padded[:, None], conv_first))]
    conv_general_dilated x6 -> x0, local copies, waits for them, and re-layouts: 80.2 us -> none  [convolve_strip(): lax.conv_general_dilated(field_in, kernel, (1, 1, 1), ((0, 0), (1, 1), (1...]
    conv_general_dilated x2 -> x0, matrix products: 55.7 us -> none  [convolve_strip(): lax.conv_general_dilated(field_in, kernel, (1, 1, 1), ((0, 0), (1, 1), (1...]
    transpose x1 -> x0, local copies, waits for them, and re-layouts: 51.2 us -> none  [local(): patch_cubes.transpose(0, 2, 4, 6, 1, 3, 5, 7)]
    pallas_call x0 -> x3, Pallas kernels: none -> 38.7 us  [the longest x1 26.6 us: local(): pl.pallas_call(encode_kernel, out_shape=(jax.ShapeDtypeStruct((128, D), B...]
    dot_general x6 -> x0, matrix products: 27.1 us -> none  [the longest x1 11.8 us: local(): jnp.dot(patch_cubes, patch_weight, preferred_element_type=jnp.float32)]
    dot_general x1 -> x0, local copies, waits for them, and re-layouts: 27 us -> none  [local(): jnp.dot(patch_cubes, patch_weight, preferred_element_type=jnp.float32)]
    conv_general_dilated x2 -> x0, other arithmetic: 23.9 us -> none  [convolve_strip(): lax.conv_general_dilated(field_in, kernel, (1, 1, 1), ((0, 0), (1, 1), (1...]
  transfers between devices with their start and end apart: 7 -> 7, of which waited for: 2 -> 4; matrix products, arithmetic and copies ran while one was open for 76% -> 4% of each run, Pallas kernels for 0% -> 15%
where the time goes in v1:
time: 198 us; the launch traced here: 197 us
  waiting for transfers between devices  119 us (60%)
  Pallas kernels  38.7 us (20%)
  between operations  14.2 us (7%)
  local copies, waits for them, and re-layouts  11.3 us (6%)
  starting transfers between devices  10.2 us (5%)
  other arithmetic  4.46 us (2%)
    all_gather x1, waiting for transfers between devices, local(): wide = lax.all_gather(attend_weight.T, 'tile', axis=0, tiled=True)  92.9 us
    pallas_call x1, Pallas kernels, local(): pl.pallas_call(encode_kernel, out_shape=(jax.ShapeDtypeStruct((128, D), B...  26.6 us
    all_gather x1, waiting for transfers between devices, local(): mixing = lax.all_gather(mixing_weight.T, 'tile', axis=0, tiled=True)  18.5 us
    pallas_call x1, Pallas kernels, local(): pl.pallas_call(attend_kernel, out_shape=jax.ShapeDtypeStruct((128, 512),...  9.74 us
    unnamed x16, local copies, waits for them, and re-layouts  6.25 us
    ppermute x1, waiting for transfers between devices, local(): by_chip = lax.ppermute(normed, 'tm', [(0, 2), (2, 0), (1, 3), (3, 1)])  4.52 us
    ppermute x1, starting transfers between devices, local(): left = lax.ppermute(volume[:, 6:8], 'tile', up)  4.36 us
  transfers between devices with their start and end apart: 7, of which 4 were waited for; matrix products, arithmetic and copies ran while one was open for 4% of the time, Pallas kernels for 15%

profile of v1, /device:TPU:1, one launch (start us, length us, event | category | flops | bytes accessed | tf_op | source)
XLA Modules:
  0.0 197.3 jit_solution(14974439312902786444)
XLA Ops:
  6.5 0.0 all-gather.5.cloned.1.call-start
  6.5 0.7 all-gather.5.cloned.1.call-update
  7.3 0.0 all-gather.3.cloned.1.call-start
  7.3 0.7 all-gather.3.cloned.1.call-update
  8.0 0.8 fusion.8
  8.8 4.4 %collective-permute-start = (bf16[4,2,16,128]{3,2,1,0:T(8,128)(2,1)S(1)}, bf16[4,2,16,128]{3,2,1,0:T(8,128)(2,1)S(1)}, u32[]{:S(2)}, u32[]{:S(2)}) collective-permute-start(bf16[4,2,16,128]{3,2,1,0:T(8,128)(2,1)S(1)} %get-tuple-element.14), channel_id=1, source_target_pairs={{0,4},{4,8},{8,12},{12,16},{16,20},{20,24},{24,28},{28,32},{32,36}... | collective-permute-start | bytes 98312 | tf_op jit(solution)/shard_map/ppermute | solution.py:276
  13.2 1.3 collective-permute-start.1
  14.5 1.4 fusion.9
  16.5 0.7 convert_element_type.29
  17.2 0.1 broadcast_in_dim.7
  17.2 0.1 mul.82
  17.3 0.6 fusion.7
  17.9 0.7 add_convert_fusion
  18.6 0.1 fusion.1
  18.6 0.9 add_sine_fusion.along_y_ref
  19.6 0.9 sine_add_fusion
  20.5 0.6 pad_add_fusion.place_ref
  21.1 1.0 copy.15
  22.2 0.1 reshape.55.second_ref
  22.3 0.8 reshape.51
  23.1 2.3 %conv_weights.1 = (bf16[9,48,256]{2,1,0:T(8,128)(2,1)S(1)}, bf16[9,512,256]{2,1,0:T(8,128)(2,1)S(1)}) custom-call(bf16[16,48]{1,0:T(8,128)(2,1)S(1)} %pad.4.first_ref, bf16[144,48]{1,0:T(8,128)(2,1)S(1)} %reshape.55.second_ref), custom_call_target="tpu_custom_call" | custom-call | tf_op jit(solution)/shard_map/conv_weights/pallas_call | solution.py:295
  25.4 0.0 copy-start
  25.4 1.5 copy-done
  26.9 0.0 copy-start.5
  26.9 0.7 copy-done.5
  27.6 0.0 collective-permute-done.left_ref
  27.6 0.0 copy-start.6
  27.6 0.0 collective-permute-done.1.right_ref
  27.6 0.0 copy-start.7
  27.6 0.6 copy-done.6
  28.2 0.0 copy-done.7
  28.2 0.0 copy-start.2
  28.2 26.6 %encode.1 = (bf16[128,1024]{1,0:T(8,128)(2,1)}, bf16[128,1024]{1,0:T(8,128)(2,1)}) custom-call(s32[2]{0:T(128)} %pad_add_fusion.place_ref, bf16[4,8,16,128]{3,2,1,0:T(8,128)(2,1)} %volume_ref.1, bf16[4,2,16,128]{3,2,1,0:T(8,128)(2,1)} %copy-done.6, bf16[4,2,16,128]{3,2,1,0:T(8,128)(2,1)} %copy-done.7, bf16[9,48,256]{2,1,0:T(8,128)(2,1)} %copy-done.5, ...), custom_call_target="tpu_custom_call" | custom-call | tf_op jit(solution)/shard_map/encode/pallas_call | solution.py:307
  54.9 1.4 collective-permute-start.3
  56.3 1.2 collective-permute-start.2
  57.5 4.5 %collective-permute-done.3.n2_ref = bf16[128,1024]{1,0:T(8,128)(2,1)S(1)} collective-permute-done((bf16[128,1024]{1,0:T(8,128)(2,1)}, bf16[128,1024]{1,0:T(8,128)(2,1)S(1)}, u32[]{:S(2)}, u32[]{:S(2)}) %collective-permute-start.3) | collective-permute-done | bytes 262176 | tf_op jit(solution)/shard_map/ppermute | solution.py:341
  62.0 1.9 collective-permute-start.4
  63.9 0.0 collective-permute-done.2.n1_ref
  63.9 1.2 collective-permute-done.4.n3_ref
  65.1 18.5 %all-gather.5.cloned.1.call-done.mixing_ref = bf16[1024,1024]{1,0:T(8,128)(2,1)} async-done(((bf16[32,1024]{1,0:T(8,128)(2,1)}), bf16[1024,1024]{1,0:T(8,128)(2,1)}) %all-gather.5.cloned.1.call-update) | async-done | bytes 2097168 | tf_op jit(solution)/shard_map/all_gather | solution.py:280
  83.6 92.9 %all-gather.3.cloned.1.call-done.wide_ref = bf16[3072,1024]{1,0:T(8,128)(2,1)} async-done(((bf16[96,1024]{1,0:T(8,128)(2,1)}), bf16[3072,1024]{1,0:T(8,128)(2,1)}) %all-gather.3.cloned.1.call-update) | async-done | bytes 6291472 | tf_op jit(solution)/shard_map/all_gather | solution.py:279
  176.5 0.0 copy-done.2
  176.5 1.6 copy-done.1
  178.1 0.9 copy-done.3
  179.0 0.9 copy-done.4
  180.0 9.7 %attend.1 = bf16[128,512]{1,0:T(8,128)(2,1)S(1)} custom-call(s32[1]{0:T(128)} %bitcast.place_ref, bf16[128,1024]{1,0:T(8,128)(2,1)S(1)} %copy-done.3, bf16[128,1024]{1,0:T(8,128)(2,1)S(1)} %copy-done.4, bf16[128,1024]{1,0:T(8,128)(2,1)S(1)} %collective-permute-done.2.n1_ref, bf16[128,1024]{1,0:T(8,128)(2,1)S(1)} %collective-permute-done.3.n2_ref, ...), custom_call_target="tpu_custom_call" | custom-call | tf_op jit(solution)/shard_map/attend/pallas_call | solution.py:345
  189.7 0.1 reshape.54
  189.8 0.7 copy.18
  (5 shorter events, 0.0 us)
Async XLA Ops:
  6.5 77.0 %all-gather.5.cloned.1.call-start = ((), (), s32[]{:S(2)}) async-start(), calls=%async_computation.1 | async-start | bytes 2162688 | tf_op jit(solution)/shard_map/all_gather | solution.py:280
  7.3 169.2 %all-gather.3.cloned.1.call-start = ((), (), s32[]{:S(2)}) async-start(), calls=%async_computation | async-start | bytes 6488064 | tf_op jit(solution)/shard_map/all_gather | solution.py:279
  8.8 18.8 %collective-permute-start = (bf16[4,2,16,128]{3,2,1,0:T(8,128)(2,1)S(1)}, bf16[4,2,16,128]{3,2,1,0:T(8,128)(2,1)S(1)}, u32[]{:S(2)}, u32[]{:S(2)}) collective-permute-start(bf16[4,2,16,128]{3,2,1,0:T(8,128)(2,1)S(1)} %get-tuple-element.14), channel_id=1, source_target_pairs={{0,4},{4,8},{8,12},{12,16},{16,20},{20,24},{24,28},{28,32},{32,36}... | collective-permute-start | bytes 98312 | tf_op jit(solution)/shard_map/ppermute | solution.py:276
  13.2 14.4 %collective-permute-start.1 = (bf16[4,2,16,128]{3,2,1,0:T(8,128)(2,1)S(1)}, bf16[4,2,16,128]{3,2,1,0:T(8,128)(2,1)S(1)}, u32[]{:S(2)}, u32[]{:S(2)}) collective-permute-start(bf16[4,2,16,128]{3,2,1,0:T(8,128)(2,1)S(1)} %get-tuple-element.13), channel_id=1, source_target_pairs={{4,0},{8,4},{12,8},{16,12},{20,16},{24,20},{28,24},{32,28},{36,32}... | collective-permute-start | bytes 98312 | tf_op jit(solution)/shard_map/ppermute | solution.py:277
  25.4 1.5 copy-start
  26.9 0.7 copy-start.5
  27.6 0.6 copy-start.6
  27.6 0.6 copy-start.7
  28.2 148.3 %copy-start.2 = (bf16[1024,512]{1,0:T(8,128)(2,1)S(1)}, bf16[1024,512]{1,0:T(8,128)(2,1)}, u32[]{:S(2)}) copy-start(bf16[1024,512]{1,0:T(8,128)(2,1)} %projector_ref.1) | copy-start | bytes 3145732
  54.9 7.1 %collective-permute-start.3 = (bf16[128,1024]{1,0:T(8,128)(2,1)}, bf16[128,1024]{1,0:T(8,128)(2,1)S(1)}, u32[]{:S(2)}, u32[]{:S(2)}) collective-permute-start(bf16[128,1024]{1,0:T(8,128)(2,1)} %get-tuple-element.12.n0_ref), channel_id=1, source_target_pairs={{0,2},{2,0},{1,3},{3,1},{4,6},{6,4},{5,7},{7,5},{8,10},{10,8},{9,1... | collective-permute-start | bytes 786440 | tf_op jit(solution)/shard_map/ppermute | solution.py:341
  56.3 7.6 %collective-permute-start.2 = (bf16[128,1024]{1,0:T(8,128)(2,1)}, bf16[128,1024]{1,0:T(8,128)(2,1)S(1)}, u32[]{:S(2)}, u32[]{:S(2)}) collective-permute-start(bf16[128,1024]{1,0:T(8,128)(2,1)} %get-tuple-element.12.n0_ref), channel_id=1, source_target_pairs={{0,1},{1,0},{2,3},{3,2},{4,5},{5,4},{6,7},{7,6},{8,9},{9,8},{10,11... | collective-permute-start | bytes 786440 | tf_op jit(solution)/shard_map/ppermute | solution.py:342
  62.0 3.0 %collective-permute-start.4 = (bf16[128,1024]{1,0:T(8,128)(2,1)S(1)}, bf16[128,1024]{1,0:T(8,128)(2,1)S(1)}, u32[]{:S(2)}, u32[]{:S(2)}) collective-permute-start(bf16[128,1024]{1,0:T(8,128)(2,1)S(1)} %collective-permute-done.3.n2_ref), channel_id=1, source_target_pairs={{0,1},{1,0},{2,3},{3,2},{4,5},{5,4},{6,7},{7,6},{8,9},{9,8},{10,11... | collective-permute-start | bytes 786440 | tf_op jit(solution)/shard_map/ppermute | solution.py:343
  176.5 1.6 copy-start.1
  178.1 0.9 copy-start.3
  179.0 0.9 copy-start.4
Sparse Core Ops, SparseCore 0:
  10.5 73.0 all-gather.4
  86.6 89.7 all-gather.2

commit v2 on v1

--- a/solution.py
+++ b/solution.py
@@ -24,6 +24,7 @@
 ZM = 10
 BLK = 128
 PAIRS = 8
+EARLY = 3
 
 
 def silu(v):
@@ -67,39 +68,44 @@
         w2_ref[tap] = total.astype(BF16)
 
 
-def encode_kernel(
+def second_convolution(first, last, maps_even, maps_odd, w2_ref, second):
+    def second_step(p, carry):
+        lanes = pl.ds(pl.multiple_of(256 * p, 256), 512)
+        acc = jnp.zeros((512, 256), F32)
+        for dx in range(3):
+            for dz in range(3):
+                if dz == 1:
+                    source = maps_odd[dx : dx + 8, :, lanes]
+                else:
+                    source = maps_even[dx : dx + 8, 8 * dz : 8 * dz + 64, lanes]
+                acc = acc + jnp.dot(
+                    source.reshape(512, 512), w2_ref[3 * dx + dz], preferred_element_type=F32
+                )
+        out = silu(acc)
+        both = jnp.concatenate(
+            [out[:, :BLK].reshape(64, 8, BLK), out[:, BLK:].reshape(64, 8, BLK)], axis=1
+        )
+        second[:, pl.ds(pl.multiple_of(16 * (p - first), 16), 16), :] = both.astype(BF16)
+        return carry
+
+    lax.fori_loop(first, last, second_step, 0)
+
+
+def convolve_kernel(
     place_ref,
     volume_ref,
     left_ref,
     right_ref,
     g_ref,
     w2_ref,
-    time_ref,
-    space_ref,
-    along_y_ref,
-    patch_hbm,
-    tokens_ref,
-    normed_ref,
+    second,
+    maps_even,
+    maps_odd,
     cells,
     planes,
     taps,
     w1,
-    maps_even,
-    maps_odd,
-    second,
-    patch,
-    patch_sem,
 ):
-    copies = [
-        pltpu.make_async_copy(
-            patch_hbm.at[:, pl.ds(8 * i, 8)],
-            patch.at[:, pl.ds(8 * i, 8)],
-            patch_sem.at[i],
-        )
-        for i in range(8)
-    ]
-    for copy in copies:
-        copy.start()
     place = place_ref[0]
     count = place_ref[1]
 
@@ -151,33 +157,43 @@
 
     lax.fori_loop(0, PAIRS, first_step, 0)
 
-    def second_step(p, carry):
-        lanes = pl.ds(pl.multiple_of(256 * p, 256), 512)
-        acc = jnp.zeros((512, 256), F32)
-        for dx in range(3):
-            for dz in range(3):
-                if dz == 1:
-                    source = maps_odd[dx : dx + 8, :, lanes]
-                else:
-                    source = maps_even[dx : dx + 8, 8 * dz : 8 * dz + 64, lanes]
-                acc = acc + jnp.dot(
-                    source.reshape(512, 512), w2_ref[3 * dx + dz], preferred_element_type=F32
-                )
-        out = silu(acc)
-        both = jnp.concatenate(
-            [out[:, :BLK].reshape(64, 8, BLK), out[:, BLK:].reshape(64, 8, BLK)], axis=1
+    second_convolution(0, EARLY, maps_even, maps_odd, w2_ref, second)
+
+
+def patch_kernel(
+    early,
+    maps_even,
+    maps_odd,
+    w2_ref,
+    time_ref,
+    space_ref,
+    along_y_ref,
+    patch_hbm,
+    tokens_ref,
+    normed_ref,
+    late,
+    patch,
+    patch_sem,
+):
+    copies = [
+        pltpu.make_async_copy(
+            patch_hbm.at[:, pl.ds(8 * i, 8)],
+            patch.at[:, pl.ds(8 * i, 8)],
+            patch_sem.at[i],
         )
-        second[:, pl.ds(pl.multiple_of(16 * p, 16), 16), :] = both.astype(BF16)
-        return carry
-
-    lax.fori_loop(0, PAIRS, second_step, 0)
-
+        for i in range(8)
+    ]
+    for copy in copies:
+        copy.start()
+    second_convolution(EARLY, PAIRS, maps_even, maps_odd, w2_ref, late)
     encoded = jnp.zeros((128, D), F32)
     for x in range(8):
         copies[x].wait()
         for z in range(0, 8, 2):
             i = 8 * x + z
-            lhs = jnp.concatenate([second[i], second[i + 1]], axis=1)
+            lhs = jnp.concatenate(
+                [jnp.concatenate([early[j], late[j]], axis=0) for j in (i, i + 1)], axis=1
+            )
             rhs = jnp.concatenate(
                 [patch[:, i].reshape(BLK, D), patch[:, i + 1].reshape(BLK, D)], axis=0
             )
@@ -192,33 +208,62 @@
     normed_ref[...] = (wide * scale).astype(BF16)
 
 
+def pair_kernel(at_ref, own_ref, other_ref, by_z_ref, by_x_ref):
+    high = at_ref[1]
+    for a, ref in enumerate((by_z_ref, by_x_ref)):
+        ref[pl.ds(high, 1)] = own_ref[a : a + 1]
+        ref[pl.ds(1 - high, 1)] = other_ref[a : a + 1]
+
+
+def plane_kernel(at_ref, z0, z1, z3, z2, x0, x1, x3, x2, by_z_ref, by_x_ref):
+    for i, ref in enumerate((z0, z1, z2, z3)):
+        by_z_ref[:, pl.ds((at_ref[2] + 4 - i) % 4, 1)] = ref[...][:, None]
+    for i, ref in enumerate((x0, x1, x2, x3)):
+        by_x_ref[pl.ds((at_ref[0] + 4 - i) % 4, 1)] = ref[...][None]
+
+
 def attend_kernel(
     place_ref,
+    at_ref,
     tokens_ref,
     n0_ref,
     n1_ref,
     n2_ref,
     n3_ref,
-    wide_ref,
-    mixing_ref,
     projector_ref,
-    out_ref,
-    normed,
-    query,
-    keys,
-    attended,
+    *rest,
 ):
+    parts = rest[:16]
+    out_ref, wide, mixing, sems, normed, query, keys, attended = rest[16:]
+    copies = []
+    for i, part in enumerate(parts):
+        core = at_ref[3] if i < 8 else 1 - at_ref[3]
+        quarter = 2 * core + (i % 8) // 4
+        if i % 8 < 4:
+            spot = (at_ref[0] + 4 - i % 4) % 4
+            ends = [w.at[spot, :, :, quarter] for w in (wide, mixing)]
+        else:
+            spot = (at_ref[2] + 4 - i % 4) % 4
+            ends = [w.at[:, :, spot, quarter] for w in (wide, mixing)]
+        starts = [part.at[:, :, 0:3], part.at[:, :, 3:4]]
+        for j in range(2):
+            copies.append(pltpu.make_async_copy(starts[j], ends[j], sems.at[2 * i + j]))
+    for copy in copies:
+        copy.start()
     place = place_ref[0]
     contract = (((1,), (1,)), ((), ()))
     for i, ref in enumerate((n0_ref, n1_ref, n2_ref, n3_ref)):
         normed[128 * i : 128 * (i + 1)] = ref[...]
+    for copy in copies:
+        copy.wait()
+    columns = wide.reshape(384, 8, D)
     query[...] = lax.dot_general(
-        normed[0:128], wide_ref[0:D], contract, preferred_element_type=F32
+        normed[0:128], columns[0:128].reshape(D, D), contract, preferred_element_type=F32
     ).astype(BF16)
     for i in range(4):
         keys[:, 512 * i : 512 * (i + 1)] = lax.dot_general(
             normed[...],
-            wide_ref[D + 512 * i : D + 512 * (i + 1)],
+            columns[128 + 64 * i : 128 + 64 * (i + 1)].reshape(512, D),
             contract,
             preferred_element_type=F32,
         ).astype(BF16)
@@ -240,7 +285,7 @@
             weights.astype(BF16), v, preferred_element_type=F32
         ).astype(BF16)
     residual = tokens_ref[...].astype(F32) + lax.dot_general(
-        attended[...], mixing_ref[...], contract, preferred_element_type=F32
+        attended[...], mixing[...].reshape(D, D), contract, preferred_element_type=F32
     )
     scale = lax.rsqrt(jnp.mean(residual * residual, axis=-1, keepdims=True) + 1e-05)
     final = (residual * scale).astype(BF16)
@@ -255,6 +300,20 @@
 
 def smem():
     return pl.BlockSpec(memory_space=pltpu.SMEM)
+
+
+def send(array, where):
+    pairs = []
+    for x in range(4):
+        for y in range(4):
+            for z in range(4):
+                for c in range(2):
+                    ends = []
+                    for a, b, d, e in ((x, y, z, c), where(x, y, z, c)):
+                        a, b, d = a % 4, b % 4, d % 4
+                        ends.append(4 * (8 * a + 4 * (b // 2) + d) + 2 * (b % 2) + e)
+                    pairs.append(tuple(ends))
+    return lax.ppermute(array, ("tile", "tm"), pairs)
 
 
 def local(
@@ -276,18 +335,56 @@
     left = lax.ppermute(volume[:, 6:8], "tile", up)
     right = lax.ppermute(volume[:, 0:2], "tile", down)
 
-    wide = lax.all_gather(attend_weight.T, "tile", axis=0, tiled=True)
-    mixing = lax.all_gather(mixing_weight.T, "tile", axis=0, tiled=True)
+    core = tm_place % 2
+    at = jnp.stack([tile_place // 8, (tile_place // 4) % 2, tile_place % 4, core])
+    at = at.astype(jnp.int32)
+    shard = jnp.concatenate(
+        [attend_weight.T.reshape(4, 3, 8, D), mixing_weight.T.reshape(4, 1, 8, D)], axis=1
+    )
+    shard = lax.dynamic_slice_in_dim(shard, 2 * core, 2, axis=0)
+    other = send(shard, lambda x, y, z, c: (x, 3 - y, z, c))
+    unit = jax.ShapeDtypeStruct((2, 4, 8, D), BF16)
+    by_z, by_x = pl.pallas_call(
+        pair_kernel,
+        out_shape=(unit, unit),
+        in_specs=[smem(), vmem(), vmem()],
+        out_specs=(vmem(), vmem()),
+        name="pairs",
+    )(at, shard, other)
+    planes = [by_z] + [
+        send(by_z, lambda x, y, z, c, k=k: (x, y, z + k, c)) for k in (1, 3, 2)
+    ]
+    planes += [by_x] + [
+        send(by_x, lambda x, y, z, c, k=k: (x + k, y, z, c)) for k in (1, 3, 2)
+    ]
+    by_z, by_x = pl.pallas_call(
+        plane_kernel,
+        out_shape=(
+            jax.ShapeDtypeStruct((2, 4, 4, 8, D), BF16),
+            jax.ShapeDtypeStruct((4, 2, 4, 8, D), BF16),
+        ),
+        in_specs=[smem()] + [vmem()] * 8,
+        out_specs=(vmem(), vmem()),
+        name="planes",
+        compiler_params=pltpu.CompilerParams(vmem_limit_bytes=8 << 20),
+    )(at, *planes)
+    volume, left, right, by_z, by_x = lax.optimization_barrier(
+        (volume, left, right, by_z, by_x)
+    )
+    x_step = lambda part, k: send(part, lambda x, y, z, c: (x + k, y, z, c))
+    z_step = lambda part, k: send(part, lambda x, y, z, c: (x, y, z + k, c))
+    along = {k: x_step(by_z, k) for k in (1, 3)}
+    across = {k: z_step(by_x, k) for k in (1, 3)}
 
     frequency = jnp.exp(-math.log(1000.0) * jnp.arange(D, dtype=F32) / D)
     phase_shift = (jnp.arange(D) % 2).astype(F32) * (math.pi / 2)
     time_emb = jnp.sin(
         jnp.repeat(frame_index.astype(F32), 2)[:, None] * frequency + phase_shift
     )
-    at = lambda axis, place: (tile_offset[axis] + BLOCK_EDGE_UNITS * place).astype(F32)
-    along_x = jnp.sin(at(0, tile_place) * frequency)
-    along_z = jnp.sin(at(1, jnp.arange(8) % 2)[:, None] * frequency + 1.0)
-    along_y = jnp.sin(at(2, jnp.arange(16))[:, None] * frequency + 2.0)
+    spot = lambda axis, place: (tile_offset[axis] + BLOCK_EDGE_UNITS * place).astype(F32)
+    along_x = jnp.sin(spot(0, tile_place) * frequency)
+    along_z = jnp.sin(spot(1, jnp.arange(8) % 2)[:, None] * frequency + 1.0)
+    along_y = jnp.sin(spot(2, jnp.arange(16))[:, None] * frequency + 2.0)
 
     first = conv_first.transpose(2, 3, 1, 4, 0).reshape(9, 48)
     first = jnp.pad(first, ((0, 7), (0, 0)))
@@ -301,30 +398,29 @@
         in_specs=[vmem(), vmem()],
         out_specs=(vmem(), vmem()),
         name="conv_weights",
-        compiler_params=pltpu.CompilerParams(vmem_limit_bytes=24 << 20),
+        compiler_params=pltpu.CompilerParams(vmem_limit_bytes=12 << 20),
     )(first, second)
 
-    tokens, normed = pl.pallas_call(
-        encode_kernel,
+    early, even, odd = pl.pallas_call(
+        convolve_kernel,
         out_shape=(
-            jax.ShapeDtypeStruct((128, D), BF16),
-            jax.ShapeDtypeStruct((128, D), BF16),
+            jax.ShapeDtypeStruct((64, 16 * EARLY, BLK), BF16),
+            jax.ShapeDtypeStruct((XM, 80, 18 * BLK), BF16),
+            jax.ShapeDtypeStruct((XM, 64, 18 * BLK), BF16),
         ),
-        in_specs=[smem()] + [vmem()] * 8 + [pl.BlockSpec(memory_space=pl.ANY)],
-        out_specs=(vmem(), vmem()),
+        in_specs=[smem()] + [vmem()] * 5,
+        out_specs=(vmem(),) * 3,
         scratch_shapes=[
             pltpu.VMEM((4, XV, 16, 128), F32),
             pltpu.VMEM((XV, ZV * ROWS, 128), F32),
             pltpu.VMEM((XM, 80, 9 * BLK), BF16),
             pltpu.VMEM((9, 160, 256), BF16),
-            pltpu.VMEM((XM, 80, 18 * BLK), BF16),
-            pltpu.VMEM((XM, 64, 18 * BLK), BF16),
-            pltpu.VMEM((64, 128, BLK), BF16),
-            pltpu.VMEM((CH, 64, 8, D), BF16),
-            pltpu.SemaphoreType.DMA((8,)),
         ],
-        name="encode",
-        compiler_params=pltpu.CompilerParams(vmem_limit_bytes=56 << 20),
+        name="convolve",
+        compiler_params=pltpu.CompilerParams(vmem_limit_bytes=16 << 20),
+        cost_estimate=pl.CostEstimate(
+            flops=15_000_000_000, transcendentals=3_000_000, bytes_accessed=8_000_000
+        ),
     )(
         jnp.stack([tile_place, jnp.int32(count)]).astype(jnp.int32),
         volume,
@@ -332,12 +428,46 @@
         right,
         g,
         w2,
+    )
+    early, by_z, by_x, along[1], along[3], across[1], across[3] = (
+        lax.optimization_barrier(
+            (early, by_z, by_x, along[1], along[3], across[1], across[3])
+        )
+    )
+    along[2] = x_step(by_z, 2)
+    across[2] = z_step(by_x, 2)
+    tokens, normed = pl.pallas_call(
+        patch_kernel,
+        out_shape=(
+            jax.ShapeDtypeStruct((128, D), BF16),
+            jax.ShapeDtypeStruct((128, D), BF16),
+        ),
+        in_specs=[vmem()] * 7 + [pl.BlockSpec(memory_space=pl.ANY)],
+        out_specs=(vmem(), vmem()),
+        scratch_shapes=[
+            pltpu.VMEM((64, 16 * (PAIRS - EARLY), BLK), BF16),
+            pltpu.VMEM((CH, 64, 8, D), BF16),
+            pltpu.SemaphoreType.DMA((8,)),
+        ],
+        name="patches",
+        compiler_params=pltpu.CompilerParams(vmem_limit_bytes=28 << 20),
+        cost_estimate=pl.CostEstimate(
+            flops=0, transcendentals=0, bytes_accessed=1_000
+        ),
+    )(
+        early,
+        even,
+        odd,
+        w2,
         time_emb,
         along_x[None] + along_z,
         along_y,
         patch_weight.reshape(CH, 64, 8, D),
     )
 
+    parts = [by_z, along[1], along[2], along[3], by_x, across[1], across[2], across[3]]
+    normed, *parts = lax.optimization_barrier((normed, *parts))
+    parts += [send(part, lambda x, y, z, c: (x, y, z, 1 - c)) for part in parts]
     by_chip = lax.ppermute(normed, "tm", [(0, 2), (2, 0), (1, 3), (3, 1)])
     by_core = lax.ppermute(normed, "tm", [(0, 1), (1, 0), (2, 3), (3, 2)])
     by_both = lax.ppermute(by_chip, "tm", [(0, 1), (1, 0), (2, 3), (3, 2)])
@@ -345,26 +475,31 @@
     out = pl.pallas_call(
         attend_kernel,
         out_shape=jax.ShapeDtypeStruct((128, 512), BF16),
-        in_specs=[smem()] + [vmem()] * 8,
+        in_specs=[smem()] * 2
+        + [vmem()] * 6
+        + [pl.BlockSpec(memory_space=pl.ANY)] * len(parts),
         out_specs=vmem(),
         scratch_shapes=[
+            pltpu.VMEM((4, 2, 4, 4, 3, 8, D), BF16),
+            pltpu.VMEM((4, 2, 4, 4, 1, 8, D), BF16),
+            pltpu.SemaphoreType.DMA((2 * len(parts),)),
             pltpu.VMEM((512, D), BF16),
             pltpu.VMEM((128, D), BF16),
             pltpu.VMEM((512, 2 * D), BF16),
             pltpu.VMEM((128, D), BF16),
         ],
         name="attend",
-        compiler_params=pltpu.CompilerParams(vmem_limit_bytes=48 << 20),
+        compiler_params=pltpu.CompilerParams(vmem_limit_bytes=26 << 20),
     )(
         tm_place[None].astype(jnp.int32),
+        at,
         tokens,
         normed,
         by_core,
         by_chip,
         by_both,
-        wide,
-        mixing,
         cube_output_projector,
+        *parts,
     )
     return out.reshape(16, 4, 2, 512).transpose(1, 2, 0, 3)[:, None]
 

time: 198 us -> 98.7 us (0.50)
  waiting for transfers between devices: 119 us -> 5.53 us
  starting transfers between devices: 10.2 us -> 40.4 us
  between operations: 14.2 us -> 0.93 us
  local copies, waits for them, and re-layouts: 11.3 us -> 9.06 us
    all_gather x2 -> x0, waiting for transfers between devices: 111 us -> none  [the longest x1 92.9 us: local(): wide = lax.all_gather(attend_weight.T, 'tile', axis=0, tiled=True)]
    ppermute x0 -> x21, starting transfers between devices: none -> 30.5 us  [send(): return lax.ppermute(array, ('tile', 'tm'), pairs)]
    ppermute x1, waiting for transfers between devices: 4.52 us -> 1.37 us  [local(): by_chip = lax.ppermute(normed, 'tm', [(0, 2), (2, 0), (1, 3), (3, 1)])]
    ppermute x0 -> x21, waiting for transfers between devices: none -> 3 us  [send(): return lax.ppermute(array, ('tile', 'tm'), pairs)]
    ppermute x1, starting transfers between devices: 1.87 us -> 4.42 us  [local(): by_both = lax.ppermute(by_chip, 'tm', [(0, 1), (1, 0), (2, 3), (3, 2)])]
    unnamed x16, local copies, waits for them, and re-layouts: 6.25 us -> 4 us
    pallas_call x1 -> x4, Pallas kernels: 26.6 us -> 26.8 us  [the longest x1 14.4 us: local(): pl.pallas_call(convolve_kernel, out_shape=(jax.ShapeDtypeStruct((64, 16 *...]
  transfers between devices with their start and end apart: 7 -> 26, of which waited for: 4 -> 6; matrix products, arithmetic and copies ran while one was open for 4% -> 8% of each run, Pallas kernels for 15% -> 28%
where the time goes in v2:
time: 98.7 us; the launch traced here: 98.2 us
  starting transfers between devices  40.4 us (41%)
  Pallas kernels  38.2 us (39%)
  local copies, waits for them, and re-layouts  9.06 us (9%)
  waiting for transfers between devices  5.53 us (6%)
  other arithmetic  4.16 us (4%)
    ppermute x21, starting transfers between devices, send(): return lax.ppermute(array, ('tile', 'tm'), pairs)  30.5 us
    pallas_call x1, Pallas kernels, local(): pl.pallas_call(convolve_kernel, out_shape=(jax.ShapeDtypeStruct((64, 16 *...  14.4 us
    pallas_call x1, Pallas kernels, local(): pl.pallas_call(patch_kernel, out_shape=(jax.ShapeDtypeStruct((128, D), BF...  10.1 us
    pallas_call x1, Pallas kernels, local(): pl.pallas_call(attend_kernel, out_shape=jax.ShapeDtypeStruct((128, 512),...  9.05 us
    ppermute x1, starting transfers between devices, local(): by_both = lax.ppermute(by_chip, 'tm', [(0, 1), (1, 0), (2, 3), (3, 2)])  4.42 us
    unnamed x16, local copies, waits for them, and re-layouts  4 us
    ppermute x1, starting transfers between devices, local(): left = lax.ppermute(volume[:, 6:8], 'tile', up)  3.99 us
    ppermute x21, waiting for transfers between devices, send(): return lax.ppermute(array, ('tile', 'tm'), pairs)  3 us
  transfers between devices with their start and end apart: 26, of which 6 were waited for; matrix products, arithmetic and copies ran while one was open for 8% of the time, Pallas kernels for 28%

profile of v2, /device:TPU:1, one launch (start us, length us, event | category | flops | bytes accessed | tf_op | source)
XLA Modules:
  0.0 98.2 jit_solution(16293454253982069040)
XLA Ops:
  0.0 0.9 fusion.own_ref
  0.9 3.6 %collective-permute-start.2 = (bf16[2,4,8,1024]{3,2,1,0:T(8,128)(2,1)S(1)}, bf16[2,4,8,1024]{3,2,1,0:T(8,128)(2,1)S(1)}, u32[]{:S(2)}, u32[]{:S(2)}) collective-permute-start(bf16[2,4,8,1024]{3,2,1,0:T(8,128)(2,1)S(1)} %fusion.own_ref), channel_id=1, source_target_pairs={{0,18},{1,19},{4,22},{5,23},{8,26},{9,27},{12,30},{13,31},{2,16},{... | collective-permute-start | bytes 393224 | tf_op jit(solution)/shard_map/ppermute | solution.py:316
  4.6 0.8 fusion.9
  5.3 1.4 %fusion.10 = (s32[1]{0:T(128)}, s32[1]{0:T(128)}, s32[1]{0:T(128)}) fusion(s32[3]{0:T(128)} %param.11), kind=kLoop, calls=%fused_computation.24 | loop fusion | bytes 24 | tf_op jit(solution)/shard_map/slice | solution.py:384
  7.4 0.6 pad_add_fusion.at_ref
  8.0 0.7 copy-done.7
  8.7 1.7 %pairs.1 = (bf16[2,4,8,1024]{3,2,1,0:T(8,128)(2,1)}, bf16[2,4,8,1024]{3,2,1,0:T(8,128)(2,1)}) custom-call(s32[4]{0:T(128)} %pad_add_fusion.at_ref, bf16[2,4,8,1024]{3,2,1,0:T(8,128)(2,1)} %copy-done.6, bf16[2,4,8,1024]{3,2,1,0:T(8,128)(2,1)} %copy-done.7), custom_call_target="tpu_custom_call" | custom-call | tf_op jit(solution)/shard_map/pairs/pallas_call | solution.py:347
  10.4 3.6 %collective-permute-start.5 = (bf16[2,4,8,1024]{3,2,1,0:T(8,128)(2,1)}, bf16[2,4,8,1024]{3,2,1,0:T(8,128)(2,1)S(1)}, u32[]{:S(2)}, u32[]{:S(2)}) collective-permute-start(bf16[2,4,8,1024]{3,2,1,0:T(8,128)(2,1)} %get-tuple-element.37.z0), channel_id=1, source_target_pairs={{0,8},{1,9},{4,12},{5,13},{8,0},{9,1},{12,4},{13,5},{2,10},{3,11},... | collective-permute-start | bytes 393224 | tf_op jit(solution)/shard_map/ppermute | solution.py:316
  14.0 0.5 collective-permute-start.4
  14.5 1.0 %collective-permute-start.3 = (bf16[2,4,8,1024]{3,2,1,0:T(8,128)(2,1)}, bf16[2,4,8,1024]{3,2,1,0:T(8,128)(2,1)S(1)}, u32[]{:S(2)}, u32[]{:S(2)}) collective-permute-start(bf16[2,4,8,1024]{3,2,1,0:T(8,128)(2,1)} %get-tuple-element.37.z0), channel_id=1, source_target_pairs={{0,4},{1,5},{4,8},{5,9},{8,12},{9,13},{12,0},{13,1},{2,6},{3,7},{6... | collective-permute-start | bytes 393224 | tf_op jit(solution)/shard_map/ppermute | solution.py:316
  15.6 2.7 %collective-permute-start.8 = (bf16[2,4,8,1024]{3,2,1,0:T(8,128)(2,1)}, bf16[2,4,8,1024]{3,2,1,0:T(8,128)(2,1)S(1)}, u32[]{:S(2)}, u32[]{:S(2)}) collective-permute-start(bf16[2,4,8,1024]{3,2,1,0:T(8,128)(2,1)} %get-tuple-element.38.x0), channel_id=1, source_target_pairs={{0,64},{1,65},{4,68},{5,69},{8,72},{9,73},{12,76},{13,77},{2,66},{... | collective-permute-start | bytes 393224 | tf_op jit(solution)/shard_map/ppermute | solution.py:316
  18.3 0.9 collective-permute-start.7
  19.2 0.6 collective-permute-start.6
  19.8 0.7 add_convert_fusion
  20.5 1.3 %collective-permute-start.1 = (bf16[4,2,16,128]{3,2,1,0:T(8,128)(2,1)S(1)}, bf16[4,2,16,128]{3,2,1,0:T(8,128)(2,1)S(1)}, u32[]{:S(2)}, u32[]{:S(2)}) collective-permute-start(bf16[4,2,16,128]{3,2,1,0:T(8,128)(2,1)S(1)} %get-tuple-element.69), channel_id=1, source_target_pairs={{4,0},{8,4},{12,8},{16,12},{20,16},{24,20},{28,24},{32,28},{36,32}... | collective-permute-start | bytes 98312 | tf_op jit(solution)/shard_map/ppermute | solution.py:336
  21.8 4.0 %collective-permute-start = (bf16[4,2,16,128]{3,2,1,0:T(8,128)(2,1)S(1)}, bf16[4,2,16,128]{3,2,1,0:T(8,128)(2,1)S(1)}, u32[]{:S(2)}, u32[]{:S(2)}) collective-permute-start(bf16[4,2,16,128]{3,2,1,0:T(8,128)(2,1)S(1)} %get-tuple-element.70), channel_id=1, source_target_pairs={{0,4},{4,8},{8,12},{12,16},{16,20},{20,24},{24,28},{28,32},{32,36}... | collective-permute-start | bytes 98312 | tf_op jit(solution)/shard_map/ppermute | solution.py:335
  25.9 0.7 convert_element_type.29
  26.7 0.8 reshape.59
  27.5 1.0 %copy.15 = bf16[3,3,16,3,16]{4,3,2,1,0:T(4,128)(2,1)S(1)} copy(bf16[3,3,16,3,16]{2,4,3,1,0:T(8,128)(2,1)} %bitcast.27) | data formatting | bytes 27648 | tf_op jit(solution)/shard_map/reshape | solution.py:391
  28.7 2.3 %conv_weights.1 = (bf16[9,48,256]{2,1,0:T(8,128)(2,1)S(1)}, bf16[9,512,256]{2,1,0:T(8,128)(2,1)S(1)}) custom-call(bf16[16,48]{1,0:T(8,128)(2,1)S(1)} %pad.4.first_ref, bf16[144,48]{1,0:T(8,128)(2,1)S(1)} %reshape.63.second_ref), custom_call_target="tpu_custom_call" | custom-call | tf_op jit(solution)/shard_map/conv_weights/pallas_call | solution.py:392
  31.0 0.9 copy-done.1
  31.9 0.9 copy-done.2
  32.8 0.6 copy-done.4
  33.4 0.6 planes.1
  34.1 4.9 %collective-permute-start.10 = (bf16[2,4,4,8,1024]{4,3,2,1,0:T(8,128)(2,1)S(1)}, bf16[2,4,4,8,1024]{4,3,2,1,0:T(8,128)(2,1)S(1)}, u32[]{:S(2)}, u32[]{:S(2)}) collective-permute-start(bf16[2,4,4,8,1024]{4,3,2,1,0:T(8,128)(2,1)S(1)} %get-tuple-element.61.rest_0_), channel_id=1, source_target_pairs={{0,96},{1,97},{4,100},{5,101},{8,104},{9,105},{12,108},{13,109},{2... | collective-permute-start | bytes 1572872 | tf_op jit(solution)/shard_map/ppermute | solution.py:316
  39.0 4.6 %collective-permute-start.12 = (bf16[4,2,4,8,1024]{4,3,2,1,0:T(8,128)(2,1)S(1)}, bf16[4,2,4,8,1024]{4,3,2,1,0:T(8,128)(2,1)S(1)}, u32[]{:S(2)}, u32[]{:S(2)}) collective-permute-start(bf16[4,2,4,8,1024]{4,3,2,1,0:T(8,128)(2,1)S(1)} %get-tuple-element.65.rest_4_), channel_id=1, source_target_pairs={{0,12},{1,13},{4,0},{5,1},{8,4},{9,5},{12,8},{13,9},{2,14},{3,15},... | collective-permute-start | bytes 1572872 | tf_op jit(solution)/shard_map/ppermute | solution.py:316
  43.7 0.9 copy-done.3
  44.6 14.4 %convolve.1 = (bf16[64,48,128]{2,1,0:T(8,128)(2,1)S(1)}, bf16[10,80,2304]{2,1,0:T(8,128)(2,1)S(1)}, bf16[10,64,2304]{2,1,0:T(8,128)(2,1)S(1)}) custom-call(s32[2]{0:T(128)S(1)} %pad_add_fusion.1.place_ref, bf16[4,8,16,128]{3,2,1,0:T(8,128)(2,1)S(1)} %copy-done.3, bf16[4,2,16,128]{3,2,1,0:T(8,128)(2,1)S(1)} %collective-permute-done.left_ref, ...), custom_call_target="tpu_custom_call" | custom-call | flops 15000000512 | bytes 8000000 | tf_op jit(solution)/shard_map/convolve/pallas_call | solution.py:404
  59.0 1.8 %collective-permute-start.13 = (bf16[2,4,4,8,1024]{4,3,2,1,0:T(8,128)(2,1)S(1)}, bf16[2,4,4,8,1024]{4,3,2,1,0:T(8,128)(2,1)S(1)}, u32[]{:S(2)}, u32[]{:S(2)}) collective-permute-start(bf16[2,4,4,8,1024]{4,3,2,1,0:T(8,128)(2,1)S(1)} %get-tuple-element.61.rest_0_), channel_id=1, source_target_pairs={{0,64},{1,65},{4,68},{5,69},{8,72},{9,73},{12,76},{13,77},{2,66},{... | collective-permute-start | bytes 1572872 | tf_op jit(solution)/shard_map/ppermute | solution.py:316
  60.9 1.2 %collective-permute-start.14 = (bf16[4,2,4,8,1024]{4,3,2,1,0:T(8,128)(2,1)S(1)}, bf16[4,2,4,8,1024]{4,3,2,1,0:T(8,128)(2,1)S(1)}, u32[]{:S(2)}, u32[]{:S(2)}) collective-permute-start(bf16[4,2,4,8,1024]{4,3,2,1,0:T(8,128)(2,1)S(1)} %get-tuple-element.65.rest_4_), channel_id=1, source_target_pairs={{0,8},{1,9},{4,12},{5,13},{8,0},{9,1},{12,4},{13,5},{2,10},{3,11},... | collective-permute-start | bytes 1572872 | tf_op jit(solution)/shard_map/ppermute | solution.py:316
  62.0 0.6 fusion.8
  62.6 0.3 add_sine_fusion.along_y_ref
  62.9 0.3 sine_add_fusion
  63.2 10.1 %patches.1 = (bf16[128,1024]{1,0:T(8,128)(2,1)S(1)}, bf16[128,1024]{1,0:T(8,128)(2,1)S(1)}) custom-call(bf16[64,48,128]{2,1,0:T(8,128)(2,1)S(1)} %get-tuple-element.49.early, bf16[10,80,2304]{2,1,0:T(8,128)(2,1)S(1)} %get-tuple-element.50.maps_even, bf16[10,64,2304]{2,1,0:T(8,128)(2,1)S(1)} %get-tuple-element.51.maps_odd, ...), custom_call_target="tpu_custom_call" | custom-call | bytes 1000 | tf_op jit(solution)/shard_map/patches/pallas_call | solution.py:439
  73.5 3.3 %collective-permute-start.18 = (bf16[2,4,4,8,1024]{4,3,2,1,0:T(8,128)(2,1)S(1)}, bf16[2,4,4,8,1024]{4,3,2,1,0:T(8,128)(2,1)S(1)}, u32[]{:S(2)}, u32[]{:S(2)}) collective-permute-start(bf16[2,4,4,8,1024]{4,3,2,1,0:T(8,128)(2,1)S(1)} %get-tuple-element.61.rest_0_), channel_id=1, source_target_pairs={{0,1},{1,0},{4,5},{5,4},{8,9},{9,8},{12,13},{13,12},{2,3},{3,2},{6... | collective-permute-start | bytes 1572872 | tf_op jit(solution)/shard_map/ppermute | solution.py:316
  76.8 0.5 collective-permute-start.20
  77.3 1.4 %collective-permute-done.16.n2_ref = bf16[128,1024]{1,0:T(8,128)(2,1)S(1)} collective-permute-done((bf16[128,1024]{1,0:T(8,128)(2,1)S(1)}, bf16[128,1024]{1,0:T(8,128)(2,1)S(1)}, u32[]{:S(2)}, u32[]{:S(2)}) %collective-permute-start.16) | collective-permute-done | bytes 262176 | tf_op jit(solution)/shard_map/ppermute | solution.py:471
  78.7 4.4 %collective-permute-start.17 = (bf16[128,1024]{1,0:T(8,128)(2,1)S(1)}, bf16[128,1024]{1,0:T(8,128)(2,1)S(1)}, u32[]{:S(2)}, u32[]{:S(2)}) collective-permute-start(bf16[128,1024]{1,0:T(8,128)(2,1)S(1)} %collective-permute-done.16.n2_ref), channel_id=1, source_target_pairs={{0,1},{1,0},{2,3},{3,2},{4,5},{5,4},{6,7},{7,6},{8,9},{9,8},{10,11... | collective-permute-start | bytes 786440 | tf_op jit(solution)/shard_map/ppermute | solution.py:473
  83.1 1.2 %collective-permute-done.17.n3_ref = bf16[128,1024]{1,0:T(8,128)(2,1)S(1)} collective-permute-done((bf16[128,1024]{1,0:T(8,128)(2,1)S(1)}, bf16[128,1024]{1,0:T(8,128)(2,1)S(1)}, u32[]{:S(2)}, u32[]{:S(2)}) %collective-permute-start.17) | collective-permute-done | bytes 262176 | tf_op jit(solution)/shard_map/ppermute | solution.py:473
  84.2 0.4 collective-permute-start.22
  84.8 0.4 collective-permute-start.24
  85.1 0.3 collective-permute-start.25
  85.4 0.7 collective-permute-done.22.rest_12_
  86.2 0.7 collective-permute-done.23.rest_13_
  86.9 0.7 collective-permute-done.24.rest_14_
  87.7 0.7 collective-permute-done.25.rest_15_
  88.4 9.0 %attend.1 = bf16[128,512]{1,0:T(8,128)(2,1)S(1)} custom-call(s32[1]{0:T(128)} %bitcast.place_ref, s32[4]{0:T(128)S(1)} %copy-done.5, bf16[128,1024]{1,0:T(8,128)(2,1)S(1)} %get-tuple-element.52.tokens_ref, bf16[128,1024]{1,0:T(8,128)(2,1)S(1)} %get-tuple-element.60.n0_ref, bf16[128,1024]{1,0:T(8,128)(2,1)S(1)} %collective-permute-done.15.n1_ref, ...), custom_call_target="tpu_custom_call" | custom-call | tf_op jit(solution)/shard_map/attend/pallas_call | solution.py:475
  97.5 0.7 copy.18
  (46 shorter events, 0.9 us)
Async XLA Ops:
  0.9 7.1 %copy-start.6 = (bf16[2,4,8,1024]{3,2,1,0:T(8,128)(2,1)}, bf16[2,4,8,1024]{3,2,1,0:T(8,128)(2,1)S(1)}, u32[]{:S(2)}) copy-start(bf16[2,4,8,1024]{3,2,1,0:T(8,128)(2,1)S(1)} %fusion.own_ref) | copy-start | bytes 393220
  0.9 7.1 %collective-permute-start.2 = (bf16[2,4,8,1024]{3,2,1,0:T(8,128)(2,1)S(1)}, bf16[2,4,8,1024]{3,2,1,0:T(8,128)(2,1)S(1)}, u32[]{:S(2)}, u32[]{:S(2)}) collective-permute-start(bf16[2,4,8,1024]{3,2,1,0:T(8,128)(2,1)S(1)} %fusion.own_ref), channel_id=1, source_target_pairs={{0,18},{1,19},{4,22},{5,23},{8,26},{9,27},{12,30},{13,31},{2,16},{... | collective-permute-start | bytes 393224 | tf_op jit(solution)/shard_map/ppermute | solution.py:316
  8.0 0.7 copy-start.7
  10.4 8.8 %collective-permute-start.5 = (bf16[2,4,8,1024]{3,2,1,0:T(8,128)(2,1)}, bf16[2,4,8,1024]{3,2,1,0:T(8,128)(2,1)S(1)}, u32[]{:S(2)}, u32[]{:S(2)}) collective-permute-start(bf16[2,4,8,1024]{3,2,1,0:T(8,128)(2,1)} %get-tuple-element.37.z0), channel_id=1, source_target_pairs={{0,8},{1,9},{4,12},{5,13},{8,0},{9,1},{12,4},{13,5},{2,10},{3,11},... | collective-permute-start | bytes 393224 | tf_op jit(solution)/shard_map/ppermute | solution.py:316
  14.0 6.5 %collective-permute-start.4 = (bf16[2,4,8,1024]{3,2,1,0:T(8,128)(2,1)}, bf16[2,4,8,1024]{3,2,1,0:T(8,128)(2,1)S(1)}, u32[]{:S(2)}, u32[]{:S(2)}) collective-permute-start(bf16[2,4,8,1024]{3,2,1,0:T(8,128)(2,1)} %get-tuple-element.37.z0), channel_id=1, source_target_pairs={{0,12},{1,13},{4,0},{5,1},{8,4},{9,5},{12,8},{13,9},{2,14},{3,15},... | collective-permute-start | bytes 393224 | tf_op jit(solution)/shard_map/ppermute | solution.py:316
  14.5 7.3 %collective-permute-start.3 = (bf16[2,4,8,1024]{3,2,1,0:T(8,128)(2,1)}, bf16[2,4,8,1024]{3,2,1,0:T(8,128)(2,1)S(1)}, u32[]{:S(2)}, u32[]{:S(2)}) collective-permute-start(bf16[2,4,8,1024]{3,2,1,0:T(8,128)(2,1)} %get-tuple-element.37.z0), channel_id=1, source_target_pairs={{0,4},{1,5},{4,8},{5,9},{8,12},{9,13},{12,0},{13,1},{2,6},{3,7},{6... | collective-permute-start | bytes 393224 | tf_op jit(solution)/shard_map/ppermute | solution.py:316
  15.6 15.4 %collective-permute-start.8 = (bf16[2,4,8,1024]{3,2,1,0:T(8,128)(2,1)}, bf16[2,4,8,1024]{3,2,1,0:T(8,128)(2,1)S(1)}, u32[]{:S(2)}, u32[]{:S(2)}) collective-permute-start(bf16[2,4,8,1024]{3,2,1,0:T(8,128)(2,1)} %get-tuple-element.38.x0), channel_id=1, source_target_pairs={{0,64},{1,65},{4,68},{5,69},{8,72},{9,73},{12,76},{13,77},{2,66},{... | collective-permute-start | bytes 393224 | tf_op jit(solution)/shard_map/ppermute | solution.py:316
  18.3 12.7 %collective-permute-start.7 = (bf16[2,4,8,1024]{3,2,1,0:T(8,128)(2,1)}, bf16[2,4,8,1024]{3,2,1,0:T(8,128)(2,1)S(1)}, u32[]{:S(2)}, u32[]{:S(2)}) collective-permute-start(bf16[2,4,8,1024]{3,2,1,0:T(8,128)(2,1)} %get-tuple-element.38.x0), channel_id=1, source_target_pairs={{0,96},{1,97},{4,100},{5,101},{8,104},{9,105},{12,108},{13,109},{2... | collective-permute-start | bytes 393224 | tf_op jit(solution)/shard_map/ppermute | solution.py:316
  19.2 11.8 %collective-permute-start.6 = (bf16[2,4,8,1024]{3,2,1,0:T(8,128)(2,1)}, bf16[2,4,8,1024]{3,2,1,0:T(8,128)(2,1)S(1)}, u32[]{:S(2)}, u32[]{:S(2)}) collective-permute-start(bf16[2,4,8,1024]{3,2,1,0:T(8,128)(2,1)} %get-tuple-element.38.x0), channel_id=1, source_target_pairs={{0,32},{1,33},{4,36},{5,37},{8,40},{9,41},{12,44},{13,45},{2,34},{... | collective-permute-start | bytes 393224 | tf_op jit(solution)/shard_map/ppermute | solution.py:316
  20.5 13.6 %collective-permute-start.1 = (bf16[4,2,16,128]{3,2,1,0:T(8,128)(2,1)S(1)}, bf16[4,2,16,128]{3,2,1,0:T(8,128)(2,1)S(1)}, u32[]{:S(2)}, u32[]{:S(2)}) collective-permute-start(bf16[4,2,16,128]{3,2,1,0:T(8,128)(2,1)S(1)} %get-tuple-element.69), channel_id=1, source_target_pairs={{4,0},{8,4},{12,8},{16,12},{20,16},{24,20},{28,24},{32,28},{36,32}... | collective-permute-start | bytes 98312 | tf_op jit(solution)/shard_map/ppermute | solution.py:336
  21.8 12.3 %collective-permute-start = (bf16[4,2,16,128]{3,2,1,0:T(8,128)(2,1)S(1)}, bf16[4,2,16,128]{3,2,1,0:T(8,128)(2,1)S(1)}, u32[]{:S(2)}, u32[]{:S(2)}) collective-permute-start(bf16[4,2,16,128]{3,2,1,0:T(8,128)(2,1)S(1)} %get-tuple-element.70), channel_id=1, source_target_pairs={{0,4},{4,8},{8,12},{12,16},{16,20},{20,24},{24,28},{28,32},{32,36}... | collective-permute-start | bytes 98312 | tf_op jit(solution)/shard_map/ppermute | solution.py:335
  31.0 0.9 copy-start.1
  31.9 0.9 copy-start.2
  32.8 0.6 copy-start.4
  34.1 24.9 %collective-permute-start.10 = (bf16[2,4,4,8,1024]{4,3,2,1,0:T(8,128)(2,1)S(1)}, bf16[2,4,4,8,1024]{4,3,2,1,0:T(8,128)(2,1)S(1)}, u32[]{:S(2)}, u32[]{:S(2)}) collective-permute-start(bf16[2,4,4,8,1024]{4,3,2,1,0:T(8,128)(2,1)S(1)} %get-tuple-element.61.rest_0_), channel_id=1, source_target_pairs={{0,96},{1,97},{4,100},{5,101},{8,104},{9,105},{12,108},{13,109},{2... | collective-permute-start | bytes 1572872 | tf_op jit(solution)/shard_map/ppermute | solution.py:316
  39.0 20.0 %collective-permute-start.9 = (bf16[2,4,4,8,1024]{4,3,2,1,0:T(8,128)(2,1)S(1)}, bf16[2,4,4,8,1024]{4,3,2,1,0:T(8,128)(2,1)S(1)}, u32[]{:S(2)}, u32[]{:S(2)}) collective-permute-start(bf16[2,4,4,8,1024]{4,3,2,1,0:T(8,128)(2,1)S(1)} %get-tuple-element.61.rest_0_), channel_id=1, source_target_pairs={{0,32},{1,33},{4,36},{5,37},{8,40},{9,41},{12,44},{13,45},{2,34},{... | collective-permute-start | bytes 1572872 | tf_op jit(solution)/shard_map/ppermute | solution.py:316
  39.0 20.0 %collective-permute-start.12 = (bf16[4,2,4,8,1024]{4,3,2,1,0:T(8,128)(2,1)S(1)}, bf16[4,2,4,8,1024]{4,3,2,1,0:T(8,128)(2,1)S(1)}, u32[]{:S(2)}, u32[]{:S(2)}) collective-permute-start(bf16[4,2,4,8,1024]{4,3,2,1,0:T(8,128)(2,1)S(1)} %get-tuple-element.65.rest_4_), channel_id=1, source_target_pairs={{0,12},{1,13},{4,0},{5,1},{8,4},{9,5},{12,8},{13,9},{2,14},{3,15},... | collective-permute-start | bytes 1572872 | tf_op jit(solution)/shard_map/ppermute | solution.py:316
  43.7 15.4 %collective-permute-start.11 = (bf16[4,2,4,8,1024]{4,3,2,1,0:T(8,128)(2,1)S(1)}, bf16[4,2,4,8,1024]{4,3,2,1,0:T(8,128)(2,1)S(1)}, u32[]{:S(2)}, u32[]{:S(2)}) collective-permute-start(bf16[4,2,4,8,1024]{4,3,2,1,0:T(8,128)(2,1)S(1)} %get-tuple-element.65.rest_4_), channel_id=1, source_target_pairs={{0,4},{1,5},{4,8},{5,9},{8,12},{9,13},{12,0},{13,1},{2,6},{3,7},{6... | collective-permute-start | bytes 1572872 | tf_op jit(solution)/shard_map/ppermute | solution.py:316
  43.7 0.9 copy-start.3
  59.0 14.3 %collective-permute-start.13 = (bf16[2,4,4,8,1024]{4,3,2,1,0:T(8,128)(2,1)S(1)}, bf16[2,4,4,8,1024]{4,3,2,1,0:T(8,128)(2,1)S(1)}, u32[]{:S(2)}, u32[]{:S(2)}) collective-permute-start(bf16[2,4,4,8,1024]{4,3,2,1,0:T(8,128)(2,1)S(1)} %get-tuple-element.61.rest_0_), channel_id=1, source_target_pairs={{0,64},{1,65},{4,68},{5,69},{8,72},{9,73},{12,76},{13,77},{2,66},{... | collective-permute-start | bytes 1572872 | tf_op jit(solution)/shard_map/ppermute | solution.py:316
  60.9 12.5 %collective-permute-start.14 = (bf16[4,2,4,8,1024]{4,3,2,1,0:T(8,128)(2,1)S(1)}, bf16[4,2,4,8,1024]{4,3,2,1,0:T(8,128)(2,1)S(1)}, u32[]{:S(2)}, u32[]{:S(2)}) collective-permute-start(bf16[4,2,4,8,1024]{4,3,2,1,0:T(8,128)(2,1)S(1)} %get-tuple-element.65.rest_4_), channel_id=1, source_target_pairs={{0,8},{1,9},{4,12},{5,13},{8,0},{9,1},{12,4},{13,5},{2,10},{3,11},... | collective-permute-start | bytes 1572872 | tf_op jit(solution)/shard_map/ppermute | solution.py:316
  63.2 25.2 %copy-start = (bf16[1024,512]{1,0:T(8,128)(2,1)S(1)}, bf16[1024,512]{1,0:T(8,128)(2,1)}, u32[]{:S(2)}) copy-start(bf16[1024,512]{1,0:T(8,128)(2,1)} %projector_ref.1) | copy-start | bytes 3145732
  63.2 25.2 %copy-start.5 = (s32[4]{0:T(128)S(1)}, s32[4]{0:T(128)}, u32[]{:S(2)}) copy-start(s32[4]{0:T(128)} %pad_add_fusion.at_ref) | copy-start | bytes 52
  73.4 5.3 %collective-permute-start.16 = (bf16[128,1024]{1,0:T(8,128)(2,1)S(1)}, bf16[128,1024]{1,0:T(8,128)(2,1)S(1)}, u32[]{:S(2)}, u32[]{:S(2)}) collective-permute-start(bf16[128,1024]{1,0:T(8,128)(2,1)S(1)} %get-tuple-element.60.n0_ref), channel_id=1, source_target_pairs={{0,2},{2,0},{1,3},{3,1},{4,6},{6,4},{5,7},{7,5},{8,10},{10,8},{9,1... | collective-permute-start | bytes 786440 | tf_op jit(solution)/shard_map/ppermute | solution.py:471
  73.5 11.2 %collective-permute-start.18 = (bf16[2,4,4,8,1024]{4,3,2,1,0:T(8,128)(2,1)S(1)}, bf16[2,4,4,8,1024]{4,3,2,1,0:T(8,128)(2,1)S(1)}, u32[]{:S(2)}, u32[]{:S(2)}) collective-permute-start(bf16[2,4,4,8,1024]{4,3,2,1,0:T(8,128)(2,1)S(1)} %get-tuple-element.61.rest_0_), channel_id=1, source_target_pairs={{0,1},{1,0},{4,5},{5,4},{8,9},{9,8},{12,13},{13,12},{2,3},{3,2},{6... | collective-permute-start | bytes 1572872 | tf_op jit(solution)/shard_map/ppermute | solution.py:316
  76.7 8.0 %collective-permute-start.19 = (bf16[2,4,4,8,1024]{4,3,2,1,0:T(8,128)(2,1)S(1)}, bf16[2,4,4,8,1024]{4,3,2,1,0:T(8,128)(2,1)S(1)}, u32[]{:S(2)}, u32[]{:S(2)}) collective-permute-start(bf16[2,4,4,8,1024]{4,3,2,1,0:T(8,128)(2,1)S(1)} %collective-permute-done.9.rest_1_), channel_id=1, source_target_pairs={{0,1},{1,0},{4,5},{5,4},{8,9},{9,8},{12,13},{13,12},{2,3},{3,2},{6... | collective-permute-start | bytes 1572872 | tf_op jit(solution)/shard_map/ppermute | solution.py:316
  76.8 8.4 %collective-permute-start.20 = (bf16[2,4,4,8,1024]{4,3,2,1,0:T(8,128)(2,1)S(1)}, bf16[2,4,4,8,1024]{4,3,2,1,0:T(8,128)(2,1)S(1)}, u32[]{:S(2)}, u32[]{:S(2)}) collective-permute-start(bf16[2,4,4,8,1024]{4,3,2,1,0:T(8,128)(2,1)S(1)} %collective-permute-done.13.rest_2_), channel_id=1, source_target_pairs={{0,1},{1,0},{4,5},{5,4},{8,9},{9,8},{12,13},{13,12},{2,3},{3,2},{6... | collective-permute-start | bytes 1572872 | tf_op jit(solution)/shard_map/ppermute | solution.py:316
  77.3 5.8 %collective-permute-start.15 = (bf16[128,1024]{1,0:T(8,128)(2,1)S(1)}, bf16[128,1024]{1,0:T(8,128)(2,1)S(1)}, u32[]{:S(2)}, u32[]{:S(2)}) collective-permute-start(bf16[128,1024]{1,0:T(8,128)(2,1)S(1)} %get-tuple-element.60.n0_ref), channel_id=1, source_target_pairs={{0,1},{1,0},{2,3},{3,2},{4,5},{5,4},{6,7},{7,6},{8,9},{9,8},{10,11... | collective-permute-start | bytes 786440 | tf_op jit(solution)/shard_map/ppermute | solution.py:472
  78.7 5.6 %collective-permute-start.17 = (bf16[128,1024]{1,0:T(8,128)(2,1)S(1)}, bf16[128,1024]{1,0:T(8,128)(2,1)S(1)}, u32[]{:S(2)}, u32[]{:S(2)}) collective-permute-start(bf16[128,1024]{1,0:T(8,128)(2,1)S(1)} %collective-permute-done.16.n2_ref), channel_id=1, source_target_pairs={{0,1},{1,0},{2,3},{3,2},{4,5},{5,4},{6,7},{7,6},{8,9},{9,8},{10,11... | collective-permute-start | bytes 786440 | tf_op jit(solution)/shard_map/ppermute | solution.py:473
  83.1 2.4 %collective-permute-start.21 = (bf16[2,4,4,8,1024]{4,3,2,1,0:T(8,128)(2,1)S(1)}, bf16[2,4,4,8,1024]{4,3,2,1,0:T(8,128)(2,1)S(1)}, u32[]{:S(2)}, u32[]{:S(2)}) collective-permute-start(bf16[2,4,4,8,1024]{4,3,2,1,0:T(8,128)(2,1)S(1)} %collective-permute-done.10.rest_3_), channel_id=1, source_target_pairs={{0,1},{1,0},{4,5},{5,4},{8,9},{9,8},{12,13},{13,12},{2,3},{3,2},{6... | collective-permute-start | bytes 1572872 | tf_op jit(solution)/shard_map/ppermute | solution.py:316
  84.2 1.9 %collective-permute-start.22 = (bf16[4,2,4,8,1024]{4,3,2,1,0:T(8,128)(2,1)S(1)}, bf16[4,2,4,8,1024]{4,3,2,1,0:T(8,128)(2,1)S(1)}, u32[]{:S(2)}, u32[]{:S(2)}) collective-permute-start(bf16[4,2,4,8,1024]{4,3,2,1,0:T(8,128)(2,1)S(1)} %get-tuple-element.65.rest_4_), channel_id=1, source_target_pairs={{0,1},{1,0},{4,5},{5,4},{8,9},{9,8},{12,13},{13,12},{2,3},{3,2},{6... | collective-permute-start | bytes 1572872 | tf_op jit(solution)/shard_map/ppermute | solution.py:316
  84.6 2.3 %collective-permute-start.23 = (bf16[4,2,4,8,1024]{4,3,2,1,0:T(8,128)(2,1)S(1)}, bf16[4,2,4,8,1024]{4,3,2,1,0:T(8,128)(2,1)S(1)}, u32[]{:S(2)}, u32[]{:S(2)}) collective-permute-start(bf16[4,2,4,8,1024]{4,3,2,1,0:T(8,128)(2,1)S(1)} %collective-permute-done.11.rest_5_), channel_id=1, source_target_pairs={{0,1},{1,0},{4,5},{5,4},{8,9},{9,8},{12,13},{13,12},{2,3},{3,2},{6... | collective-permute-start | bytes 1572872 | tf_op jit(solution)/shard_map/ppermute | solution.py:316
  84.8 2.9 %collective-permute-start.24 = (bf16[4,2,4,8,1024]{4,3,2,1,0:T(8,128)(2,1)S(1)}, bf16[4,2,4,8,1024]{4,3,2,1,0:T(8,128)(2,1)S(1)}, u32[]{:S(2)}, u32[]{:S(2)}) collective-permute-start(bf16[4,2,4,8,1024]{4,3,2,1,0:T(8,128)(2,1)S(1)} %collective-permute-done.14.rest_6_), channel_id=1, source_target_pairs={{0,1},{1,0},{4,5},{5,4},{8,9},{9,8},{12,13},{13,12},{2,3},{3,2},{6... | collective-permute-start | bytes 1572872 | tf_op jit(solution)/shard_map/ppermute | solution.py:316
  85.1 3.3 %collective-permute-start.25 = (bf16[4,2,4,8,1024]{4,3,2,1,0:T(8,128)(2,1)S(1)}, bf16[4,2,4,8,1024]{4,3,2,1,0:T(8,128)(2,1)S(1)}, u32[]{:S(2)}, u32[]{:S(2)}) collective-permute-start(bf16[4,2,4,8,1024]{4,3,2,1,0:T(8,128)(2,1)S(1)} %collective-permute-done.12.rest_7_), channel_id=1, source_target_pairs={{0,1},{1,0},{4,5},{5,4},{8,9},{9,8},{12,13},{13,12},{2,3},{3,2},{6... | collective-permute-start | bytes 1572872 | tf_op jit(solution)/shard_map/ppermute | solution.py:316

commit v3 on v1

--- a/solution.py
+++ b/solution.py
@@ -67,6 +67,29 @@
         w2_ref[tap] = total.astype(BF16)
 
 
+def second_convolution(maps_even, maps_odd, w2_ref, second):
+    def second_step(p, carry):
+        lanes = pl.ds(pl.multiple_of(256 * p, 256), 512)
+        acc = jnp.zeros((512, 256), F32)
+        for dx in range(3):
+            for dz in range(3):
+                if dz == 1:
+                    source = maps_odd[dx : dx + 8, :, lanes]
+                else:
+                    source = maps_even[dx : dx + 8, 8 * dz : 8 * dz + 64, lanes]
+                acc = acc + jnp.dot(
+                    source.reshape(512, 512), w2_ref[3 * dx + dz], preferred_element_type=F32
+                )
+        out = silu(acc)
+        both = jnp.concatenate(
+            [out[:, :BLK].reshape(64, 8, BLK), out[:, BLK:].reshape(64, 8, BLK)], axis=1
+        )
+        second[:, pl.ds(pl.multiple_of(16 * p, 16), 16), :] = both.astype(BF16)
+        return carry
+
+    lax.fori_loop(0, PAIRS, second_step, 0)
+
+
 def encode_kernel(
     place_ref,
     volume_ref,
@@ -80,13 +103,13 @@
     patch_hbm,
     tokens_ref,
     normed_ref,
+    second,
+    maps_even,
+    maps_odd,
     cells,
     planes,
     taps,
     w1,
-    maps_even,
-    maps_odd,
-    second,
     patch,
     patch_sem,
 ):
@@ -151,27 +174,7 @@
 
     lax.fori_loop(0, PAIRS, first_step, 0)
 
-    def second_step(p, carry):
-        lanes = pl.ds(pl.multiple_of(256 * p, 256), 512)
-        acc = jnp.zeros((512, 256), F32)
-        for dx in range(3):
-            for dz in range(3):
-                if dz == 1:
-                    source = maps_odd[dx : dx + 8, :, lanes]
-                else:
-                    source = maps_even[dx : dx + 8, 8 * dz : 8 * dz + 64, lanes]
-                acc = acc + jnp.dot(
-                    source.reshape(512, 512), w2_ref[3 * dx + dz], preferred_element_type=F32
-                )
-        out = silu(acc)
-        both = jnp.concatenate(
-            [out[:, :BLK].reshape(64, 8, BLK), out[:, BLK:].reshape(64, 8, BLK)], axis=1
-        )
-        second[:, pl.ds(pl.multiple_of(16 * p, 16), 16), :] = both.astype(BF16)
-        return carry
-
-    lax.fori_loop(0, PAIRS, second_step, 0)
-
+    second_convolution(maps_even, maps_odd, w2_ref, second)
     encoded = jnp.zeros((128, D), F32)
     for x in range(8):
         copies[x].wait()
@@ -192,33 +195,75 @@
     normed_ref[...] = (wide * scale).astype(BF16)
 
 
+def pair_kernel(at_ref, own_ref, other_ref, pair_ref):
+    high = at_ref[1]
+    pair_ref[pl.ds(high, 1)] = own_ref[...][None]
+    pair_ref[pl.ds(1 - high, 1)] = other_ref[...][None]
+
+
+def plane_kernel(at_ref, own_ref, one_ref, three_ref, two_ref, plane_ref):
+    spot = jnp.where(at_ref[3] == 0, at_ref[2], at_ref[0])
+    for i, ref in enumerate((own_ref, one_ref, two_ref, three_ref)):
+        plane_ref[pl.ds((spot + 4 - i) % 4, 1)] = ref[...][None]
+
+
 def attend_kernel(
     place_ref,
+    at_ref,
     tokens_ref,
     n0_ref,
     n1_ref,
     n2_ref,
     n3_ref,
-    wide_ref,
-    mixing_ref,
     projector_ref,
-    out_ref,
-    normed,
-    query,
-    keys,
-    attended,
+    *rest,
 ):
+    parts = rest[:8]
+    out_ref, wide, mixing, sems, normed, query, keys, attended = rest[8:]
+
+    def copies(core):
+        out = []
+        for i, part in enumerate(parts):
+            owner = core if i < 4 else 1 - core
+            spot = (at_ref[2 * owner] + 4 - i % 4) % 4
+            for high in range(2):
+                for j, weight in enumerate((wide, mixing)):
+                    if owner == 0:
+                        end = weight.at[spot, high, :, owner]
+                    else:
+                        end = weight.at[:, high, spot, owner]
+                    start = part.at[:, high, 0:6] if j == 0 else part.at[:, high, 6:8]
+                    out.append(
+                        pltpu.make_async_copy(start, end, sems.at[4 * i + 2 * high + j])
+                    )
+        return out
+
+    for core in range(2):
+
+        @pl.when(at_ref[3] == core)
+        def _():
+            for copy in copies(core):
+                copy.start()
+
     place = place_ref[0]
     contract = (((1,), (1,)), ((), ()))
     for i, ref in enumerate((n0_ref, n1_ref, n2_ref, n3_ref)):
         normed[128 * i : 128 * (i + 1)] = ref[...]
+    for core in range(2):
+
+        @pl.when(at_ref[3] == core)
+        def _():
+            for copy in copies(core):
+                copy.wait()
+
+    columns = wide.reshape(384, 8, D)
     query[...] = lax.dot_general(
-        normed[0:128], wide_ref[0:D], contract, preferred_element_type=F32
+        normed[0:128], columns[0:128].reshape(D, D), contract, preferred_element_type=F32
     ).astype(BF16)
     for i in range(4):
         keys[:, 512 * i : 512 * (i + 1)] = lax.dot_general(
             normed[...],
-            wide_ref[D + 512 * i : D + 512 * (i + 1)],
+            columns[128 + 64 * i : 128 + 64 * (i + 1)].reshape(512, D),
             contract,
             preferred_element_type=F32,
         ).astype(BF16)
@@ -240,7 +285,7 @@
             weights.astype(BF16), v, preferred_element_type=F32
         ).astype(BF16)
     residual = tokens_ref[...].astype(F32) + lax.dot_general(
-        attended[...], mixing_ref[...], contract, preferred_element_type=F32
+        attended[...], mixing[...].reshape(D, D), contract, preferred_element_type=F32
     )
     scale = lax.rsqrt(jnp.mean(residual * residual, axis=-1, keepdims=True) + 1e-05)
     final = (residual * scale).astype(BF16)
@@ -255,6 +300,20 @@
 
 def smem():
     return pl.BlockSpec(memory_space=pltpu.SMEM)
+
+
+def send(array, where):
+    pairs = []
+    for x in range(4):
+        for y in range(4):
+            for z in range(4):
+                for c in range(2):
+                    ends = []
+                    for a, b, d, e in ((x, y, z, c), where(x, y, z, c)):
+                        a, b, d = a % 4, b % 4, d % 4
+                        ends.append(4 * (8 * a + 4 * (b // 2) + d) + 2 * (b % 2) + e)
+                    pairs.append(tuple(ends))
+    return lax.ppermute(array, ("tile", "tm"), pairs)
 
 
 def local(
@@ -276,18 +335,49 @@
     left = lax.ppermute(volume[:, 6:8], "tile", up)
     right = lax.ppermute(volume[:, 0:2], "tile", down)
 
-    wide = lax.all_gather(attend_weight.T, "tile", axis=0, tiled=True)
-    mixing = lax.all_gather(mixing_weight.T, "tile", axis=0, tiled=True)
+    core = tm_place % 2
+    at = jnp.stack([tile_place // 8, (tile_place // 4) % 2, tile_place % 4, core])
+    at = at.astype(jnp.int32)
+    shard = jnp.concatenate(
+        [attend_weight.T.reshape(2, 6, 8, D), mixing_weight.T.reshape(2, 2, 8, D)], axis=1
+    )
+    shard = lax.dynamic_index_in_dim(shard, core, axis=0, keepdims=False)
+    other = send(shard, lambda x, y, z, c: (x, 3 - y, z, c))
+    pair = pl.pallas_call(
+        pair_kernel,
+        out_shape=jax.ShapeDtypeStruct((2, 8, 8, D), BF16),
+        in_specs=[smem(), vmem(), vmem()],
+        out_specs=vmem(),
+        name="pairs",
+    )(at, shard, other)
+    line = lambda part, k: send(
+        part, lambda x, y, z, c: (x + k * c, y, z + k * (1 - c), c)
+    )
+    cross = lambda part, k: send(
+        part, lambda x, y, z, c: (x + k * (1 - c), y, z + k * c, c)
+    )
+    swap = lambda part: send(part, lambda x, y, z, c: (x, y, z, 1 - c))
+    plane = pl.pallas_call(
+        plane_kernel,
+        out_shape=jax.ShapeDtypeStruct((4, 2, 8, 8, D), BF16),
+        in_specs=[smem()] + [vmem()] * 4,
+        out_specs=vmem(),
+        name="planes",
+        compiler_params=pltpu.CompilerParams(vmem_limit_bytes=8 << 20),
+    )(at, pair, line(pair, 1), line(pair, 3), line(pair, 2))
+    volume, left, right, plane = lax.optimization_barrier((volume, left, right, plane))
+    one, two, three = cross(plane, 1), cross(plane, 2), cross(plane, 3)
+    swapped = swap(plane)
 
     frequency = jnp.exp(-math.log(1000.0) * jnp.arange(D, dtype=F32) / D)
     phase_shift = (jnp.arange(D) % 2).astype(F32) * (math.pi / 2)
     time_emb = jnp.sin(
         jnp.repeat(frame_index.astype(F32), 2)[:, None] * frequency + phase_shift
     )
-    at = lambda axis, place: (tile_offset[axis] + BLOCK_EDGE_UNITS * place).astype(F32)
-    along_x = jnp.sin(at(0, tile_place) * frequency)
-    along_z = jnp.sin(at(1, jnp.arange(8) % 2)[:, None] * frequency + 1.0)
-    along_y = jnp.sin(at(2, jnp.arange(16))[:, None] * frequency + 2.0)
+    spot = lambda axis, place: (tile_offset[axis] + BLOCK_EDGE_UNITS * place).astype(F32)
+    along_x = jnp.sin(spot(0, tile_place) * frequency)
+    along_z = jnp.sin(spot(1, jnp.arange(8) % 2)[:, None] * frequency + 1.0)
+    along_y = jnp.sin(spot(2, jnp.arange(16))[:, None] * frequency + 2.0)
 
     first = conv_first.transpose(2, 3, 1, 4, 0).reshape(9, 48)
     first = jnp.pad(first, ((0, 7), (0, 0)))
@@ -301,7 +391,7 @@
         in_specs=[vmem(), vmem()],
         out_specs=(vmem(), vmem()),
         name="conv_weights",
-        compiler_params=pltpu.CompilerParams(vmem_limit_bytes=24 << 20),
+        compiler_params=pltpu.CompilerParams(vmem_limit_bytes=12 << 20),
     )(first, second)
 
     tokens, normed = pl.pallas_call(
@@ -313,18 +403,21 @@
         in_specs=[smem()] + [vmem()] * 8 + [pl.BlockSpec(memory_space=pl.ANY)],
         out_specs=(vmem(), vmem()),
         scratch_shapes=[
+            pltpu.VMEM((64, 128, BLK), BF16),
+            pltpu.VMEM((XM, 80, 18 * BLK), BF16),
+            pltpu.VMEM((XM, 64, 18 * BLK), BF16),
             pltpu.VMEM((4, XV, 16, 128), F32),
             pltpu.VMEM((XV, ZV * ROWS, 128), F32),
             pltpu.VMEM((XM, 80, 9 * BLK), BF16),
             pltpu.VMEM((9, 160, 256), BF16),
-            pltpu.VMEM((XM, 80, 18 * BLK), BF16),
-            pltpu.VMEM((XM, 64, 18 * BLK), BF16),
-            pltpu.VMEM((64, 128, BLK), BF16),
             pltpu.VMEM((CH, 64, 8, D), BF16),
             pltpu.SemaphoreType.DMA((8,)),
         ],
         name="encode",
-        compiler_params=pltpu.CompilerParams(vmem_limit_bytes=56 << 20),
+        compiler_params=pltpu.CompilerParams(vmem_limit_bytes=40 << 20),
+        cost_estimate=pl.CostEstimate(
+            flops=15_000_000_000, transcendentals=3_000_000, bytes_accessed=20_000_000
+        ),
     )(
         jnp.stack([tile_place, jnp.int32(count)]).astype(jnp.int32),
         volume,
@@ -337,7 +430,10 @@
         along_y,
         patch_weight.reshape(CH, 64, 8, D),
     )
-
+    normed, one, two, three, swapped = lax.optimization_barrier(
+        (normed, one, two, three, swapped)
+    )
+    parts = [plane, one, two, three, swapped, swap(one), swap(two), swap(three)]
     by_chip = lax.ppermute(normed, "tm", [(0, 2), (2, 0), (1, 3), (3, 1)])
     by_core = lax.ppermute(normed, "tm", [(0, 1), (1, 0), (2, 3), (3, 2)])
     by_both = lax.ppermute(by_chip, "tm", [(0, 1), (1, 0), (2, 3), (3, 2)])
@@ -345,26 +441,31 @@
     out = pl.pallas_call(
         attend_kernel,
         out_shape=jax.ShapeDtypeStruct((128, 512), BF16),
-        in_specs=[smem()] + [vmem()] * 8,
+        in_specs=[smem()] * 2
+        + [vmem()] * 6
+        + [pl.BlockSpec(memory_space=pl.ANY)] * len(parts),
         out_specs=vmem(),
         scratch_shapes=[
+            pltpu.VMEM((4, 2, 4, 2, 6, 8, D), BF16),
+            pltpu.VMEM((4, 2, 4, 2, 2, 8, D), BF16),
+            pltpu.SemaphoreType.DMA((4 * len(parts),)),
             pltpu.VMEM((512, D), BF16),
             pltpu.VMEM((128, D), BF16),
             pltpu.VMEM((512, 2 * D), BF16),
             pltpu.VMEM((128, D), BF16),
         ],
         name="attend",
-        compiler_params=pltpu.CompilerParams(vmem_limit_bytes=48 << 20),
+        compiler_params=pltpu.CompilerParams(vmem_limit_bytes=26 << 20),
     )(
         tm_place[None].astype(jnp.int32),
+        at,
         tokens,
         normed,
         by_core,
         by_chip,
         by_both,
-        wide,
-        mixing,
         cube_output_projector,
+        *parts,
     )
     return out.reshape(16, 4, 2, 512).transpose(1, 2, 0, 3)[:, None]
 

time: 198 us -> 90.1 us (0.46)
  waiting for transfers between devices: 119 us -> 10.3 us
  starting transfers between devices: 10.2 us -> 27.4 us
  between operations: 14.2 us -> 0.89 us
  local copies, waits for them, and re-layouts: 11.3 us -> 8.17 us
    all_gather x2 -> x0, waiting for transfers between devices: 111 us -> none  [the longest x1 92.9 us: local(): wide = lax.all_gather(attend_weight.T, 'tile', axis=0, tiled=True)]
    ppermute x0 -> x11, starting transfers between devices: none -> 20 us  [send(): return lax.ppermute(array, ('tile', 'tm'), pairs)]
    unnamed x16 -> x12, local copies, waits for them, and re-layouts: 6.25 us -> 3.1 us
    ppermute x1, waiting for transfers between devices: 4.52 us -> 7.63 us  [local(): by_chip = lax.ppermute(normed, 'tm', [(0, 2), (2, 0), (1, 3), (3, 1)])]
    pallas_call x0 -> x2, Pallas kernels: none -> 2.31 us  [the longest x1 1.69 us: local(): pl.pallas_call(pair_kernel, out_shape=jax.ShapeDtypeStruct((2, 8, 8, D),...]
    pallas_call x1, Pallas kernels: 26.6 us -> 24.5 us  [local(): pl.pallas_call(encode_kernel, out_shape=(jax.ShapeDtypeStruct((128, D), B...]
  transfers between devices with their start and end apart: 7 -> 16, of which waited for: 4 -> 5; matrix products, arithmetic and copies ran while one was open for 4% -> 9% of each run, Pallas kernels for 15% -> 32%
where the time goes in v3:
time: 90.1 us; the launch traced here: 89.7 us
  Pallas kernels  38.8 us (43%)
  starting transfers between devices  27.4 us (30%)
  waiting for transfers between devices  10.3 us (11%)
  local copies, waits for them, and re-layouts  8.17 us (9%)
  other arithmetic  4.2 us (5%)
    pallas_call x1, Pallas kernels, local(): pl.pallas_call(encode_kernel, out_shape=(jax.ShapeDtypeStruct((128, D), B...  24.5 us
    ppermute x11, starting transfers between devices, send(): return lax.ppermute(array, ('tile', 'tm'), pairs)  20 us
    pallas_call x1, Pallas kernels, local(): pl.pallas_call(attend_kernel, out_shape=jax.ShapeDtypeStruct((128, 512),...  9.64 us
    ppermute x1, waiting for transfers between devices, local(): by_chip = lax.ppermute(normed, 'tm', [(0, 2), (2, 0), (1, 3), (3, 1)])  7.63 us
    ppermute x1, starting transfers between devices, local(): left = lax.ppermute(volume[:, 6:8], 'tile', up)  5 us
    unnamed x12, local copies, waits for them, and re-layouts  3.1 us
    pallas_call x1, Pallas kernels, local(): pl.pallas_call(weights_kernel, out_shape=(jax.ShapeDtypeStruct((9, 48, 25...  2.32 us
  transfers between devices with their start and end apart: 16, of which 5 were waited for; matrix products, arithmetic and copies ran while one was open for 9% of the time, Pallas kernels for 32%

profile of v3, /device:TPU:1, one launch (start us, length us, event | category | flops | bytes accessed | tf_op | source)
XLA Modules:
  0.0 89.7 jit_solution(480477175186760306)
XLA Ops:
  0.0 0.8 fusion.10
  0.8 1.3 %collective-permute-start.1 = (bf16[4,2,16,128]{3,2,1,0:T(8,128)(2,1)S(1)}, bf16[4,2,16,128]{3,2,1,0:T(8,128)(2,1)S(1)}, u32[]{:S(2)}, u32[]{:S(2)}) collective-permute-start(bf16[4,2,16,128]{3,2,1,0:T(8,128)(2,1)S(1)} %get-tuple-element.31), channel_id=1, source_target_pairs={{4,0},{8,4},{12,8},{16,12},{20,16},{24,20},{28,24},{32,28},{36,32}... | collective-permute-start | bytes 98312 | tf_op jit(solution)/shard_map/ppermute | solution.py:336
  2.1 5.0 %collective-permute-start = (bf16[4,2,16,128]{3,2,1,0:T(8,128)(2,1)S(1)}, bf16[4,2,16,128]{3,2,1,0:T(8,128)(2,1)S(1)}, u32[]{:S(2)}, u32[]{:S(2)}) collective-permute-start(bf16[4,2,16,128]{3,2,1,0:T(8,128)(2,1)S(1)} %get-tuple-element.32), channel_id=1, source_target_pairs={{0,4},{4,8},{8,12},{12,16},{16,20},{20,24},{24,28},{28,32},{32,36}... | collective-permute-start | bytes 98312 | tf_op jit(solution)/shard_map/ppermute | solution.py:335
  7.1 0.9 %fusion.1.own_ref = bf16[8,8,1024]{2,1,0:T(8,128)(2,1)S(1)} fusion(s32[]{:T(128)S(6)} %select_n.51, bf16[2,6,8,1024]{3,2,1,0:T(8,128)(2,1)} %bitcast.27, bf16[2,2,8,1024]{3,2,1,0:T(8,128)(2,1)} %bitcast.29), kind=kLoop, calls=%fused_computation.3 | loop fusion | flops 65536 | bytes 393220 | tf_op jit(solution)/shard_map/jit(dynamic_index_in_dim)/squeeze | solution.py:344
  8.0 0.0 copy-start.4
  8.0 5.6 %collective-permute-start.2 = (bf16[8,8,1024]{2,1,0:T(8,128)(2,1)S(1)}, bf16[8,8,1024]{2,1,0:T(8,128)(2,1)S(1)}, u32[]{:S(2)}, u32[]{:S(2)}) collective-permute-start(bf16[8,8,1024]{2,1,0:T(8,128)(2,1)S(1)} %fusion.1.own_ref), channel_id=1, source_target_pairs={{0,18},{1,19},{4,22},{5,23},{8,26},{9,27},{12,30},{13,31},{2,16},{... | collective-permute-start | bytes 393224 | tf_op jit(solution)/shard_map/ppermute | solution.py:316
  13.6 0.7 convert_element_type.29
  14.3 0.1 broadcast_in_dim.7
  14.4 0.1 mul.82
  14.5 1.4 %fusion.11 = (s32[1]{0:T(128)}, s32[1]{0:T(128)}, s32[1]{0:T(128)}) fusion(s32[3]{0:T(128)} %param.11), kind=kLoop, calls=%fused_computation.25 | loop fusion | bytes 24 | tf_op jit(solution)/shard_map/slice | solution.py:377
  16.5 0.6 fusion.9
  17.2 0.1 fusion.3
  17.2 0.3 sine_add_fusion
  17.5 0.7 add_convert_fusion
  18.3 0.6 pad_add_fusion.at_ref
  18.8 0.6 copy-done.5
  19.5 1.7 %pairs.1.own_ref = bf16[2,8,8,1024]{3,2,1,0:T(8,128)(2,1)} custom-call(s32[4]{0:T(128)} %pad_add_fusion.at_ref, bf16[8,8,1024]{2,1,0:T(8,128)(2,1)} %copy-done.4, bf16[8,8,1024]{2,1,0:T(8,128)(2,1)} %copy-done.5), custom_call_target="tpu_custom_call" | custom-call | tf_op jit(solution)/shard_map/pairs/pallas_call | solution.py:346
  21.2 2.7 %collective-permute-start.5 = (bf16[2,8,8,1024]{3,2,1,0:T(8,128)(2,1)}, bf16[2,8,8,1024]{3,2,1,0:T(8,128)(2,1)S(1)}, u32[]{:S(2)}, u32[]{:S(2)}) collective-permute-start(bf16[2,8,8,1024]{3,2,1,0:T(8,128)(2,1)} %pairs.1.own_ref), channel_id=1, source_target_pairs={{0,8},{1,65},{4,12},{5,69},{8,0},{9,73},{12,4},{13,77},{2,10},{3,6... | collective-permute-start | bytes 786440 | tf_op jit(solution)/shard_map/ppermute | solution.py:316
  23.9 0.9 collective-permute-start.4
  24.8 0.6 collective-permute-start.3
  25.4 0.3 add_sine_fusion.along_y_ref
  25.7 0.1 pad_add_fusion.1.place_ref
  25.8 0.8 reshape.59
  26.6 1.0 %copy.15 = bf16[3,3,16,3,16]{4,3,2,1,0:T(4,128)(2,1)S(1)} copy(bf16[3,3,16,3,16]{2,4,3,1,0:T(8,128)(2,1)} %bitcast.28) | data formatting | bytes 27648 | tf_op jit(solution)/shard_map/reshape | solution.py:384
  27.6 0.1 reshape.63.second_ref
  27.7 2.3 %conv_weights.1 = (bf16[9,48,256]{2,1,0:T(8,128)(2,1)S(1)}, bf16[9,512,256]{2,1,0:T(8,128)(2,1)S(1)}) custom-call(bf16[16,48]{1,0:T(8,128)(2,1)S(1)} %pad.4.first_ref, bf16[144,48]{1,0:T(8,128)(2,1)S(1)} %reshape.63.second_ref), custom_call_target="tpu_custom_call" | custom-call | tf_op jit(solution)/shard_map/conv_weights/pallas_call | solution.py:385
  30.1 0.0 collective-permute-done.5.two_ref
  30.1 1.0 %collective-permute-done.4.three_ref = bf16[2,8,8,1024]{3,2,1,0:T(8,128)(2,1)S(1)} collective-permute-done((bf16[2,8,8,1024]{3,2,1,0:T(8,128)(2,1)}, bf16[2,8,8,1024]{3,2,1,0:T(8,128)(2,1)S(1)}, u32[]{:S(2)}, u32[]{:S(2)}) %collective-permute-start.4) | collective-permute-done | bytes 262176 | tf_op jit(solution)/shard_map/ppermute | solution.py:316
  31.1 0.4 collective-permute-done.3.one_ref
  31.4 0.9 %copy-done = bf16[2,8,8,1024]{3,2,1,0:T(8,128)(2,1)S(1)} copy-done((bf16[2,8,8,1024]{3,2,1,0:T(8,128)(2,1)S(1)}, bf16[2,8,8,1024]{3,2,1,0:T(8,128)(2,1)}, u32[]{:S(2)}) %copy-start) | copy-done | bytes 262168
  32.4 0.6 copy-done.3
  33.0 0.6 planes.1.rest_0_
  33.6 5.2 %collective-permute-start.9 = (bf16[4,2,8,8,1024]{4,3,2,1,0:T(8,128)(2,1)S(1)}, bf16[4,2,8,8,1024]{4,3,2,1,0:T(8,128)(2,1)S(1)}, u32[]{:S(2)}, u32[]{:S(2)}) collective-permute-start(bf16[4,2,8,8,1024]{4,3,2,1,0:T(8,128)(2,1)S(1)} %planes.1.rest_0_), channel_id=1, source_target_pairs={{0,1},{1,0},{4,5},{5,4},{8,9},{9,8},{12,13},{13,12},{2,3},{3,2},{6... | collective-permute-start | bytes 3145736 | tf_op jit(solution)/shard_map/ppermute | solution.py:316
  38.8 2.1 %collective-permute-start.8 = (bf16[4,2,8,8,1024]{4,3,2,1,0:T(8,128)(2,1)S(1)}, bf16[4,2,8,8,1024]{4,3,2,1,0:T(8,128)(2,1)S(1)}, u32[]{:S(2)}, u32[]{:S(2)}) collective-permute-start(bf16[4,2,8,8,1024]{4,3,2,1,0:T(8,128)(2,1)S(1)} %planes.1.rest_0_), channel_id=1, source_target_pairs={{0,96},{1,13},{4,100},{5,1},{8,104},{9,5},{12,108},{13,9},{2,98},{... | collective-permute-start | bytes 3145736 | tf_op jit(solution)/shard_map/ppermute | solution.py:316
  40.9 0.6 collective-permute-start.6
  41.5 0.9 %copy-done.2 = bf16[4,8,16,128]{3,2,1,0:T(8,128)(2,1)S(1)} copy-done((bf16[4,8,16,128]{3,2,1,0:T(8,128)(2,1)S(1)}, bf16[4,8,16,128]{3,2,1,0:T(8,128)(2,1)}, u32[]{:S(2)}) %copy-start.2) | copy-done | bytes 131096
  42.4 24.5 %encode.1 = (bf16[128,1024]{1,0:T(8,128)(2,1)S(1)}, bf16[128,1024]{1,0:T(8,128)(2,1)S(1)}) custom-call(s32[2]{0:T(128)S(1)} %pad_add_fusion.1.place_ref, bf16[4,8,16,128]{3,2,1,0:T(8,128)(2,1)S(1)} %copy-done.2, bf16[4,2,16,128]{3,2,1,0:T(8,128)(2,1)S(1)} %collective-permute-done.left_ref, bf16[4,2,16,128]{3,2,1,0:T(8,128)(2,1)S(1)} %collective-permute-done.1.right_ref, ...), custom_call_target="tpu_custom_call" | custom-call | flops 15000000512 | bytes 20000000 | tf_op jit(solution)/shard_map/encode/pallas_call | solution.py:397
  66.9 0.1 collective-permute-done.6.rest_1_
  67.0 1.9 %collective-permute-start.13 = (bf16[4,2,8,8,1024]{4,3,2,1,0:T(8,128)(2,1)S(1)}, bf16[4,2,8,8,1024]{4,3,2,1,0:T(8,128)(2,1)S(1)}, u32[]{:S(2)}, u32[]{:S(2)}) collective-permute-start(bf16[4,2,8,8,1024]{4,3,2,1,0:T(8,128)(2,1)S(1)} %collective-permute-done.6.rest_1_), channel_id=1, source_target_pairs={{0,1},{1,0},{4,5},{5,4},{8,9},{9,8},{12,13},{13,12},{2,3},{3,2},{6... | collective-permute-start | bytes 3145736 | tf_op jit(solution)/shard_map/ppermute | solution.py:316
  68.9 0.1 collective-permute-start.14
  69.0 0.4 collective-permute-start.15
  69.4 0.2 collective-permute-start.10
  69.6 7.6 %collective-permute-done.11.n2_ref = bf16[128,1024]{1,0:T(8,128)(2,1)S(1)} collective-permute-done((bf16[128,1024]{1,0:T(8,128)(2,1)S(1)}, bf16[128,1024]{1,0:T(8,128)(2,1)S(1)}, u32[]{:S(2)}, u32[]{:S(2)}) %collective-permute-start.11) | collective-permute-done | bytes 262176 | tf_op jit(solution)/shard_map/ppermute | solution.py:437
  77.2 0.9 collective-permute-start.12
  78.1 1.2 %collective-permute-done.12.n3_ref = bf16[128,1024]{1,0:T(8,128)(2,1)S(1)} collective-permute-done((bf16[128,1024]{1,0:T(8,128)(2,1)S(1)}, bf16[128,1024]{1,0:T(8,128)(2,1)S(1)}, u32[]{:S(2)}, u32[]{:S(2)}) %collective-permute-start.12) | collective-permute-done | bytes 262176 | tf_op jit(solution)/shard_map/ppermute | solution.py:439
  79.3 9.6 %attend.1 = bf16[128,512]{1,0:T(8,128)(2,1)S(1)} custom-call(s32[1]{0:T(128)} %bitcast.place_ref, s32[4]{0:T(128)S(1)} %copy-done.3, bf16[128,1024]{1,0:T(8,128)(2,1)S(1)} %get-tuple-element.23.tokens_ref, bf16[128,1024]{1,0:T(8,128)(2,1)S(1)} %get-tuple-element.26.n0_ref, bf16[128,1024]{1,0:T(8,128)(2,1)S(1)} %collective-permute-done.10.n1_ref, ...), custom_call_target="tpu_custom_call" | custom-call | tf_op jit(solution)/shard_map/attend/pallas_call | solution.py:441
  88.9 0.1 reshape.62
  89.0 0.7 copy.18
  (21 shorter events, 0.1 us)
Async XLA Ops:
  0.8 32.8 %collective-permute-start.1 = (bf16[4,2,16,128]{3,2,1,0:T(8,128)(2,1)S(1)}, bf16[4,2,16,128]{3,2,1,0:T(8,128)(2,1)S(1)}, u32[]{:S(2)}, u32[]{:S(2)}) collective-permute-start(bf16[4,2,16,128]{3,2,1,0:T(8,128)(2,1)S(1)} %get-tuple-element.31), channel_id=1, source_target_pairs={{4,0},{8,4},{12,8},{16,12},{20,16},{24,20},{28,24},{32,28},{36,32}... | collective-permute-start | bytes 98312 | tf_op jit(solution)/shard_map/ppermute | solution.py:336
  2.1 31.5 %collective-permute-start = (bf16[4,2,16,128]{3,2,1,0:T(8,128)(2,1)S(1)}, bf16[4,2,16,128]{3,2,1,0:T(8,128)(2,1)S(1)}, u32[]{:S(2)}, u32[]{:S(2)}) collective-permute-start(bf16[4,2,16,128]{3,2,1,0:T(8,128)(2,1)S(1)} %get-tuple-element.32), channel_id=1, source_target_pairs={{0,4},{4,8},{8,12},{12,16},{16,20},{20,24},{24,28},{28,32},{32,36}... | collective-permute-start | bytes 98312 | tf_op jit(solution)/shard_map/ppermute | solution.py:335
  8.0 10.8 %copy-start.4 = (bf16[8,8,1024]{2,1,0:T(8,128)(2,1)}, bf16[8,8,1024]{2,1,0:T(8,128)(2,1)S(1)}, u32[]{:S(2)}) copy-start(bf16[8,8,1024]{2,1,0:T(8,128)(2,1)S(1)} %fusion.1.own_ref) | copy-start | bytes 393220
  8.0 10.8 %collective-permute-start.2 = (bf16[8,8,1024]{2,1,0:T(8,128)(2,1)S(1)}, bf16[8,8,1024]{2,1,0:T(8,128)(2,1)S(1)}, u32[]{:S(2)}, u32[]{:S(2)}) collective-permute-start(bf16[8,8,1024]{2,1,0:T(8,128)(2,1)S(1)} %fusion.1.own_ref), channel_id=1, source_target_pairs={{0,18},{1,19},{4,22},{5,23},{8,26},{9,27},{12,30},{13,31},{2,16},{... | collective-permute-start | bytes 393224 | tf_op jit(solution)/shard_map/ppermute | solution.py:316
  18.8 0.6 copy-start.5
  21.2 8.9 %collective-permute-start.5 = (bf16[2,8,8,1024]{3,2,1,0:T(8,128)(2,1)}, bf16[2,8,8,1024]{3,2,1,0:T(8,128)(2,1)S(1)}, u32[]{:S(2)}, u32[]{:S(2)}) collective-permute-start(bf16[2,8,8,1024]{3,2,1,0:T(8,128)(2,1)} %pairs.1.own_ref), channel_id=1, source_target_pairs={{0,8},{1,65},{4,12},{5,69},{8,0},{9,73},{12,4},{13,77},{2,10},{3,6... | collective-permute-start | bytes 786440 | tf_op jit(solution)/shard_map/ppermute | solution.py:316
  23.9 7.1 %collective-permute-start.4 = (bf16[2,8,8,1024]{3,2,1,0:T(8,128)(2,1)}, bf16[2,8,8,1024]{3,2,1,0:T(8,128)(2,1)S(1)}, u32[]{:S(2)}, u32[]{:S(2)}) collective-permute-start(bf16[2,8,8,1024]{3,2,1,0:T(8,128)(2,1)} %pairs.1.own_ref), channel_id=1, source_target_pairs={{0,12},{1,97},{4,0},{5,101},{8,4},{9,105},{12,8},{13,109},{2,14},{... | collective-permute-start | bytes 786440 | tf_op jit(solution)/shard_map/ppermute | solution.py:316
  24.8 6.6 %collective-permute-start.3 = (bf16[2,8,8,1024]{3,2,1,0:T(8,128)(2,1)}, bf16[2,8,8,1024]{3,2,1,0:T(8,128)(2,1)S(1)}, u32[]{:S(2)}, u32[]{:S(2)}) collective-permute-start(bf16[2,8,8,1024]{3,2,1,0:T(8,128)(2,1)} %pairs.1.own_ref), channel_id=1, source_target_pairs={{0,4},{1,33},{4,8},{5,37},{8,12},{9,41},{12,0},{13,45},{2,6},{3,35... | collective-permute-start | bytes 786440 | tf_op jit(solution)/shard_map/ppermute | solution.py:316
  31.4 1.0 %copy-start = (bf16[2,8,8,1024]{3,2,1,0:T(8,128)(2,1)S(1)}, bf16[2,8,8,1024]{3,2,1,0:T(8,128)(2,1)}, u32[]{:S(2)}) copy-start(bf16[2,8,8,1024]{3,2,1,0:T(8,128)(2,1)} %pairs.1.own_ref) | copy-start | bytes 786436
  32.4 0.6 copy-start.3
  33.6 33.2 %collective-permute-start.9 = (bf16[4,2,8,8,1024]{4,3,2,1,0:T(8,128)(2,1)S(1)}, bf16[4,2,8,8,1024]{4,3,2,1,0:T(8,128)(2,1)S(1)}, u32[]{:S(2)}, u32[]{:S(2)}) collective-permute-start(bf16[4,2,8,8,1024]{4,3,2,1,0:T(8,128)(2,1)S(1)} %planes.1.rest_0_), channel_id=1, source_target_pairs={{0,1},{1,0},{4,5},{5,4},{8,9},{9,8},{12,13},{13,12},{2,3},{3,2},{6... | collective-permute-start | bytes 3145736 | tf_op jit(solution)/shard_map/ppermute | solution.py:316
  38.8 28.1 %collective-permute-start.8 = (bf16[4,2,8,8,1024]{4,3,2,1,0:T(8,128)(2,1)S(1)}, bf16[4,2,8,8,1024]{4,3,2,1,0:T(8,128)(2,1)S(1)}, u32[]{:S(2)}, u32[]{:S(2)}) collective-permute-start(bf16[4,2,8,8,1024]{4,3,2,1,0:T(8,128)(2,1)S(1)} %planes.1.rest_0_), channel_id=1, source_target_pairs={{0,96},{1,13},{4,100},{5,1},{8,104},{9,5},{12,108},{13,9},{2,98},{... | collective-permute-start | bytes 3145736 | tf_op jit(solution)/shard_map/ppermute | solution.py:316
  40.9 26.0 %collective-permute-start.7 = (bf16[4,2,8,8,1024]{4,3,2,1,0:T(8,128)(2,1)S(1)}, bf16[4,2,8,8,1024]{4,3,2,1,0:T(8,128)(2,1)S(1)}, u32[]{:S(2)}, u32[]{:S(2)}) collective-permute-start(bf16[4,2,8,8,1024]{4,3,2,1,0:T(8,128)(2,1)S(1)} %planes.1.rest_0_), channel_id=1, source_target_pairs={{0,64},{1,9},{4,68},{5,13},{8,72},{9,1},{12,76},{13,5},{2,66},{3,1... | collective-permute-start | bytes 3145736 | tf_op jit(solution)/shard_map/ppermute | solution.py:316
  40.9 26.1 %collective-permute-start.6 = (bf16[4,2,8,8,1024]{4,3,2,1,0:T(8,128)(2,1)S(1)}, bf16[4,2,8,8,1024]{4,3,2,1,0:T(8,128)(2,1)S(1)}, u32[]{:S(2)}, u32[]{:S(2)}) collective-permute-start(bf16[4,2,8,8,1024]{4,3,2,1,0:T(8,128)(2,1)S(1)} %planes.1.rest_0_), channel_id=1, source_target_pairs={{0,32},{1,5},{4,36},{5,9},{8,40},{9,13},{12,44},{13,1},{2,34},{3,7... | collective-permute-start | bytes 3145736 | tf_op jit(solution)/shard_map/ppermute | solution.py:316
  41.5 0.9 %copy-start.2 = (bf16[4,8,16,128]{3,2,1,0:T(8,128)(2,1)S(1)}, bf16[4,8,16,128]{3,2,1,0:T(8,128)(2,1)}, u32[]{:S(2)}) copy-start(bf16[4,8,16,128]{3,2,1,0:T(8,128)(2,1)} %volume_ref) | copy-start | bytes 393220
  42.4 36.9 %copy-start.1 = (bf16[1024,512]{1,0:T(8,128)(2,1)S(1)}, bf16[1024,512]{1,0:T(8,128)(2,1)}, u32[]{:S(2)}) copy-start(bf16[1024,512]{1,0:T(8,128)(2,1)} %projector_ref.1) | copy-start | bytes 3145732
  67.0 12.3 %collective-permute-start.13 = (bf16[4,2,8,8,1024]{4,3,2,1,0:T(8,128)(2,1)S(1)}, bf16[4,2,8,8,1024]{4,3,2,1,0:T(8,128)(2,1)S(1)}, u32[]{:S(2)}, u32[]{:S(2)}) collective-permute-start(bf16[4,2,8,8,1024]{4,3,2,1,0:T(8,128)(2,1)S(1)} %collective-permute-done.6.rest_1_), channel_id=1, source_target_pairs={{0,1},{1,0},{4,5},{5,4},{8,9},{9,8},{12,13},{13,12},{2,3},{3,2},{6... | collective-permute-start | bytes 3145736 | tf_op jit(solution)/shard_map/ppermute | solution.py:316
  68.9 10.4 %collective-permute-start.14 = (bf16[4,2,8,8,1024]{4,3,2,1,0:T(8,128)(2,1)S(1)}, bf16[4,2,8,8,1024]{4,3,2,1,0:T(8,128)(2,1)S(1)}, u32[]{:S(2)}, u32[]{:S(2)}) collective-permute-start(bf16[4,2,8,8,1024]{4,3,2,1,0:T(8,128)(2,1)S(1)} %collective-permute-done.7.rest_2_), channel_id=1, source_target_pairs={{0,1},{1,0},{4,5},{5,4},{8,9},{9,8},{12,13},{13,12},{2,3},{3,2},{6... | collective-permute-start | bytes 3145736 | tf_op jit(solution)/shard_map/ppermute | solution.py:316
  69.0 10.3 %collective-permute-start.15 = (bf16[4,2,8,8,1024]{4,3,2,1,0:T(8,128)(2,1)S(1)}, bf16[4,2,8,8,1024]{4,3,2,1,0:T(8,128)(2,1)S(1)}, u32[]{:S(2)}, u32[]{:S(2)}) collective-permute-start(bf16[4,2,8,8,1024]{4,3,2,1,0:T(8,128)(2,1)S(1)} %collective-permute-done.8.rest_3_), channel_id=1, source_target_pairs={{0,1},{1,0},{4,5},{5,4},{8,9},{9,8},{12,13},{13,12},{2,3},{3,2},{6... | collective-permute-start | bytes 3145736 | tf_op jit(solution)/shard_map/ppermute | solution.py:316
  69.4 7.9 %collective-permute-start.11 = (bf16[128,1024]{1,0:T(8,128)(2,1)S(1)}, bf16[128,1024]{1,0:T(8,128)(2,1)S(1)}, u32[]{:S(2)}, u32[]{:S(2)}) collective-permute-start(bf16[128,1024]{1,0:T(8,128)(2,1)S(1)} %get-tuple-element.26.n0_ref), channel_id=1, source_target_pairs={{0,2},{2,0},{1,3},{3,1},{4,6},{6,4},{5,7},{7,5},{8,10},{10,8},{9,1... | collective-permute-start | bytes 786440 | tf_op jit(solution)/shard_map/ppermute | solution.py:437
  69.4 8.7 %collective-permute-start.10 = (bf16[128,1024]{1,0:T(8,128)(2,1)S(1)}, bf16[128,1024]{1,0:T(8,128)(2,1)S(1)}, u32[]{:S(2)}, u32[]{:S(2)}) collective-permute-start(bf16[128,1024]{1,0:T(8,128)(2,1)S(1)} %get-tuple-element.26.n0_ref), channel_id=1, source_target_pairs={{0,1},{1,0},{2,3},{3,2},{4,5},{5,4},{6,7},{7,6},{8,9},{9,8},{10,11... | collective-permute-start | bytes 786440 | tf_op jit(solution)/shard_map/ppermute | solution.py:438
  77.2 2.0 %collective-permute-start.12 = (bf16[128,1024]{1,0:T(8,128)(2,1)S(1)}, bf16[128,1024]{1,0:T(8,128)(2,1)S(1)}, u32[]{:S(2)}, u32[]{:S(2)}) collective-permute-start(bf16[128,1024]{1,0:T(8,128)(2,1)S(1)} %collective-permute-done.11.n2_ref), channel_id=1, source_target_pairs={{0,1},{1,0},{2,3},{3,2},{4,5},{5,4},{6,7},{7,6},{8,9},{9,8},{10,11... | collective-permute-start | bytes 786440 | tf_op jit(solution)/shard_map/ppermute | solution.py:439

commit v4 on v3

--- a/solution.py
+++ b/solution.py
@@ -159,13 +159,11 @@
         for tap in range(9):
             w1[tap, before, :] = jnp.zeros((16, 256), BF16)
             w1[tap, now, :] = g_ref[tap]
-        acc = jnp.zeros((XM * 80, 256), F32)
-        for tap in range(9):
-            acc = acc + jnp.dot(
-                taps[:, :, BLK * tap : BLK * (tap + 1)].reshape(XM * 80, BLK),
-                w1[tap, 16:144, :],
-                preferred_element_type=F32,
-            )
+        acc = jnp.dot(
+            taps[...].reshape(XM * 80, 9 * BLK),
+            jnp.concatenate([w1[tap, 16:144, :] for tap in range(9)], axis=0),
+            preferred_element_type=F32,
+        )
         out = jnp.where(inside, silu(acc).reshape(XM, 80, 256), 0.0)
         lanes = pl.ds(pl.multiple_of(256 * n + BLK, BLK), 256)
         maps_even[:, :, lanes] = out.astype(BF16)
@@ -193,12 +191,6 @@
     wide = tokens.astype(F32)
     scale = lax.rsqrt(jnp.mean(wide * wide, axis=-1, keepdims=True) + 1e-05)
     normed_ref[...] = (wide * scale).astype(BF16)
-
-
-def pair_kernel(at_ref, own_ref, other_ref, pair_ref):
-    high = at_ref[1]
-    pair_ref[pl.ds(high, 1)] = own_ref[...][None]
-    pair_ref[pl.ds(1 - high, 1)] = other_ref[...][None]
 
 
 def plane_kernel(at_ref, own_ref, one_ref, three_ref, two_ref, plane_ref):
@@ -343,13 +335,10 @@
     )
     shard = lax.dynamic_index_in_dim(shard, core, axis=0, keepdims=False)
     other = send(shard, lambda x, y, z, c: (x, 3 - y, z, c))
-    pair = pl.pallas_call(
-        pair_kernel,
-        out_shape=jax.ShapeDtypeStruct((2, 8, 8, D), BF16),
-        in_specs=[smem(), vmem(), vmem()],
-        out_specs=vmem(),
-        name="pairs",
-    )(at, shard, other)
+    high = at[1] == 0
+    pair = jnp.stack(
+        [jnp.where(high, shard, other), jnp.where(high, other, shard)], axis=0
+    )
     line = lambda part, k: send(
         part, lambda x, y, z, c: (x + k * c, y, z + k * (1 - c), c)
     )

time: 90.1 us -> 83.9 us (0.931)
  Pallas kernels: 38.8 us -> 33.9 us
  waiting for transfers between devices: 10.3 us -> 12.6 us
  local copies, waits for them, and re-layouts: 8.17 us -> 5.98 us
  starting transfers between devices: 27.4 us -> 26.4 us
    pallas_call x1, Pallas kernels: 24.5 us -> 21.3 us  [local(): pl.pallas_call(encode_kernel, out_shape=(jax.ShapeDtypeStruct((128, D), B...]
    ppermute x11, waiting for transfers between devices: 1.47 us -> 4.36 us  [send(): return lax.ppermute(array, ('tile', 'tm'), pairs)]
    unnamed x12 -> x4, local copies, waits for them, and re-layouts: 3.1 us -> 0.91 us
    pallas_call x1 -> x0, Pallas kernels: 1.69 us -> none  [local(): pl.pallas_call(pair_kernel, out_shape=jax.ShapeDtypeStruct((2, 8, 8, D),...]
    ppermute x11, starting transfers between devices: 20 us -> 18.5 us  [send(): return lax.ppermute(array, ('tile', 'tm'), pairs)]
  transfers between devices with their start and end apart: 16 -> 16, of which waited for: 5 -> 6; matrix products, arithmetic and copies ran while one was open for 9% -> 9% of each run, Pallas kernels for 32% -> 29%
where the time goes in v4:
time: 83.9 us; the launch traced here: 83.5 us
  Pallas kernels  33.9 us (40%)
  starting transfers between devices  26.4 us (31%)
  waiting for transfers between devices  12.6 us (15%)
  local copies, waits for them, and re-layouts  5.98 us (7%)
  other arithmetic  3.8 us (5%)
  between operations  0.84 us (1%)
    pallas_call x1, Pallas kernels, local(): pl.pallas_call(encode_kernel, out_shape=(jax.ShapeDtypeStruct((128, D), B...  21.3 us
    ppermute x11, starting transfers between devices, send(): return lax.ppermute(array, ('tile', 'tm'), pairs)  18.5 us
    pallas_call x1, Pallas kernels, local(): pl.pallas_call(attend_kernel, out_shape=jax.ShapeDtypeStruct((128, 512),...  9.64 us
    ppermute x1, waiting for transfers between devices, local(): by_chip = lax.ppermute(normed, 'tm', [(0, 2), (2, 0), (1, 3), (3, 1)])  7.06 us
    ppermute x1, starting transfers between devices, local(): left = lax.ppermute(volume[:, 6:8], 'tile', up)  5 us
    ppermute x11, waiting for transfers between devices, send(): return lax.ppermute(array, ('tile', 'tm'), pairs)  4.36 us
    pallas_call x1, Pallas kernels, local(): pl.pallas_call(weights_kernel, out_shape=(jax.ShapeDtypeStruct((9, 48, 25...  2.32 us
  transfers between devices with their start and end apart: 16, of which 6 were waited for; matrix products, arithmetic and copies ran while one was open for 9% of the time, Pallas kernels for 29%

profile of v4, /device:TPU:1, one launch (start us, length us, event | category | flops | bytes accessed | tf_op | source)
XLA Modules:
  0.0 83.5 jit_solution(12411012589662658520)
XLA Ops:
  0.0 0.8 fusion.10
  0.8 1.3 %collective-permute-start.1 = (bf16[4,2,16,128]{3,2,1,0:T(8,128)(2,1)S(1)}, bf16[4,2,16,128]{3,2,1,0:T(8,128)(2,1)S(1)}, u32[]{:S(2)}, u32[]{:S(2)}) collective-permute-start(bf16[4,2,16,128]{3,2,1,0:T(8,128)(2,1)S(1)} %get-tuple-element.33), channel_id=1, source_target_pairs={{4,0},{8,4},{12,8},{16,12},{20,16},{24,20},{28,24},{32,28},{36,32}... | collective-permute-start | bytes 98312 | tf_op jit(solution)/shard_map/ppermute | solution.py:328
  2.1 5.0 %collective-permute-start = (bf16[4,2,16,128]{3,2,1,0:T(8,128)(2,1)S(1)}, bf16[4,2,16,128]{3,2,1,0:T(8,128)(2,1)S(1)}, u32[]{:S(2)}, u32[]{:S(2)}) collective-permute-start(bf16[4,2,16,128]{3,2,1,0:T(8,128)(2,1)S(1)} %get-tuple-element.34), channel_id=1, source_target_pairs={{0,4},{4,8},{8,12},{12,16},{16,20},{20,24},{24,28},{28,32},{32,36}... | collective-permute-start | bytes 98312 | tf_op jit(solution)/shard_map/ppermute | solution.py:327
  7.1 0.9 %fusion.1 = bf16[8,8,1024]{2,1,0:T(8,128)(2,1)S(1)} fusion(s32[]{:T(128)S(6)} %select_n.64, bf16[2,6,8,1024]{3,2,1,0:T(8,128)(2,1)} %bitcast.31, bf16[2,2,8,1024]{3,2,1,0:T(8,128)(2,1)} %bitcast.33), kind=kLoop, calls=%fused_computation.4 | loop fusion | flops 65536 | bytes 393220 | tf_op jit(solution)/shard_map/jit(dynamic_index_in_dim)/squeeze | solution.py:336
  8.0 5.6 %collective-permute-start.2 = (bf16[8,8,1024]{2,1,0:T(8,128)(2,1)S(1)}, bf16[8,8,1024]{2,1,0:T(8,128)(2,1)S(1)}, u32[]{:S(2)}, u32[]{:S(2)}) collective-permute-start(bf16[8,8,1024]{2,1,0:T(8,128)(2,1)S(1)} %fusion.1), channel_id=1, source_target_pairs={{0,18},{1,19},{4,22},{5,23},{8,26},{9,27},{12,30},{13,31},{2,16},{... | collective-permute-start | bytes 393224 | tf_op jit(solution)/shard_map/ppermute | solution.py:308
  13.6 0.7 convert_element_type.29
  14.3 0.1 broadcast_in_dim.7
  14.4 0.1 mul.82
  14.4 1.4 %fusion.11 = (s32[1]{0:T(128)}, s32[1]{0:T(128)}, s32[1]{0:T(128)}) fusion(s32[3]{0:T(128)} %param.11), kind=kLoop, calls=%fused_computation.28 | loop fusion | bytes 24 | tf_op jit(solution)/shard_map/slice | solution.py:366
  16.5 0.7 fusion.9
  17.2 0.1 fusion.3
  17.2 0.3 sine_add_fusion
  17.6 0.7 add_convert_fusion
  18.3 2.8 %collective-permute-start.5 = (bf16[2,8,8,1024]{3,2,1,0:T(8,128)(2,1)S(1)}, bf16[2,8,8,1024]{3,2,1,0:T(8,128)(2,1)S(1)}, u32[]{:S(2)}, u32[]{:S(2)}) collective-permute-start(bf16[2,8,8,1024]{3,2,1,0:T(8,128)(2,1)S(1)} %pad_maximum_fusion.own_ref), channel_id=1, source_target_pairs={{0,8},{1,65},{4,12},{5,69},{8,0},{9,73},{12,4},{13,77},{2,10},{3,6... | collective-permute-start | bytes 786440 | tf_op jit(solution)/shard_map/ppermute | solution.py:308
  21.1 0.9 %collective-permute-start.4 = (bf16[2,8,8,1024]{3,2,1,0:T(8,128)(2,1)S(1)}, bf16[2,8,8,1024]{3,2,1,0:T(8,128)(2,1)S(1)}, u32[]{:S(2)}, u32[]{:S(2)}) collective-permute-start(bf16[2,8,8,1024]{3,2,1,0:T(8,128)(2,1)S(1)} %pad_maximum_fusion.own_ref), channel_id=1, source_target_pairs={{0,12},{1,97},{4,0},{5,101},{8,4},{9,105},{12,8},{13,109},{2,14},{... | collective-permute-start | bytes 786440 | tf_op jit(solution)/shard_map/ppermute | solution.py:308
  22.0 0.6 collective-permute-start.3
  22.6 0.3 add_sine_fusion.along_y_ref
  22.9 0.1 pad_add_fusion.1.place_ref
  23.0 0.1 pad_add_fusion.at_ref
  23.1 0.8 reshape.59
  23.9 1.0 %copy.15 = bf16[3,3,16,3,16]{4,3,2,1,0:T(4,128)(2,1)S(1)} copy(bf16[3,3,16,3,16]{2,4,3,1,0:T(8,128)(2,1)} %bitcast.32) | data formatting | bytes 27648 | tf_op jit(solution)/shard_map/reshape | solution.py:373
  24.9 0.1 reshape.63.second_ref
  25.1 2.3 %conv_weights.1 = (bf16[9,48,256]{2,1,0:T(8,128)(2,1)S(1)}, bf16[9,512,256]{2,1,0:T(8,128)(2,1)S(1)}) custom-call(bf16[16,48]{1,0:T(8,128)(2,1)S(1)} %pad.4.first_ref, bf16[144,48]{1,0:T(8,128)(2,1)S(1)} %reshape.63.second_ref), custom_call_target="tpu_custom_call" | custom-call | tf_op jit(solution)/shard_map/conv_weights/pallas_call | solution.py:374
  27.4 0.7 collective-permute-done.4.three_ref
  28.1 0.4 collective-permute-done.3.one_ref
  28.4 0.6 planes.1.rest_0_
  29.1 0.0 collective-permute-done.1.right_ref
  29.1 5.2 %collective-permute-start.9 = (bf16[4,2,8,8,1024]{4,3,2,1,0:T(8,128)(2,1)S(1)}, bf16[4,2,8,8,1024]{4,3,2,1,0:T(8,128)(2,1)S(1)}, u32[]{:S(2)}, u32[]{:S(2)}) collective-permute-start(bf16[4,2,8,8,1024]{4,3,2,1,0:T(8,128)(2,1)S(1)} %planes.1.rest_0_), channel_id=1, source_target_pairs={{0,1},{1,0},{4,5},{5,4},{8,9},{9,8},{12,13},{13,12},{2,3},{3,2},{6... | collective-permute-start | bytes 3145736 | tf_op jit(solution)/shard_map/ppermute | solution.py:308
  34.3 2.1 %collective-permute-start.8 = (bf16[4,2,8,8,1024]{4,3,2,1,0:T(8,128)(2,1)S(1)}, bf16[4,2,8,8,1024]{4,3,2,1,0:T(8,128)(2,1)S(1)}, u32[]{:S(2)}, u32[]{:S(2)}) collective-permute-start(bf16[4,2,8,8,1024]{4,3,2,1,0:T(8,128)(2,1)S(1)} %planes.1.rest_0_), channel_id=1, source_target_pairs={{0,96},{1,13},{4,100},{5,1},{8,104},{9,5},{12,108},{13,9},{2,98},{... | collective-permute-start | bytes 3145736 | tf_op jit(solution)/shard_map/ppermute | solution.py:308
  36.4 0.0 collective-permute-start.7
  36.4 0.6 collective-permute-start.6
  37.0 0.9 %copy-done.1 = bf16[4,8,16,128]{3,2,1,0:T(8,128)(2,1)S(1)} copy-done((bf16[4,8,16,128]{3,2,1,0:T(8,128)(2,1)S(1)}, bf16[4,8,16,128]{3,2,1,0:T(8,128)(2,1)}, u32[]{:S(2)}) %copy-start.1) | copy-done | bytes 131096
  37.9 21.3 %encode.1 = (bf16[128,1024]{1,0:T(8,128)(2,1)S(1)}, bf16[128,1024]{1,0:T(8,128)(2,1)S(1)}) custom-call(s32[2]{0:T(128)S(1)} %pad_add_fusion.1.place_ref, bf16[4,8,16,128]{3,2,1,0:T(8,128)(2,1)S(1)} %copy-done.1, bf16[4,2,16,128]{3,2,1,0:T(8,128)(2,1)S(1)} %collective-permute-done.left_ref, bf16[4,2,16,128]{3,2,1,0:T(8,128)(2,1)S(1)} %collective-permute-done.1.right_ref, ...), custom_call_target="tpu_custom_call" | custom-call | flops 15000000512 | bytes 20000000 | tf_op jit(solution)/shard_map/encode/pallas_call | solution.py:386
  59.2 0.2 collective-permute-done.8.rest_3_
  59.4 3.1 %collective-permute-done.6.rest_1_ = bf16[4,2,8,8,1024]{4,3,2,1,0:T(8,128)(2,1)S(1)} collective-permute-done((bf16[4,2,8,8,1024]{4,3,2,1,0:T(8,128)(2,1)S(1)}, bf16[4,2,8,8,1024]{4,3,2,1,0:T(8,128)(2,1)S(1)}, u32[]{:S(2)}, u32[]{:S(2)}) %collective-permute-start.6) | collective-permute-done | bytes 1048608 | tf_op jit(solution)/shard_map/ppermute | solution.py:308
  62.5 0.2 collective-permute-start.13
  62.7 0.3 collective-permute-start.14
  63.0 0.2 collective-permute-start.15
  63.2 0.1 collective-permute-start.11
  63.3 0.4 collective-permute-start.10
  63.7 7.1 %collective-permute-done.11.n2_ref = bf16[128,1024]{1,0:T(8,128)(2,1)S(1)} collective-permute-done((bf16[128,1024]{1,0:T(8,128)(2,1)S(1)}, bf16[128,1024]{1,0:T(8,128)(2,1)S(1)}, u32[]{:S(2)}, u32[]{:S(2)}) %collective-permute-start.11) | collective-permute-done | bytes 262176 | tf_op jit(solution)/shard_map/ppermute | solution.py:426
  70.8 1.1 %collective-permute-start.12 = (bf16[128,1024]{1,0:T(8,128)(2,1)S(1)}, bf16[128,1024]{1,0:T(8,128)(2,1)S(1)}, u32[]{:S(2)}, u32[]{:S(2)}) collective-permute-start(bf16[128,1024]{1,0:T(8,128)(2,1)S(1)} %collective-permute-done.11.n2_ref), channel_id=1, source_target_pairs={{0,1},{1,0},{2,3},{3,2},{4,5},{5,4},{6,7},{7,6},{8,9},{9,8},{10,11... | collective-permute-start | bytes 786440 | tf_op jit(solution)/shard_map/ppermute | solution.py:428
  71.9 1.2 %collective-permute-done.12.n3_ref = bf16[128,1024]{1,0:T(8,128)(2,1)S(1)} collective-permute-done((bf16[128,1024]{1,0:T(8,128)(2,1)S(1)}, bf16[128,1024]{1,0:T(8,128)(2,1)S(1)}, u32[]{:S(2)}, u32[]{:S(2)}) %collective-permute-start.12) | collective-permute-done | bytes 262176 | tf_op jit(solution)/shard_map/ppermute | solution.py:428
  73.1 0.0 collective-permute-done.13.rest_5_
  73.1 0.0 collective-permute-done.14.rest_6_
  73.1 9.6 %attend.1 = bf16[128,512]{1,0:T(8,128)(2,1)S(1)} custom-call(s32[1]{0:T(128)} %bitcast.place_ref, s32[4]{0:T(128)S(1)} %pad_add_fusion.at_ref, bf16[128,1024]{1,0:T(8,128)(2,1)S(1)} %get-tuple-element.23.tokens_ref, bf16[128,1024]{1,0:T(8,128)(2,1)S(1)} %get-tuple-element.26.n0_ref, bf16[128,1024]{1,0:T(8,128)(2,1)S(1)} %collective-permute-done.10.n1_ref, ...), custom_call_target="tpu_custom_call" | custom-call | tf_op jit(solution)/shard_map/attend/pallas_call | solution.py:430
  82.8 0.1 reshape.62
  82.8 0.7 copy.18
  (14 shorter events, 0.1 us)
Async XLA Ops:
  0.8 28.3 %collective-permute-start.1 = (bf16[4,2,16,128]{3,2,1,0:T(8,128)(2,1)S(1)}, bf16[4,2,16,128]{3,2,1,0:T(8,128)(2,1)S(1)}, u32[]{:S(2)}, u32[]{:S(2)}) collective-permute-start(bf16[4,2,16,128]{3,2,1,0:T(8,128)(2,1)S(1)} %get-tuple-element.33), channel_id=1, source_target_pairs={{4,0},{8,4},{12,8},{16,12},{20,16},{24,20},{28,24},{32,28},{36,32}... | collective-permute-start | bytes 98312 | tf_op jit(solution)/shard_map/ppermute | solution.py:328
  2.1 27.0 %collective-permute-start = (bf16[4,2,16,128]{3,2,1,0:T(8,128)(2,1)S(1)}, bf16[4,2,16,128]{3,2,1,0:T(8,128)(2,1)S(1)}, u32[]{:S(2)}, u32[]{:S(2)}) collective-permute-start(bf16[4,2,16,128]{3,2,1,0:T(8,128)(2,1)S(1)} %get-tuple-element.34), channel_id=1, source_target_pairs={{0,4},{4,8},{8,12},{12,16},{16,20},{20,24},{24,28},{28,32},{32,36}... | collective-permute-start | bytes 98312 | tf_op jit(solution)/shard_map/ppermute | solution.py:327
  8.0 10.2 %collective-permute-start.2 = (bf16[8,8,1024]{2,1,0:T(8,128)(2,1)S(1)}, bf16[8,8,1024]{2,1,0:T(8,128)(2,1)S(1)}, u32[]{:S(2)}, u32[]{:S(2)}) collective-permute-start(bf16[8,8,1024]{2,1,0:T(8,128)(2,1)S(1)} %fusion.1), channel_id=1, source_target_pairs={{0,18},{1,19},{4,22},{5,23},{8,26},{9,27},{12,30},{13,31},{2,16},{... | collective-permute-start | bytes 393224 | tf_op jit(solution)/shard_map/ppermute | solution.py:308
  18.3 9.1 %collective-permute-start.5 = (bf16[2,8,8,1024]{3,2,1,0:T(8,128)(2,1)S(1)}, bf16[2,8,8,1024]{3,2,1,0:T(8,128)(2,1)S(1)}, u32[]{:S(2)}, u32[]{:S(2)}) collective-permute-start(bf16[2,8,8,1024]{3,2,1,0:T(8,128)(2,1)S(1)} %pad_maximum_fusion.own_ref), channel_id=1, source_target_pairs={{0,8},{1,65},{4,12},{5,69},{8,0},{9,73},{12,4},{13,77},{2,10},{3,6... | collective-permute-start | bytes 786440 | tf_op jit(solution)/shard_map/ppermute | solution.py:308
  21.1 6.9 %collective-permute-start.4 = (bf16[2,8,8,1024]{3,2,1,0:T(8,128)(2,1)S(1)}, bf16[2,8,8,1024]{3,2,1,0:T(8,128)(2,1)S(1)}, u32[]{:S(2)}, u32[]{:S(2)}) collective-permute-start(bf16[2,8,8,1024]{3,2,1,0:T(8,128)(2,1)S(1)} %pad_maximum_fusion.own_ref), channel_id=1, source_target_pairs={{0,12},{1,97},{4,0},{5,101},{8,4},{9,105},{12,8},{13,109},{2,14},{... | collective-permute-start | bytes 786440 | tf_op jit(solution)/shard_map/ppermute | solution.py:308
  22.0 6.4 %collective-permute-start.3 = (bf16[2,8,8,1024]{3,2,1,0:T(8,128)(2,1)S(1)}, bf16[2,8,8,1024]{3,2,1,0:T(8,128)(2,1)S(1)}, u32[]{:S(2)}, u32[]{:S(2)}) collective-permute-start(bf16[2,8,8,1024]{3,2,1,0:T(8,128)(2,1)S(1)} %pad_maximum_fusion.own_ref), channel_id=1, source_target_pairs={{0,4},{1,33},{4,8},{5,37},{8,12},{9,41},{12,0},{13,45},{2,6},{3,35... | collective-permute-start | bytes 786440 | tf_op jit(solution)/shard_map/ppermute | solution.py:308
  29.1 30.1 %collective-permute-start.9 = (bf16[4,2,8,8,1024]{4,3,2,1,0:T(8,128)(2,1)S(1)}, bf16[4,2,8,8,1024]{4,3,2,1,0:T(8,128)(2,1)S(1)}, u32[]{:S(2)}, u32[]{:S(2)}) collective-permute-start(bf16[4,2,8,8,1024]{4,3,2,1,0:T(8,128)(2,1)S(1)} %planes.1.rest_0_), channel_id=1, source_target_pairs={{0,1},{1,0},{4,5},{5,4},{8,9},{9,8},{12,13},{13,12},{2,3},{3,2},{6... | collective-permute-start | bytes 3145736 | tf_op jit(solution)/shard_map/ppermute | solution.py:308
  34.3 25.1 %collective-permute-start.8 = (bf16[4,2,8,8,1024]{4,3,2,1,0:T(8,128)(2,1)S(1)}, bf16[4,2,8,8,1024]{4,3,2,1,0:T(8,128)(2,1)S(1)}, u32[]{:S(2)}, u32[]{:S(2)}) collective-permute-start(bf16[4,2,8,8,1024]{4,3,2,1,0:T(8,128)(2,1)S(1)} %planes.1.rest_0_), channel_id=1, source_target_pairs={{0,96},{1,13},{4,100},{5,1},{8,104},{9,5},{12,108},{13,9},{2,98},{... | collective-permute-start | bytes 3145736 | tf_op jit(solution)/shard_map/ppermute | solution.py:308
  36.4 23.0 %collective-permute-start.7 = (bf16[4,2,8,8,1024]{4,3,2,1,0:T(8,128)(2,1)S(1)}, bf16[4,2,8,8,1024]{4,3,2,1,0:T(8,128)(2,1)S(1)}, u32[]{:S(2)}, u32[]{:S(2)}) collective-permute-start(bf16[4,2,8,8,1024]{4,3,2,1,0:T(8,128)(2,1)S(1)} %planes.1.rest_0_), channel_id=1, source_target_pairs={{0,64},{1,9},{4,68},{5,13},{8,72},{9,1},{12,76},{13,5},{2,66},{3,1... | collective-permute-start | bytes 3145736 | tf_op jit(solution)/shard_map/ppermute | solution.py:308
  36.4 26.1 %collective-permute-start.6 = (bf16[4,2,8,8,1024]{4,3,2,1,0:T(8,128)(2,1)S(1)}, bf16[4,2,8,8,1024]{4,3,2,1,0:T(8,128)(2,1)S(1)}, u32[]{:S(2)}, u32[]{:S(2)}) collective-permute-start(bf16[4,2,8,8,1024]{4,3,2,1,0:T(8,128)(2,1)S(1)} %planes.1.rest_0_), channel_id=1, source_target_pairs={{0,32},{1,5},{4,36},{5,9},{8,40},{9,13},{12,44},{13,1},{2,34},{3,7... | collective-permute-start | bytes 3145736 | tf_op jit(solution)/shard_map/ppermute | solution.py:308
  37.0 0.9 %copy-start.1 = (bf16[4,8,16,128]{3,2,1,0:T(8,128)(2,1)S(1)}, bf16[4,8,16,128]{3,2,1,0:T(8,128)(2,1)}, u32[]{:S(2)}) copy-start(bf16[4,8,16,128]{3,2,1,0:T(8,128)(2,1)} %volume_ref) | copy-start | bytes 393220
  37.9 35.2 %copy-start = (bf16[1024,512]{1,0:T(8,128)(2,1)S(1)}, bf16[1024,512]{1,0:T(8,128)(2,1)}, u32[]{:S(2)}) copy-start(bf16[1024,512]{1,0:T(8,128)(2,1)} %projector_ref.1) | copy-start | bytes 3145732
  62.5 10.6 %collective-permute-start.13 = (bf16[4,2,8,8,1024]{4,3,2,1,0:T(8,128)(2,1)S(1)}, bf16[4,2,8,8,1024]{4,3,2,1,0:T(8,128)(2,1)S(1)}, u32[]{:S(2)}, u32[]{:S(2)}) collective-permute-start(bf16[4,2,8,8,1024]{4,3,2,1,0:T(8,128)(2,1)S(1)} %collective-permute-done.6.rest_1_), channel_id=1, source_target_pairs={{0,1},{1,0},{4,5},{5,4},{8,9},{9,8},{12,13},{13,12},{2,3},{3,2},{6... | collective-permute-start | bytes 3145736 | tf_op jit(solution)/shard_map/ppermute | solution.py:308
  62.7 10.4 %collective-permute-start.14 = (bf16[4,2,8,8,1024]{4,3,2,1,0:T(8,128)(2,1)S(1)}, bf16[4,2,8,8,1024]{4,3,2,1,0:T(8,128)(2,1)S(1)}, u32[]{:S(2)}, u32[]{:S(2)}) collective-permute-start(bf16[4,2,8,8,1024]{4,3,2,1,0:T(8,128)(2,1)S(1)} %collective-permute-done.7.rest_2_), channel_id=1, source_target_pairs={{0,1},{1,0},{4,5},{5,4},{8,9},{9,8},{12,13},{13,12},{2,3},{3,2},{6... | collective-permute-start | bytes 3145736 | tf_op jit(solution)/shard_map/ppermute | solution.py:308
  63.0 10.1 %collective-permute-start.15 = (bf16[4,2,8,8,1024]{4,3,2,1,0:T(8,128)(2,1)S(1)}, bf16[4,2,8,8,1024]{4,3,2,1,0:T(8,128)(2,1)S(1)}, u32[]{:S(2)}, u32[]{:S(2)}) collective-permute-start(bf16[4,2,8,8,1024]{4,3,2,1,0:T(8,128)(2,1)S(1)} %collective-permute-done.8.rest_3_), channel_id=1, source_target_pairs={{0,1},{1,0},{4,5},{5,4},{8,9},{9,8},{12,13},{13,12},{2,3},{3,2},{6... | collective-permute-start | bytes 3145736 | tf_op jit(solution)/shard_map/ppermute | solution.py:308
  63.2 7.6 %collective-permute-start.11 = (bf16[128,1024]{1,0:T(8,128)(2,1)S(1)}, bf16[128,1024]{1,0:T(8,128)(2,1)S(1)}, u32[]{:S(2)}, u32[]{:S(2)}) collective-permute-start(bf16[128,1024]{1,0:T(8,128)(2,1)S(1)} %get-tuple-element.26.n0_ref), channel_id=1, source_target_pairs={{0,2},{2,0},{1,3},{3,1},{4,6},{6,4},{5,7},{7,5},{8,10},{10,8},{9,1... | collective-permute-start | bytes 786440 | tf_op jit(solution)/shard_map/ppermute | solution.py:426
  63.3 8.6 %collective-permute-start.10 = (bf16[128,1024]{1,0:T(8,128)(2,1)S(1)}, bf16[128,1024]{1,0:T(8,128)(2,1)S(1)}, u32[]{:S(2)}, u32[]{:S(2)}) collective-permute-start(bf16[128,1024]{1,0:T(8,128)(2,1)S(1)} %get-tuple-element.26.n0_ref), channel_id=1, source_target_pairs={{0,1},{1,0},{2,3},{3,2},{4,5},{5,4},{6,7},{7,6},{8,9},{9,8},{10,11... | collective-permute-start | bytes 786440 | tf_op jit(solution)/shard_map/ppermute | solution.py:427
  70.8 2.3 %collective-permute-start.12 = (bf16[128,1024]{1,0:T(8,128)(2,1)S(1)}, bf16[128,1024]{1,0:T(8,128)(2,1)S(1)}, u32[]{:S(2)}, u32[]{:S(2)}) collective-permute-start(bf16[128,1024]{1,0:T(8,128)(2,1)S(1)} %collective-permute-done.11.n2_ref), channel_id=1, source_target_pairs={{0,1},{1,0},{2,3},{3,2},{4,5},{5,4},{6,7},{7,6},{8,9},{9,8},{10,11... | collective-permute-start | bytes 786440 | tf_op jit(solution)/shard_map/ppermute | solution.py:428

commit v5 on v4

--- a/solution.py
+++ b/solution.py
@@ -322,11 +322,6 @@
     count = lax.axis_size("tile")
     tile_place = lax.axis_index("tile")
     tm_place = lax.axis_index("tm")
-    up = [(i, i + 1) for i in range(count - 1)]
-    down = [(i + 1, i) for i in range(count - 1)]
-    left = lax.ppermute(volume[:, 6:8], "tile", up)
-    right = lax.ppermute(volume[:, 0:2], "tile", down)
-
     core = tm_place % 2
     at = jnp.stack([tile_place // 8, (tile_place // 4) % 2, tile_place % 4, core])
     at = at.astype(jnp.int32)
@@ -346,6 +341,12 @@
         part, lambda x, y, z, c: (x + k * (1 - c), y, z + k * c, c)
     )
     swap = lambda part: send(part, lambda x, y, z, c: (x, y, z, 1 - c))
+    steps = [line(pair, k) for k in (1, 3, 2)]
+    volume, pair = lax.optimization_barrier((volume, pair))
+    up = [(i, i + 1) for i in range(count - 1)]
+    down = [(i + 1, i) for i in range(count - 1)]
+    left = lax.ppermute(volume[:, 6:8], "tile", up)
+    right = lax.ppermute(volume[:, 0:2], "tile", down)
     plane = pl.pallas_call(
         plane_kernel,
         out_shape=jax.ShapeDtypeStruct((4, 2, 8, 8, D), BF16),
@@ -353,7 +354,7 @@
         out_specs=vmem(),
         name="planes",
         compiler_params=pltpu.CompilerParams(vmem_limit_bytes=8 << 20),
-    )(at, pair, line(pair, 1), line(pair, 3), line(pair, 2))
+    )(at, pair, *steps)
     volume, left, right, plane = lax.optimization_barrier((volume, left, right, plane))
     one, two, three = cross(plane, 1), cross(plane, 2), cross(plane, 3)
     swapped = swap(plane)

time: 83.9 us -> 83.3 us (level)
  waiting for transfers between devices: 12.6 us -> 11.1 us
  starting transfers between devices: 26.4 us -> 27.4 us
    ppermute x1, starting transfers between devices: 0.09 us -> 1.39 us  [local(): by_chip = lax.ppermute(normed, 'tm', [(0, 2), (2, 0), (1, 3), (3, 1)])]
    ppermute x11, starting transfers between devices: 18.5 us -> 19.5 us  [send(): return lax.ppermute(array, ('tile', 'tm'), pairs)]
  transfers between devices with their start and end apart: 16 -> 16, of which waited for: 6 -> 4; matrix products, arithmetic and copies ran while one was open for 9% -> 9% of each run, Pallas kernels for 29% -> 29%
where the time goes in v5:
time: 83.3 us; the launch traced here: 83 us
  Pallas kernels  33.8 us (41%)
  starting transfers between devices  27.4 us (33%)
  waiting for transfers between devices  11.1 us (13%)
  local copies, waits for them, and re-layouts  5.98 us (7%)
  other arithmetic  3.7 us (4%)
  between operations  0.92 us (1%)
    pallas_call x1, Pallas kernels, local(): pl.pallas_call(encode_kernel, out_shape=(jax.ShapeDtypeStruct((128, D), B...  21.3 us
    ppermute x11, starting transfers between devices, send(): return lax.ppermute(array, ('tile', 'tm'), pairs)  19.5 us
    pallas_call x1, Pallas kernels, local(): pl.pallas_call(attend_kernel, out_shape=jax.ShapeDtypeStruct((128, 512),...  9.64 us
    ppermute x1, waiting for transfers between devices, local(): by_chip = lax.ppermute(normed, 'tm', [(0, 2), (2, 0), (1, 3), (3, 1)])  6.27 us
    ppermute x1, starting transfers between devices, local(): left = lax.ppermute(volume[:, 6:8], 'tile', up)  4.17 us
    ppermute x11, waiting for transfers between devices, send(): return lax.ppermute(array, ('tile', 'tm'), pairs)  3.65 us
    pallas_call x1, Pallas kernels, local(): pl.pallas_call(weights_kernel, out_shape=(jax.ShapeDtypeStruct((9, 48, 25...  2.32 us
  transfers between devices with their start and end apart: 16, of which 4 were waited for; matrix products, arithmetic and copies ran while one was open for 9% of the time, Pallas kernels for 29%

profile of v5, /device:TPU:1, one launch (start us, length us, event | category | flops | bytes accessed | tf_op | source)
XLA Modules:
  0.0 83.0 jit_solution(5230482811361710913)
XLA Ops:
  0.0 0.9 %fusion.1 = bf16[8,8,1024]{2,1,0:T(8,128)(2,1)S(1)} fusion(s32[]{:T(128)S(6)} %select_n.64, bf16[2,6,8,1024]{3,2,1,0:T(8,128)(2,1)} %bitcast.31, bf16[2,2,8,1024]{3,2,1,0:T(8,128)(2,1)} %bitcast.33), kind=kLoop, calls=%fused_computation.4 | loop fusion | flops 65536 | bytes 393220 | tf_op jit(solution)/shard_map/jit(dynamic_index_in_dim)/squeeze | solution.py:331
  0.9 3.6 %collective-permute-start = (bf16[8,8,1024]{2,1,0:T(8,128)(2,1)S(1)}, bf16[8,8,1024]{2,1,0:T(8,128)(2,1)S(1)}, u32[]{:S(2)}, u32[]{:S(2)}) collective-permute-start(bf16[8,8,1024]{2,1,0:T(8,128)(2,1)S(1)} %fusion.1), channel_id=1, source_target_pairs={{0,18},{1,19},{4,22},{5,23},{8,26},{9,27},{12,30},{13,31},{2,16},{... | collective-permute-start | bytes 393224 | tf_op jit(solution)/shard_map/ppermute | solution.py:308
  4.6 0.7 convert_element_type.29
  5.2 0.1 broadcast_in_dim.7
  5.3 0.1 mul.82
  5.4 1.4 %fusion.11 = (s32[1]{0:T(128)}, s32[1]{0:T(128)}, s32[1]{0:T(128)}) fusion(s32[3]{0:T(128)} %param.11), kind=kLoop, calls=%fused_computation.28 | loop fusion | bytes 24 | tf_op jit(solution)/shard_map/slice | solution.py:367
  7.5 0.6 add_convert_fusion
  8.1 0.7 fusion.9
  8.8 0.1 fusion.3
  8.8 0.3 sine_add_fusion
  9.1 0.3 add_sine_fusion.along_y_ref
  9.5 0.1 pad_add_fusion.1.place_ref
  9.6 2.8 %collective-permute-start.5 = (bf16[2,8,8,1024]{3,2,1,0:T(8,128)(2,1)S(1)}, bf16[2,8,8,1024]{3,2,1,0:T(8,128)(2,1)S(1)}, u32[]{:S(2)}, u32[]{:S(2)}) collective-permute-start(bf16[2,8,8,1024]{3,2,1,0:T(8,128)(2,1)S(1)} %pad_maximum_fusion.own_ref), channel_id=1, source_target_pairs={{0,8},{1,65},{4,12},{5,69},{8,0},{9,73},{12,4},{13,77},{2,10},{3,6... | collective-permute-start | bytes 786440 | tf_op jit(solution)/shard_map/ppermute | solution.py:308
  12.4 0.9 %collective-permute-start.4 = (bf16[2,8,8,1024]{3,2,1,0:T(8,128)(2,1)S(1)}, bf16[2,8,8,1024]{3,2,1,0:T(8,128)(2,1)S(1)}, u32[]{:S(2)}, u32[]{:S(2)}) collective-permute-start(bf16[2,8,8,1024]{3,2,1,0:T(8,128)(2,1)S(1)} %pad_maximum_fusion.own_ref), channel_id=1, source_target_pairs={{0,12},{1,97},{4,0},{5,101},{8,4},{9,105},{12,8},{13,109},{2,14},{... | collective-permute-start | bytes 786440 | tf_op jit(solution)/shard_map/ppermute | solution.py:308
  13.3 0.6 collective-permute-start.3
  13.9 0.8 fusion.10
  14.7 1.3 %collective-permute-start.2 = (bf16[4,2,16,128]{3,2,1,0:T(8,128)(2,1)S(1)}, bf16[4,2,16,128]{3,2,1,0:T(8,128)(2,1)S(1)}, u32[]{:S(2)}, u32[]{:S(2)}) collective-permute-start(bf16[4,2,16,128]{3,2,1,0:T(8,128)(2,1)S(1)} %get-tuple-element.37), channel_id=1, source_target_pairs={{4,0},{8,4},{12,8},{16,12},{20,16},{24,20},{28,24},{32,28},{36,32}... | collective-permute-start | bytes 98312 | tf_op jit(solution)/shard_map/ppermute | solution.py:349
  16.0 4.2 %collective-permute-start.1 = (bf16[4,2,16,128]{3,2,1,0:T(8,128)(2,1)S(1)}, bf16[4,2,16,128]{3,2,1,0:T(8,128)(2,1)S(1)}, u32[]{:S(2)}, u32[]{:S(2)}) collective-permute-start(bf16[4,2,16,128]{3,2,1,0:T(8,128)(2,1)S(1)} %get-tuple-element.38), channel_id=1, source_target_pairs={{0,4},{4,8},{8,12},{12,16},{16,20},{20,24},{24,28},{28,32},{32,36}... | collective-permute-start | bytes 98312 | tf_op jit(solution)/shard_map/ppermute | solution.py:348
  20.2 0.1 pad_add_fusion.at_ref
  20.2 0.8 reshape.59
  21.0 1.0 %copy.15 = bf16[3,3,16,3,16]{4,3,2,1,0:T(4,128)(2,1)S(1)} copy(bf16[3,3,16,3,16]{2,4,3,1,0:T(8,128)(2,1)} %bitcast.32) | data formatting | bytes 27648 | tf_op jit(solution)/shard_map/reshape | solution.py:374
  22.1 0.1 reshape.63.second_ref
  22.2 2.3 %conv_weights.1 = (bf16[9,48,256]{2,1,0:T(8,128)(2,1)S(1)}, bf16[9,512,256]{2,1,0:T(8,128)(2,1)S(1)}) custom-call(bf16[16,48]{1,0:T(8,128)(2,1)S(1)} %pad.4.first_ref, bf16[144,48]{1,0:T(8,128)(2,1)S(1)} %reshape.63.second_ref), custom_call_target="tpu_custom_call" | custom-call | tf_op jit(solution)/shard_map/conv_weights/pallas_call | solution.py:375
  24.5 0.0 collective-permute-done.5.two_ref
  24.6 0.0 collective-permute-done.3.one_ref
  24.6 0.6 planes.1.rest_0_
  25.2 0.0 collective-permute-done.2.right_ref
  25.2 3.1 %collective-permute-start.9 = (bf16[4,2,8,8,1024]{4,3,2,1,0:T(8,128)(2,1)S(1)}, bf16[4,2,8,8,1024]{4,3,2,1,0:T(8,128)(2,1)S(1)}, u32[]{:S(2)}, u32[]{:S(2)}) collective-permute-start(bf16[4,2,8,8,1024]{4,3,2,1,0:T(8,128)(2,1)S(1)} %planes.1.rest_0_), channel_id=1, source_target_pairs={{0,1},{1,0},{4,5},{5,4},{8,9},{9,8},{12,13},{13,12},{2,3},{3,2},{6... | collective-permute-start | bytes 3145736 | tf_op jit(solution)/shard_map/ppermute | solution.py:308
  28.3 5.3 %collective-permute-start.8 = (bf16[4,2,8,8,1024]{4,3,2,1,0:T(8,128)(2,1)S(1)}, bf16[4,2,8,8,1024]{4,3,2,1,0:T(8,128)(2,1)S(1)}, u32[]{:S(2)}, u32[]{:S(2)}) collective-permute-start(bf16[4,2,8,8,1024]{4,3,2,1,0:T(8,128)(2,1)S(1)} %planes.1.rest_0_), channel_id=1, source_target_pairs={{0,96},{1,13},{4,100},{5,1},{8,104},{9,5},{12,108},{13,9},{2,98},{... | collective-permute-start | bytes 3145736 | tf_op jit(solution)/shard_map/ppermute | solution.py:308
  33.6 0.0 collective-permute-start.7
  33.6 0.6 collective-permute-start.6
  34.2 0.9 %copy-done.1 = bf16[4,8,16,128]{3,2,1,0:T(8,128)(2,1)S(1)} copy-done((bf16[4,8,16,128]{3,2,1,0:T(8,128)(2,1)S(1)}, bf16[4,8,16,128]{3,2,1,0:T(8,128)(2,1)}, u32[]{:S(2)}) %copy-start.1) | copy-done | bytes 131096
  35.1 21.3 %encode.1 = (bf16[128,1024]{1,0:T(8,128)(2,1)S(1)}, bf16[128,1024]{1,0:T(8,128)(2,1)S(1)}) custom-call(s32[2]{0:T(128)S(1)} %pad_add_fusion.1.place_ref, bf16[4,8,16,128]{3,2,1,0:T(8,128)(2,1)S(1)} %copy-done.1, bf16[4,2,16,128]{3,2,1,0:T(8,128)(2,1)S(1)} %collective-permute-done.1.left_ref, bf16[4,2,16,128]{3,2,1,0:T(8,128)(2,1)S(1)} %collective-permute-done.2.right_ref, ...), custom_call_target="tpu_custom_call" | custom-call | flops 15000000512 | bytes 20000000 | tf_op jit(solution)/shard_map/encode/pallas_call | solution.py:387
  56.3 0.0 collective-permute-done.9.rest_4_
  56.3 0.2 collective-permute-done.8.rest_3_
  56.6 3.4 %collective-permute-done.6.rest_1_ = bf16[4,2,8,8,1024]{4,3,2,1,0:T(8,128)(2,1)S(1)} collective-permute-done((bf16[4,2,8,8,1024]{4,3,2,1,0:T(8,128)(2,1)S(1)}, bf16[4,2,8,8,1024]{4,3,2,1,0:T(8,128)(2,1)S(1)}, u32[]{:S(2)}, u32[]{:S(2)}) %collective-permute-start.6) | collective-permute-done | bytes 1048608 | tf_op jit(solution)/shard_map/ppermute | solution.py:308
  60.0 2.2 %collective-permute-start.13 = (bf16[4,2,8,8,1024]{4,3,2,1,0:T(8,128)(2,1)S(1)}, bf16[4,2,8,8,1024]{4,3,2,1,0:T(8,128)(2,1)S(1)}, u32[]{:S(2)}, u32[]{:S(2)}) collective-permute-start(bf16[4,2,8,8,1024]{4,3,2,1,0:T(8,128)(2,1)S(1)} %collective-permute-done.6.rest_1_), channel_id=1, source_target_pairs={{0,1},{1,0},{4,5},{5,4},{8,9},{9,8},{12,13},{13,12},{2,3},{3,2},{6... | collective-permute-start | bytes 3145736 | tf_op jit(solution)/shard_map/ppermute | solution.py:308
  62.1 0.0 collective-permute-start.14
  62.1 0.5 collective-permute-start.15
  62.6 1.4 %collective-permute-start.11 = (bf16[128,1024]{1,0:T(8,128)(2,1)S(1)}, bf16[128,1024]{1,0:T(8,128)(2,1)S(1)}, u32[]{:S(2)}, u32[]{:S(2)}) collective-permute-start(bf16[128,1024]{1,0:T(8,128)(2,1)S(1)} %get-tuple-element.30.n0_ref), channel_id=1, source_target_pairs={{0,2},{2,0},{1,3},{3,1},{4,6},{6,4},{5,7},{7,5},{8,10},{10,8},{9,1... | collective-permute-start | bytes 786440 | tf_op jit(solution)/shard_map/ppermute | solution.py:427
  64.0 0.3 collective-permute-start.10
  64.3 6.3 %collective-permute-done.11.n2_ref = bf16[128,1024]{1,0:T(8,128)(2,1)S(1)} collective-permute-done((bf16[128,1024]{1,0:T(8,128)(2,1)S(1)}, bf16[128,1024]{1,0:T(8,128)(2,1)S(1)}, u32[]{:S(2)}, u32[]{:S(2)}) %collective-permute-start.11) | collective-permute-done | bytes 262176 | tf_op jit(solution)/shard_map/ppermute | solution.py:427
  70.6 0.8 collective-permute-start.12
  71.4 0.0 collective-permute-done.10.n1_ref
  71.4 1.2 %collective-permute-done.12.n3_ref = bf16[128,1024]{1,0:T(8,128)(2,1)S(1)} collective-permute-done((bf16[128,1024]{1,0:T(8,128)(2,1)S(1)}, bf16[128,1024]{1,0:T(8,128)(2,1)S(1)}, u32[]{:S(2)}, u32[]{:S(2)}) %collective-permute-start.12) | collective-permute-done | bytes 262176 | tf_op jit(solution)/shard_map/ppermute | solution.py:429
  72.5 9.6 %attend.1 = bf16[128,512]{1,0:T(8,128)(2,1)S(1)} custom-call(s32[1]{0:T(128)} %bitcast.place_ref, s32[4]{0:T(128)S(1)} %pad_add_fusion.at_ref, bf16[128,1024]{1,0:T(8,128)(2,1)S(1)} %get-tuple-element.27.tokens_ref, bf16[128,1024]{1,0:T(8,128)(2,1)S(1)} %get-tuple-element.30.n0_ref, bf16[128,1024]{1,0:T(8,128)(2,1)S(1)} %collective-permute-done.10.n1_ref, ...), custom_call_target="tpu_custom_call" | custom-call | tf_op jit(solution)/shard_map/attend/pallas_call | solution.py:431
  82.2 0.1 reshape.62
  82.3 0.7 copy.18
  (14 shorter events, 0.1 us)
Async XLA Ops:
  0.9 8.7 %collective-permute-start = (bf16[8,8,1024]{2,1,0:T(8,128)(2,1)S(1)}, bf16[8,8,1024]{2,1,0:T(8,128)(2,1)S(1)}, u32[]{:S(2)}, u32[]{:S(2)}) collective-permute-start(bf16[8,8,1024]{2,1,0:T(8,128)(2,1)S(1)} %fusion.1), channel_id=1, source_target_pairs={{0,18},{1,19},{4,22},{5,23},{8,26},{9,27},{12,30},{13,31},{2,16},{... | collective-permute-start | bytes 393224 | tf_op jit(solution)/shard_map/ppermute | solution.py:308
  9.6 14.9 %collective-permute-start.5 = (bf16[2,8,8,1024]{3,2,1,0:T(8,128)(2,1)S(1)}, bf16[2,8,8,1024]{3,2,1,0:T(8,128)(2,1)S(1)}, u32[]{:S(2)}, u32[]{:S(2)}) collective-permute-start(bf16[2,8,8,1024]{3,2,1,0:T(8,128)(2,1)S(1)} %pad_maximum_fusion.own_ref), channel_id=1, source_target_pairs={{0,8},{1,65},{4,12},{5,69},{8,0},{9,73},{12,4},{13,77},{2,10},{3,6... | collective-permute-start | bytes 786440 | tf_op jit(solution)/shard_map/ppermute | solution.py:308
  12.4 12.1 %collective-permute-start.4 = (bf16[2,8,8,1024]{3,2,1,0:T(8,128)(2,1)S(1)}, bf16[2,8,8,1024]{3,2,1,0:T(8,128)(2,1)S(1)}, u32[]{:S(2)}, u32[]{:S(2)}) collective-permute-start(bf16[2,8,8,1024]{3,2,1,0:T(8,128)(2,1)S(1)} %pad_maximum_fusion.own_ref), channel_id=1, source_target_pairs={{0,12},{1,97},{4,0},{5,101},{8,4},{9,105},{12,8},{13,109},{2,14},{... | collective-permute-start | bytes 786440 | tf_op jit(solution)/shard_map/ppermute | solution.py:308
  13.3 11.2 %collective-permute-start.3 = (bf16[2,8,8,1024]{3,2,1,0:T(8,128)(2,1)S(1)}, bf16[2,8,8,1024]{3,2,1,0:T(8,128)(2,1)S(1)}, u32[]{:S(2)}, u32[]{:S(2)}) collective-permute-start(bf16[2,8,8,1024]{3,2,1,0:T(8,128)(2,1)S(1)} %pad_maximum_fusion.own_ref), channel_id=1, source_target_pairs={{0,4},{1,33},{4,8},{5,37},{8,12},{9,41},{12,0},{13,45},{2,6},{3,35... | collective-permute-start | bytes 786440 | tf_op jit(solution)/shard_map/ppermute | solution.py:308
  14.7 10.5 %collective-permute-start.2 = (bf16[4,2,16,128]{3,2,1,0:T(8,128)(2,1)S(1)}, bf16[4,2,16,128]{3,2,1,0:T(8,128)(2,1)S(1)}, u32[]{:S(2)}, u32[]{:S(2)}) collective-permute-start(bf16[4,2,16,128]{3,2,1,0:T(8,128)(2,1)S(1)} %get-tuple-element.37), channel_id=1, source_target_pairs={{4,0},{8,4},{12,8},{16,12},{20,16},{24,20},{28,24},{32,28},{36,32}... | collective-permute-start | bytes 98312 | tf_op jit(solution)/shard_map/ppermute | solution.py:349
  16.0 9.2 %collective-permute-start.1 = (bf16[4,2,16,128]{3,2,1,0:T(8,128)(2,1)S(1)}, bf16[4,2,16,128]{3,2,1,0:T(8,128)(2,1)S(1)}, u32[]{:S(2)}, u32[]{:S(2)}) collective-permute-start(bf16[4,2,16,128]{3,2,1,0:T(8,128)(2,1)S(1)} %get-tuple-element.38), channel_id=1, source_target_pairs={{0,4},{4,8},{8,12},{12,16},{16,20},{20,24},{24,28},{28,32},{32,36}... | collective-permute-start | bytes 98312 | tf_op jit(solution)/shard_map/ppermute | solution.py:348
  25.2 31.1 %collective-permute-start.9 = (bf16[4,2,8,8,1024]{4,3,2,1,0:T(8,128)(2,1)S(1)}, bf16[4,2,8,8,1024]{4,3,2,1,0:T(8,128)(2,1)S(1)}, u32[]{:S(2)}, u32[]{:S(2)}) collective-permute-start(bf16[4,2,8,8,1024]{4,3,2,1,0:T(8,128)(2,1)S(1)} %planes.1.rest_0_), channel_id=1, source_target_pairs={{0,1},{1,0},{4,5},{5,4},{8,9},{9,8},{12,13},{13,12},{2,3},{3,2},{6... | collective-permute-start | bytes 3145736 | tf_op jit(solution)/shard_map/ppermute | solution.py:308
  28.3 28.2 %collective-permute-start.8 = (bf16[4,2,8,8,1024]{4,3,2,1,0:T(8,128)(2,1)S(1)}, bf16[4,2,8,8,1024]{4,3,2,1,0:T(8,128)(2,1)S(1)}, u32[]{:S(2)}, u32[]{:S(2)}) collective-permute-start(bf16[4,2,8,8,1024]{4,3,2,1,0:T(8,128)(2,1)S(1)} %planes.1.rest_0_), channel_id=1, source_target_pairs={{0,96},{1,13},{4,100},{5,1},{8,104},{9,5},{12,108},{13,9},{2,98},{... | collective-permute-start | bytes 3145736 | tf_op jit(solution)/shard_map/ppermute | solution.py:308
  33.6 23.0 %collective-permute-start.7 = (bf16[4,2,8,8,1024]{4,3,2,1,0:T(8,128)(2,1)S(1)}, bf16[4,2,8,8,1024]{4,3,2,1,0:T(8,128)(2,1)S(1)}, u32[]{:S(2)}, u32[]{:S(2)}) collective-permute-start(bf16[4,2,8,8,1024]{4,3,2,1,0:T(8,128)(2,1)S(1)} %planes.1.rest_0_), channel_id=1, source_target_pairs={{0,64},{1,9},{4,68},{5,13},{8,72},{9,1},{12,76},{13,5},{2,66},{3,1... | collective-permute-start | bytes 3145736 | tf_op jit(solution)/shard_map/ppermute | solution.py:308
  33.6 26.4 %collective-permute-start.6 = (bf16[4,2,8,8,1024]{4,3,2,1,0:T(8,128)(2,1)S(1)}, bf16[4,2,8,8,1024]{4,3,2,1,0:T(8,128)(2,1)S(1)}, u32[]{:S(2)}, u32[]{:S(2)}) collective-permute-start(bf16[4,2,8,8,1024]{4,3,2,1,0:T(8,128)(2,1)S(1)} %planes.1.rest_0_), channel_id=1, source_target_pairs={{0,32},{1,5},{4,36},{5,9},{8,40},{9,13},{12,44},{13,1},{2,34},{3,7... | collective-permute-start | bytes 3145736 | tf_op jit(solution)/shard_map/ppermute | solution.py:308
  34.2 0.9 %copy-start.1 = (bf16[4,8,16,128]{3,2,1,0:T(8,128)(2,1)S(1)}, bf16[4,8,16,128]{3,2,1,0:T(8,128)(2,1)}, u32[]{:S(2)}) copy-start(bf16[4,8,16,128]{3,2,1,0:T(8,128)(2,1)} %volume_ref) | copy-start | bytes 393220
  35.1 37.5 %copy-start = (bf16[1024,512]{1,0:T(8,128)(2,1)S(1)}, bf16[1024,512]{1,0:T(8,128)(2,1)}, u32[]{:S(2)}) copy-start(bf16[1024,512]{1,0:T(8,128)(2,1)} %projector_ref.1) | copy-start | bytes 3145732
  60.0 12.6 %collective-permute-start.13 = (bf16[4,2,8,8,1024]{4,3,2,1,0:T(8,128)(2,1)S(1)}, bf16[4,2,8,8,1024]{4,3,2,1,0:T(8,128)(2,1)S(1)}, u32[]{:S(2)}, u32[]{:S(2)}) collective-permute-start(bf16[4,2,8,8,1024]{4,3,2,1,0:T(8,128)(2,1)S(1)} %collective-permute-done.6.rest_1_), channel_id=1, source_target_pairs={{0,1},{1,0},{4,5},{5,4},{8,9},{9,8},{12,13},{13,12},{2,3},{3,2},{6... | collective-permute-start | bytes 3145736 | tf_op jit(solution)/shard_map/ppermute | solution.py:308
  62.1 10.4 %collective-permute-start.14 = (bf16[4,2,8,8,1024]{4,3,2,1,0:T(8,128)(2,1)S(1)}, bf16[4,2,8,8,1024]{4,3,2,1,0:T(8,128)(2,1)S(1)}, u32[]{:S(2)}, u32[]{:S(2)}) collective-permute-start(bf16[4,2,8,8,1024]{4,3,2,1,0:T(8,128)(2,1)S(1)} %collective-permute-done.7.rest_2_), channel_id=1, source_target_pairs={{0,1},{1,0},{4,5},{5,4},{8,9},{9,8},{12,13},{13,12},{2,3},{3,2},{6... | collective-permute-start | bytes 3145736 | tf_op jit(solution)/shard_map/ppermute | solution.py:308
  62.1 10.4 %collective-permute-start.15 = (bf16[4,2,8,8,1024]{4,3,2,1,0:T(8,128)(2,1)S(1)}, bf16[4,2,8,8,1024]{4,3,2,1,0:T(8,128)(2,1)S(1)}, u32[]{:S(2)}, u32[]{:S(2)}) collective-permute-start(bf16[4,2,8,8,1024]{4,3,2,1,0:T(8,128)(2,1)S(1)} %collective-permute-done.8.rest_3_), channel_id=1, source_target_pairs={{0,1},{1,0},{4,5},{5,4},{8,9},{9,8},{12,13},{13,12},{2,3},{3,2},{6... | collective-permute-start | bytes 3145736 | tf_op jit(solution)/shard_map/ppermute | solution.py:308
  62.6 7.9 %collective-permute-start.11 = (bf16[128,1024]{1,0:T(8,128)(2,1)S(1)}, bf16[128,1024]{1,0:T(8,128)(2,1)S(1)}, u32[]{:S(2)}, u32[]{:S(2)}) collective-permute-start(bf16[128,1024]{1,0:T(8,128)(2,1)S(1)} %get-tuple-element.30.n0_ref), channel_id=1, source_target_pairs={{0,2},{2,0},{1,3},{3,1},{4,6},{6,4},{5,7},{7,5},{8,10},{10,8},{9,1... | collective-permute-start | bytes 786440 | tf_op jit(solution)/shard_map/ppermute | solution.py:427
  64.0 7.3 %collective-permute-start.10 = (bf16[128,1024]{1,0:T(8,128)(2,1)S(1)}, bf16[128,1024]{1,0:T(8,128)(2,1)S(1)}, u32[]{:S(2)}, u32[]{:S(2)}) collective-permute-start(bf16[128,1024]{1,0:T(8,128)(2,1)S(1)} %get-tuple-element.30.n0_ref), channel_id=1, source_target_pairs={{0,1},{1,0},{2,3},{3,2},{4,5},{5,4},{6,7},{7,6},{8,9},{9,8},{10,11... | collective-permute-start | bytes 786440 | tf_op jit(solution)/shard_map/ppermute | solution.py:428
  70.6 1.9 %collective-permute-start.12 = (bf16[128,1024]{1,0:T(8,128)(2,1)S(1)}, bf16[128,1024]{1,0:T(8,128)(2,1)S(1)}, u32[]{:S(2)}, u32[]{:S(2)}) collective-permute-start(bf16[128,1024]{1,0:T(8,128)(2,1)S(1)} %collective-permute-done.11.n2_ref), channel_id=1, source_target_pairs={{0,1},{1,0},{2,3},{3,2},{4,5},{5,4},{6,7},{7,6},{8,9},{9,8},{10,11... | collective-permute-start | bytes 786440 | tf_op jit(solution)/shard_map/ppermute | solution.py:429

commit v6 on v5

--- a/solution.py
+++ b/solution.py
@@ -420,12 +420,12 @@
         along_y,
         patch_weight.reshape(CH, 64, 8, D),
     )
-    normed, one, two, three, swapped = lax.optimization_barrier(
-        (normed, one, two, three, swapped)
-    )
-    parts = [plane, one, two, three, swapped, swap(one), swap(two), swap(three)]
     by_chip = lax.ppermute(normed, "tm", [(0, 2), (2, 0), (1, 3), (3, 1)])
     by_core = lax.ppermute(normed, "tm", [(0, 1), (1, 0), (2, 3), (3, 2)])
+    by_chip, one, two, three, swapped = lax.optimization_barrier(
+        (by_chip, one, two, three, swapped)
+    )
+    parts = [plane, one, two, three, swapped, swap(one), swap(two), swap(three)]
     by_both = lax.ppermute(by_chip, "tm", [(0, 1), (1, 0), (2, 3), (3, 2)])
 
     out = pl.pallas_call(

time: 83.3 us -> 82.1 us (0.986)
  starting transfers between devices: 27.4 us -> 26.3 us
    ppermute x1, waiting for transfers between devices: 0.01 us -> 4.64 us  [local(): by_core = lax.ppermute(normed, 'tm', [(0, 1), (1, 0), (2, 3), (3, 2)])]
    ppermute x11, waiting for transfers between devices: 3.65 us -> 0.03 us  [send(): return lax.ppermute(array, ('tile', 'tm'), pairs)]
    ppermute x1, starting transfers between devices: 1.39 us -> 0.09 us  [local(): by_chip = lax.ppermute(normed, 'tm', [(0, 2), (2, 0), (1, 3), (3, 1)])]
  transfers between devices with their start and end apart: 16 -> 16, of which waited for: 4 -> 3; matrix products, arithmetic and copies ran while one was open for 9% -> 9% of each run, Pallas kernels for 29% -> 30%
where the time goes in v6:
time: 82.1 us; the launch traced here: 81.7 us
  Pallas kernels  33.8 us (41%)
  starting transfers between devices  26.3 us (32%)
  waiting for transfers between devices  11 us (13%)
  local copies, waits for them, and re-layouts  5.98 us (7%)
  other arithmetic  3.7 us (5%)
  between operations  0.93 us (1%)
    pallas_call x1, Pallas kernels, local(): pl.pallas_call(encode_kernel, out_shape=(jax.ShapeDtypeStruct((128, D), B...  21.3 us
    ppermute x11, starting transfers between devices, send(): return lax.ppermute(array, ('tile', 'tm'), pairs)  20.2 us
    pallas_call x1, Pallas kernels, local(): pl.pallas_call(attend_kernel, out_shape=jax.ShapeDtypeStruct((128, 512),...  9.64 us
    ppermute x1, waiting for transfers between devices, local(): by_chip = lax.ppermute(normed, 'tm', [(0, 2), (2, 0), (1, 3), (3, 1)])  5.93 us
    ppermute x1, waiting for transfers between devices, local(): by_core = lax.ppermute(normed, 'tm', [(0, 1), (1, 0), (2, 3), (3, 2)])  4.64 us
    ppermute x1, starting transfers between devices, local(): left = lax.ppermute(volume[:, 6:8], 'tile', up)  4.17 us
    pallas_call x1, Pallas kernels, local(): pl.pallas_call(weights_kernel, out_shape=(jax.ShapeDtypeStruct((9, 48, 25...  2.32 us
  transfers between devices with their start and end apart: 16, of which 3 were waited for; matrix products, arithmetic and copies ran while one was open for 9% of the time, Pallas kernels for 30%

profile of v6, /device:TPU:1, one launch (start us, length us, event | category | flops | bytes accessed | tf_op | source)
XLA Modules:
  0.0 81.7 jit_solution(15296920464679213623)
XLA Ops:
  0.0 0.9 %fusion.1 = bf16[8,8,1024]{2,1,0:T(8,128)(2,1)S(1)} fusion(s32[]{:T(128)S(6)} %select_n.64, bf16[2,6,8,1024]{3,2,1,0:T(8,128)(2,1)} %bitcast.31, bf16[2,2,8,1024]{3,2,1,0:T(8,128)(2,1)} %bitcast.33), kind=kLoop, calls=%fused_computation.4 | loop fusion | flops 65536 | bytes 393220 | tf_op jit(solution)/shard_map/jit(dynamic_index_in_dim)/squeeze | solution.py:331
  0.9 3.6 %collective-permute-start = (bf16[8,8,1024]{2,1,0:T(8,128)(2,1)S(1)}, bf16[8,8,1024]{2,1,0:T(8,128)(2,1)S(1)}, u32[]{:S(2)}, u32[]{:S(2)}) collective-permute-start(bf16[8,8,1024]{2,1,0:T(8,128)(2,1)S(1)} %fusion.1), channel_id=1, source_target_pairs={{0,18},{1,19},{4,22},{5,23},{8,26},{9,27},{12,30},{13,31},{2,16},{... | collective-permute-start | bytes 393224 | tf_op jit(solution)/shard_map/ppermute | solution.py:308
  4.6 0.7 convert_element_type.29
  5.2 0.1 broadcast_in_dim.7
  5.3 0.1 mul.82
  5.4 1.4 %fusion.11 = (s32[1]{0:T(128)}, s32[1]{0:T(128)}, s32[1]{0:T(128)}) fusion(s32[3]{0:T(128)} %param.11), kind=kLoop, calls=%fused_computation.28 | loop fusion | bytes 24 | tf_op jit(solution)/shard_map/slice | solution.py:367
  7.5 0.6 add_convert_fusion
  8.1 0.7 fusion.9
  8.8 0.1 fusion.3
  8.8 0.3 sine_add_fusion
  9.1 0.3 add_sine_fusion.along_y_ref
  9.5 0.1 pad_add_fusion.1.place_ref
  9.6 0.0 collective-permute-done
  9.6 2.8 %collective-permute-start.5 = (bf16[2,8,8,1024]{3,2,1,0:T(8,128)(2,1)S(1)}, bf16[2,8,8,1024]{3,2,1,0:T(8,128)(2,1)S(1)}, u32[]{:S(2)}, u32[]{:S(2)}) collective-permute-start(bf16[2,8,8,1024]{3,2,1,0:T(8,128)(2,1)S(1)} %pad_maximum_fusion.own_ref), channel_id=1, source_target_pairs={{0,8},{1,65},{4,12},{5,69},{8,0},{9,73},{12,4},{13,77},{2,10},{3,6... | collective-permute-start | bytes 786440 | tf_op jit(solution)/shard_map/ppermute | solution.py:308
  12.4 0.9 %collective-permute-start.4 = (bf16[2,8,8,1024]{3,2,1,0:T(8,128)(2,1)S(1)}, bf16[2,8,8,1024]{3,2,1,0:T(8,128)(2,1)S(1)}, u32[]{:S(2)}, u32[]{:S(2)}) collective-permute-start(bf16[2,8,8,1024]{3,2,1,0:T(8,128)(2,1)S(1)} %pad_maximum_fusion.own_ref), channel_id=1, source_target_pairs={{0,12},{1,97},{4,0},{5,101},{8,4},{9,105},{12,8},{13,109},{2,14},{... | collective-permute-start | bytes 786440 | tf_op jit(solution)/shard_map/ppermute | solution.py:308
  13.3 0.6 collective-permute-start.3
  13.9 0.8 fusion.10
  14.7 1.3 %collective-permute-start.2 = (bf16[4,2,16,128]{3,2,1,0:T(8,128)(2,1)S(1)}, bf16[4,2,16,128]{3,2,1,0:T(8,128)(2,1)S(1)}, u32[]{:S(2)}, u32[]{:S(2)}) collective-permute-start(bf16[4,2,16,128]{3,2,1,0:T(8,128)(2,1)S(1)} %get-tuple-element.37), channel_id=1, source_target_pairs={{4,0},{8,4},{12,8},{16,12},{20,16},{24,20},{28,24},{32,28},{36,32}... | collective-permute-start | bytes 98312 | tf_op jit(solution)/shard_map/ppermute | solution.py:349
  16.0 4.2 %collective-permute-start.1 = (bf16[4,2,16,128]{3,2,1,0:T(8,128)(2,1)S(1)}, bf16[4,2,16,128]{3,2,1,0:T(8,128)(2,1)S(1)}, u32[]{:S(2)}, u32[]{:S(2)}) collective-permute-start(bf16[4,2,16,128]{3,2,1,0:T(8,128)(2,1)S(1)} %get-tuple-element.38), channel_id=1, source_target_pairs={{0,4},{4,8},{8,12},{12,16},{16,20},{20,24},{24,28},{28,32},{32,36}... | collective-permute-start | bytes 98312 | tf_op jit(solution)/shard_map/ppermute | solution.py:348
  20.2 0.1 pad_add_fusion.at_ref
  20.2 0.8 reshape.59
  21.0 1.0 %copy.15 = bf16[3,3,16,3,16]{4,3,2,1,0:T(4,128)(2,1)S(1)} copy(bf16[3,3,16,3,16]{2,4,3,1,0:T(8,128)(2,1)} %bitcast.32) | data formatting | bytes 27648 | tf_op jit(solution)/shard_map/reshape | solution.py:374
  22.1 0.1 reshape.63.second_ref
  22.2 2.3 %conv_weights.1 = (bf16[9,48,256]{2,1,0:T(8,128)(2,1)S(1)}, bf16[9,512,256]{2,1,0:T(8,128)(2,1)S(1)}) custom-call(bf16[16,48]{1,0:T(8,128)(2,1)S(1)} %pad.4.first_ref, bf16[144,48]{1,0:T(8,128)(2,1)S(1)} %reshape.63.second_ref), custom_call_target="tpu_custom_call" | custom-call | tf_op jit(solution)/shard_map/conv_weights/pallas_call | solution.py:375
  24.5 0.0 collective-permute-done.4.three_ref
  24.6 0.0 collective-permute-done.3.one_ref
  24.6 0.6 planes.1.rest_0_
  25.2 0.0 collective-permute-done.1.left_ref
  25.2 3.1 %collective-permute-start.11 = (bf16[4,2,8,8,1024]{4,3,2,1,0:T(8,128)(2,1)S(1)}, bf16[4,2,8,8,1024]{4,3,2,1,0:T(8,128)(2,1)S(1)}, u32[]{:S(2)}, u32[]{:S(2)}) collective-permute-start(bf16[4,2,8,8,1024]{4,3,2,1,0:T(8,128)(2,1)S(1)} %planes.1.rest_0_), channel_id=1, source_target_pairs={{0,1},{1,0},{4,5},{5,4},{8,9},{9,8},{12,13},{13,12},{2,3},{3,2},{6... | collective-permute-start | bytes 3145736 | tf_op jit(solution)/shard_map/ppermute | solution.py:308
  28.3 5.3 %collective-permute-start.10 = (bf16[4,2,8,8,1024]{4,3,2,1,0:T(8,128)(2,1)S(1)}, bf16[4,2,8,8,1024]{4,3,2,1,0:T(8,128)(2,1)S(1)}, u32[]{:S(2)}, u32[]{:S(2)}) collective-permute-start(bf16[4,2,8,8,1024]{4,3,2,1,0:T(8,128)(2,1)S(1)} %planes.1.rest_0_), channel_id=1, source_target_pairs={{0,96},{1,13},{4,100},{5,1},{8,104},{9,5},{12,108},{13,9},{2,98},{... | collective-permute-start | bytes 3145736 | tf_op jit(solution)/shard_map/ppermute | solution.py:308
  33.6 0.0 collective-permute-start.9
  33.6 0.6 collective-permute-start.8
  34.2 0.9 %copy-done.1 = bf16[4,8,16,128]{3,2,1,0:T(8,128)(2,1)S(1)} copy-done((bf16[4,8,16,128]{3,2,1,0:T(8,128)(2,1)S(1)}, bf16[4,8,16,128]{3,2,1,0:T(8,128)(2,1)}, u32[]{:S(2)}) %copy-start.1) | copy-done | bytes 131096
  35.1 21.3 %encode.1 = (bf16[128,1024]{1,0:T(8,128)(2,1)S(1)}, bf16[128,1024]{1,0:T(8,128)(2,1)S(1)}) custom-call(s32[2]{0:T(128)S(1)} %pad_add_fusion.1.place_ref, bf16[4,8,16,128]{3,2,1,0:T(8,128)(2,1)S(1)} %copy-done.1, bf16[4,2,16,128]{3,2,1,0:T(8,128)(2,1)S(1)} %collective-permute-done.1.left_ref, bf16[4,2,16,128]{3,2,1,0:T(8,128)(2,1)S(1)} %collective-permute-done.2.right_ref, ...), custom_call_target="tpu_custom_call" | custom-call | flops 15000000512 | bytes 20000000 | tf_op jit(solution)/shard_map/encode/pallas_call | solution.py:387
  56.3 0.1 collective-permute-start.7
  56.4 5.9 %collective-permute-done.7.n2_ref = bf16[128,1024]{1,0:T(8,128)(2,1)S(1)} collective-permute-done((bf16[128,1024]{1,0:T(8,128)(2,1)S(1)}, bf16[128,1024]{1,0:T(8,128)(2,1)S(1)}, u32[]{:S(2)}, u32[]{:S(2)}) %collective-permute-start.7) | collective-permute-done | bytes 262176 | tf_op jit(solution)/shard_map/ppermute | solution.py:423
  62.4 0.0 collective-permute-done.9.rest_2_
  62.4 0.0 collective-permute-done.8.rest_1_
  62.4 2.9 %collective-permute-start.13 = (bf16[4,2,8,8,1024]{4,3,2,1,0:T(8,128)(2,1)S(1)}, bf16[4,2,8,8,1024]{4,3,2,1,0:T(8,128)(2,1)S(1)}, u32[]{:S(2)}, u32[]{:S(2)}) collective-permute-start(bf16[4,2,8,8,1024]{4,3,2,1,0:T(8,128)(2,1)S(1)} %collective-permute-done.8.rest_1_), channel_id=1, source_target_pairs={{0,1},{1,0},{4,5},{5,4},{8,9},{9,8},{12,13},{13,12},{2,3},{3,2},{6... | collective-permute-start | bytes 3145736 | tf_op jit(solution)/shard_map/ppermute | solution.py:308
  65.2 0.1 collective-permute-start.14
  65.3 0.4 collective-permute-start.15
  65.7 0.1 collective-permute-start.6
  65.8 0.4 collective-permute-start.12
  66.3 4.6 %collective-permute-done.6.n1_ref = bf16[128,1024]{1,0:T(8,128)(2,1)S(1)} collective-permute-done((bf16[128,1024]{1,0:T(8,128)(2,1)S(1)}, bf16[128,1024]{1,0:T(8,128)(2,1)S(1)}, u32[]{:S(2)}, u32[]{:S(2)}) %collective-permute-start.6) | collective-permute-done | bytes 262176 | tf_op jit(solution)/shard_map/ppermute | solution.py:424
  70.9 0.4 collective-permute-done.12.n3_ref
  71.3 9.6 %attend.1 = bf16[128,512]{1,0:T(8,128)(2,1)S(1)} custom-call(s32[1]{0:T(128)} %bitcast.place_ref, s32[4]{0:T(128)S(1)} %pad_add_fusion.at_ref, bf16[128,1024]{1,0:T(8,128)(2,1)S(1)} %get-tuple-element.27.tokens_ref, bf16[128,1024]{1,0:T(8,128)(2,1)S(1)} %get-tuple-element.28.n0_ref, bf16[128,1024]{1,0:T(8,128)(2,1)S(1)} %collective-permute-done.6.n1_ref, ...), custom_call_target="tpu_custom_call" | custom-call | tf_op jit(solution)/shard_map/attend/pallas_call | solution.py:431
  80.9 0.1 reshape.62
  81.0 0.7 copy.18
  (14 shorter events, 0.1 us)
Async XLA Ops:
  0.9 8.7 %collective-permute-start = (bf16[8,8,1024]{2,1,0:T(8,128)(2,1)S(1)}, bf16[8,8,1024]{2,1,0:T(8,128)(2,1)S(1)}, u32[]{:S(2)}, u32[]{:S(2)}) collective-permute-start(bf16[8,8,1024]{2,1,0:T(8,128)(2,1)S(1)} %fusion.1), channel_id=1, source_target_pairs={{0,18},{1,19},{4,22},{5,23},{8,26},{9,27},{12,30},{13,31},{2,16},{... | collective-permute-start | bytes 393224 | tf_op jit(solution)/shard_map/ppermute | solution.py:308
  9.6 14.9 %collective-permute-start.5 = (bf16[2,8,8,1024]{3,2,1,0:T(8,128)(2,1)S(1)}, bf16[2,8,8,1024]{3,2,1,0:T(8,128)(2,1)S(1)}, u32[]{:S(2)}, u32[]{:S(2)}) collective-permute-start(bf16[2,8,8,1024]{3,2,1,0:T(8,128)(2,1)S(1)} %pad_maximum_fusion.own_ref), channel_id=1, source_target_pairs={{0,8},{1,65},{4,12},{5,69},{8,0},{9,73},{12,4},{13,77},{2,10},{3,6... | collective-permute-start | bytes 786440 | tf_op jit(solution)/shard_map/ppermute | solution.py:308
  12.4 12.1 %collective-permute-start.4 = (bf16[2,8,8,1024]{3,2,1,0:T(8,128)(2,1)S(1)}, bf16[2,8,8,1024]{3,2,1,0:T(8,128)(2,1)S(1)}, u32[]{:S(2)}, u32[]{:S(2)}) collective-permute-start(bf16[2,8,8,1024]{3,2,1,0:T(8,128)(2,1)S(1)} %pad_maximum_fusion.own_ref), channel_id=1, source_target_pairs={{0,12},{1,97},{4,0},{5,101},{8,4},{9,105},{12,8},{13,109},{2,14},{... | collective-permute-start | bytes 786440 | tf_op jit(solution)/shard_map/ppermute | solution.py:308
  13.3 11.2 %collective-permute-start.3 = (bf16[2,8,8,1024]{3,2,1,0:T(8,128)(2,1)S(1)}, bf16[2,8,8,1024]{3,2,1,0:T(8,128)(2,1)S(1)}, u32[]{:S(2)}, u32[]{:S(2)}) collective-permute-start(bf16[2,8,8,1024]{3,2,1,0:T(8,128)(2,1)S(1)} %pad_maximum_fusion.own_ref), channel_id=1, source_target_pairs={{0,4},{1,33},{4,8},{5,37},{8,12},{9,41},{12,0},{13,45},{2,6},{3,35... | collective-permute-start | bytes 786440 | tf_op jit(solution)/shard_map/ppermute | solution.py:308
  14.7 10.5 %collective-permute-start.2 = (bf16[4,2,16,128]{3,2,1,0:T(8,128)(2,1)S(1)}, bf16[4,2,16,128]{3,2,1,0:T(8,128)(2,1)S(1)}, u32[]{:S(2)}, u32[]{:S(2)}) collective-permute-start(bf16[4,2,16,128]{3,2,1,0:T(8,128)(2,1)S(1)} %get-tuple-element.37), channel_id=1, source_target_pairs={{4,0},{8,4},{12,8},{16,12},{20,16},{24,20},{28,24},{32,28},{36,32}... | collective-permute-start | bytes 98312 | tf_op jit(solution)/shard_map/ppermute | solution.py:349
  16.0 9.2 %collective-permute-start.1 = (bf16[4,2,16,128]{3,2,1,0:T(8,128)(2,1)S(1)}, bf16[4,2,16,128]{3,2,1,0:T(8,128)(2,1)S(1)}, u32[]{:S(2)}, u32[]{:S(2)}) collective-permute-start(bf16[4,2,16,128]{3,2,1,0:T(8,128)(2,1)S(1)} %get-tuple-element.38), channel_id=1, source_target_pairs={{0,4},{4,8},{8,12},{12,16},{16,20},{20,24},{24,28},{28,32},{32,36}... | collective-permute-start | bytes 98312 | tf_op jit(solution)/shard_map/ppermute | solution.py:348
  25.2 37.1 %collective-permute-start.11 = (bf16[4,2,8,8,1024]{4,3,2,1,0:T(8,128)(2,1)S(1)}, bf16[4,2,8,8,1024]{4,3,2,1,0:T(8,128)(2,1)S(1)}, u32[]{:S(2)}, u32[]{:S(2)}) collective-permute-start(bf16[4,2,8,8,1024]{4,3,2,1,0:T(8,128)(2,1)S(1)} %planes.1.rest_0_), channel_id=1, source_target_pairs={{0,1},{1,0},{4,5},{5,4},{8,9},{9,8},{12,13},{13,12},{2,3},{3,2},{6... | collective-permute-start | bytes 3145736 | tf_op jit(solution)/shard_map/ppermute | solution.py:308
  28.3 34.0 %collective-permute-start.10 = (bf16[4,2,8,8,1024]{4,3,2,1,0:T(8,128)(2,1)S(1)}, bf16[4,2,8,8,1024]{4,3,2,1,0:T(8,128)(2,1)S(1)}, u32[]{:S(2)}, u32[]{:S(2)}) collective-permute-start(bf16[4,2,8,8,1024]{4,3,2,1,0:T(8,128)(2,1)S(1)} %planes.1.rest_0_), channel_id=1, source_target_pairs={{0,96},{1,13},{4,100},{5,1},{8,104},{9,5},{12,108},{13,9},{2,98},{... | collective-permute-start | bytes 3145736 | tf_op jit(solution)/shard_map/ppermute | solution.py:308
  33.6 28.8 %collective-permute-start.9 = (bf16[4,2,8,8,1024]{4,3,2,1,0:T(8,128)(2,1)S(1)}, bf16[4,2,8,8,1024]{4,3,2,1,0:T(8,128)(2,1)S(1)}, u32[]{:S(2)}, u32[]{:S(2)}) collective-permute-start(bf16[4,2,8,8,1024]{4,3,2,1,0:T(8,128)(2,1)S(1)} %planes.1.rest_0_), channel_id=1, source_target_pairs={{0,64},{1,9},{4,68},{5,13},{8,72},{9,1},{12,76},{13,5},{2,66},{3,1... | collective-permute-start | bytes 3145736 | tf_op jit(solution)/shard_map/ppermute | solution.py:308
  33.6 28.8 %collective-permute-start.8 = (bf16[4,2,8,8,1024]{4,3,2,1,0:T(8,128)(2,1)S(1)}, bf16[4,2,8,8,1024]{4,3,2,1,0:T(8,128)(2,1)S(1)}, u32[]{:S(2)}, u32[]{:S(2)}) collective-permute-start(bf16[4,2,8,8,1024]{4,3,2,1,0:T(8,128)(2,1)S(1)} %planes.1.rest_0_), channel_id=1, source_target_pairs={{0,32},{1,5},{4,36},{5,9},{8,40},{9,13},{12,44},{13,1},{2,34},{3,7... | collective-permute-start | bytes 3145736 | tf_op jit(solution)/shard_map/ppermute | solution.py:308
  34.2 0.9 %copy-start.1 = (bf16[4,8,16,128]{3,2,1,0:T(8,128)(2,1)S(1)}, bf16[4,8,16,128]{3,2,1,0:T(8,128)(2,1)}, u32[]{:S(2)}) copy-start(bf16[4,8,16,128]{3,2,1,0:T(8,128)(2,1)} %volume_ref) | copy-start | bytes 393220
  35.1 36.2 %copy-start = (bf16[1024,512]{1,0:T(8,128)(2,1)S(1)}, bf16[1024,512]{1,0:T(8,128)(2,1)}, u32[]{:S(2)}) copy-start(bf16[1024,512]{1,0:T(8,128)(2,1)} %projector_ref.1) | copy-start | bytes 3145732
  56.3 6.0 %collective-permute-start.7 = (bf16[128,1024]{1,0:T(8,128)(2,1)S(1)}, bf16[128,1024]{1,0:T(8,128)(2,1)S(1)}, u32[]{:S(2)}, u32[]{:S(2)}) collective-permute-start(bf16[128,1024]{1,0:T(8,128)(2,1)S(1)} %get-tuple-element.28.n0_ref), channel_id=1, source_target_pairs={{0,2},{2,0},{1,3},{3,1},{4,6},{6,4},{5,7},{7,5},{8,10},{10,8},{9,1... | collective-permute-start | bytes 786440 | tf_op jit(solution)/shard_map/ppermute | solution.py:423
  62.4 8.9 %collective-permute-start.13 = (bf16[4,2,8,8,1024]{4,3,2,1,0:T(8,128)(2,1)S(1)}, bf16[4,2,8,8,1024]{4,3,2,1,0:T(8,128)(2,1)S(1)}, u32[]{:S(2)}, u32[]{:S(2)}) collective-permute-start(bf16[4,2,8,8,1024]{4,3,2,1,0:T(8,128)(2,1)S(1)} %collective-permute-done.8.rest_1_), channel_id=1, source_target_pairs={{0,1},{1,0},{4,5},{5,4},{8,9},{9,8},{12,13},{13,12},{2,3},{3,2},{6... | collective-permute-start | bytes 3145736 | tf_op jit(solution)/shard_map/ppermute | solution.py:308
  65.2 6.0 %collective-permute-start.14 = (bf16[4,2,8,8,1024]{4,3,2,1,0:T(8,128)(2,1)S(1)}, bf16[4,2,8,8,1024]{4,3,2,1,0:T(8,128)(2,1)S(1)}, u32[]{:S(2)}, u32[]{:S(2)}) collective-permute-start(bf16[4,2,8,8,1024]{4,3,2,1,0:T(8,128)(2,1)S(1)} %collective-permute-done.9.rest_2_), channel_id=1, source_target_pairs={{0,1},{1,0},{4,5},{5,4},{8,9},{9,8},{12,13},{13,12},{2,3},{3,2},{6... | collective-permute-start | bytes 3145736 | tf_op jit(solution)/shard_map/ppermute | solution.py:308
  65.3 6.0 %collective-permute-start.15 = (bf16[4,2,8,8,1024]{4,3,2,1,0:T(8,128)(2,1)S(1)}, bf16[4,2,8,8,1024]{4,3,2,1,0:T(8,128)(2,1)S(1)}, u32[]{:S(2)}, u32[]{:S(2)}) collective-permute-start(bf16[4,2,8,8,1024]{4,3,2,1,0:T(8,128)(2,1)S(1)} %collective-permute-done.10.rest_3_), channel_id=1, source_target_pairs={{0,1},{1,0},{4,5},{5,4},{8,9},{9,8},{12,13},{13,12},{2,3},{3,2},{6... | collective-permute-start | bytes 3145736 | tf_op jit(solution)/shard_map/ppermute | solution.py:308
  65.7 5.2 %collective-permute-start.6 = (bf16[128,1024]{1,0:T(8,128)(2,1)S(1)}, bf16[128,1024]{1,0:T(8,128)(2,1)S(1)}, u32[]{:S(2)}, u32[]{:S(2)}) collective-permute-start(bf16[128,1024]{1,0:T(8,128)(2,1)S(1)} %get-tuple-element.28.n0_ref), channel_id=1, source_target_pairs={{0,1},{1,0},{2,3},{3,2},{4,5},{5,4},{6,7},{7,6},{8,9},{9,8},{10,11... | collective-permute-start | bytes 786440 | tf_op jit(solution)/shard_map/ppermute | solution.py:424
  65.8 5.4 %collective-permute-start.12 = (bf16[128,1024]{1,0:T(8,128)(2,1)S(1)}, bf16[128,1024]{1,0:T(8,128)(2,1)S(1)}, u32[]{:S(2)}, u32[]{:S(2)}) collective-permute-start(bf16[128,1024]{1,0:T(8,128)(2,1)S(1)} %collective-permute-done.7.n2_ref), channel_id=1, source_target_pairs={{0,1},{1,0},{2,3},{3,2},{4,5},{5,4},{6,7},{7,6},{8,9},{9,8},{10,11... | collective-permute-start | bytes 786440 | tf_op jit(solution)/shard_map/ppermute | solution.py:429
